TPU v7x, 32 devices: a whole 2x2x4 slice. The times are simulated.
32 devices in a mesh: row: 4 (over x, core), tile: 8 (over z, y).
Axes of the slice: x: 2, y: 2, z: 4, core: 2. Of those that a mesh axis runs over, the one named last changes fastest.
Arguments:
- currents: bfloat16 [2, 4, 2, 128, 8192], P(None, None, None, ('row', 'tile')), may hold values from -6 to 6
- row_angles: int32 [2048], replicated, may hold values from 0 to 32767
- column_angles: int32 [2048], replicated, may hold values from 0 to 32767
- target: float32 [2, 2048, 2048], P(None, 'tile', 'row'), may hold values from 2 to 14
- weight: float32 [2, 2048, 2048], P(None, 'tile', 'row'), may hold values from 0.01 to 0.1
- tile_owner: int32 [8192, 1], P(('row', 'tile')), may hold values from 0 to 31; in each aligned block of 256 rows (0 to 255, 256 to 511, ...) at most 16 rows name the same one
- face_slot: int32 [8192], P(('row', 'tile')), may hold values from 0 to 255
Outputs:
- intensity: float32 [2, 2048, 2048], P(None, 'tile', 'row')
- faces: float32 [2, 4, 2, 8192, 128], P(None, None, None, ('row', 'tile'))
Inputs may be any that keep to these rules, and one draw needn't show every extreme that they name: `tile_owner`: among the 256 segments of one device no owner is named more than 16 times, a bound that some block reaches.
All inputs are finite; a program needn't handle non-finite values.
Results may differ from a plain program's by a relative error of at most 0.0085.
Values may be sent and summed in bfloat16 or wider, within the bound.
No kernel may reach another device: no remote copies, remote signals or barrier semaphores. Data moves between devices by JAX's collectives and lax.ppermute only.
A program may use at most 128 MiB of HBM per device.

v0:
```python
import math

import jax
import jax.numpy as jnp
from jax import lax
from jax.sharding import PartitionSpec as P

SEG = 128


def phase_pair(position, angles, modulus, scale):
    turns = position[:, None] * angles[None, :] % modulus
    angle = turns.astype(jnp.float32) * (2.0 * math.pi / modulus)
    return (jnp.cos(angle) * scale, jnp.sin(angle) * scale)


def spread_back(half):
    return jnp.stack([half[:, 0], half[:, 1], -half[:, 1], half[:, 0]], axis=1)


def polarize(fields):
    return jnp.stack([fields[:, 0] + fields[:, 3], fields[:, 1] - fields[:, 2]], axis=1)


def body(currents, row_angles, column_angles, target, weight, tile_owner, face_slot):
    row_count = lax.axis_size("row")
    tile_count = lax.axis_size("tile")
    devices = row_count * tile_count
    freq_count, comp_count, part_count, rows_dev, columns = currents.shape
    far_rows = row_angles.shape[0]
    far_cols = column_angles.shape[0]
    share_cols = far_cols // tile_count
    modulus = 4 * columns
    column_scale = 1.0 / math.sqrt(columns)
    row_scale = 1.0 / math.sqrt(rows_dev * devices)
    block_width = min(512, far_cols)
    block_count = far_cols // block_width
    channel_count = freq_count * comp_count
    column_index = jnp.arange(columns, dtype=jnp.int32)
    channels = currents.reshape(channel_count * part_count, rows_dev, columns)

    def column_block(offset):
        angles = lax.dynamic_slice_in_dim(column_angles, offset, block_width)
        cos_part, sin_part = phase_pair(column_index, angles, modulus, column_scale)
        return (cos_part.astype(jnp.bfloat16), sin_part.astype(jnp.bfloat16))

    def forward_step(state, offset):
        cos_part, sin_part = column_block(offset)
        table = jnp.stack([cos_part, sin_part], axis=1)
        products = jnp.einsum("qxy,ysv->qsvx", channels, table, preferred_element_type=jnp.float32)
        products = products.reshape(channel_count, 2, 2, block_width, rows_dev)
        real_part = products[:, 0, 0] + products[:, 1, 1]
        imag_part = products[:, 1, 0] - products[:, 0, 1]
        return (state, jnp.stack([real_part, imag_part], axis=1).astype(jnp.bfloat16))

    block_starts = jnp.arange(block_count, dtype=jnp.int32) * block_width
    _, column_pieces = lax.scan(forward_step, jnp.int32(0), block_starts)
    ordered_cols = jnp.moveaxis(column_pieces, 0, 2)
    plane_cols = ordered_cols.reshape(channel_count * part_count, tile_count, share_cols * rows_dev)
    received = lax.all_to_all(plane_cols, "tile", split_axis=1, concat_axis=1, tiled=True)
    received = received.reshape(channel_count, 2, tile_count, share_cols, rows_dev)
    here_row = lax.axis_index("row")
    group_pos = here_row * (tile_count * rows_dev) + jnp.arange(
        tile_count * rows_dev, dtype=jnp.int32
    )
    row_cos, row_sin = phase_pair(group_pos, row_angles, modulus, row_scale)
    row_cos = row_cos.astype(jnp.bfloat16).reshape(tile_count, rows_dev, far_rows)
    row_sin = row_sin.astype(jnp.bfloat16).reshape(tile_count, rows_dev, far_rows)
    table_real = jnp.stack([row_cos, row_sin])
    table_imag = jnp.stack([-row_sin, row_cos])
    field_re = jnp.einsum(
        "qrtvx,rtxu->qvu", received, table_real, preferred_element_type=jnp.float32
    )
    field_im = jnp.einsum(
        "qrtvx,rtxu->qvu", received, table_imag, preferred_element_type=jnp.float32
    )
    field_re = field_re.reshape(freq_count, comp_count, share_cols, far_rows)
    field_im = field_im.reshape(freq_count, comp_count, share_cols, far_rows)
    fields = jnp.stack([field_re, field_im], axis=2)
    own_fields = polarize(lax.psum_scatter(fields, "row", scatter_dimension=4, tiled=True))
    intensity = jnp.sum(own_fields * own_fields, axis=(1, 2))
    factor = 4.0 * weight * (intensity - target)
    far_grad = (factor[:, None, None] * own_fields).astype(jnp.bfloat16)
    portion = lax.all_gather(far_grad, "row", axis=4, tiled=True)
    extent = portion.shape[4]
    angles = row_angles
    piece_cos, piece_sin = phase_pair(group_pos, angles, modulus, row_scale)
    piece_cos = piece_cos.astype(jnp.bfloat16).reshape(tile_count, rows_dev, extent)
    piece_sin = piece_sin.astype(jnp.bfloat16).reshape(tile_count, rows_dev, extent)
    back_real = jnp.stack([piece_cos, -piece_sin])
    back_imag = jnp.stack([piece_sin, piece_cos])
    next_re = jnp.einsum(
        "fprvu,rtxu->fptvx", portion, back_real, preferred_element_type=jnp.float32
    )
    next_im = jnp.einsum(
        "fprvu,rtxu->fptvx", portion, back_imag, preferred_element_type=jnp.float32
    )
    back_re = next_re
    back_im = next_im
    plane_grad = jnp.stack([spread_back(back_re), spread_back(back_im)], axis=2).astype(
        jnp.bfloat16
    )
    plane_grad = plane_grad.reshape(channel_count * part_count, tile_count, share_cols * rows_dev)
    returned = lax.all_to_all(plane_grad, "tile", split_axis=1, concat_axis=1, tiled=True)
    returned = returned.reshape(channel_count, 2, far_cols, rows_dev)

    def adjoint_step(totals, offset):
        cos_part, sin_part = column_block(offset)
        grad_block = lax.dynamic_slice_in_dim(returned, offset, block_width, axis=2)
        with_cos = jnp.einsum(
            "qrvx,yv->qrxy", grad_block, cos_part, preferred_element_type=jnp.float32
        )
        with_sin = jnp.einsum(
            "qrvx,yv->qrxy", grad_block, sin_part, preferred_element_type=jnp.float32
        )
        next_re = totals[0] + with_cos[:, 0] - with_sin[:, 1]
        next_im = totals[1] + with_sin[:, 0] + with_cos[:, 1]
        return ((next_re, next_im), None)

    plane_zero = jnp.zeros((channel_count, rows_dev, columns), jnp.float32)
    (adjoint_re, adjoint_im), _ = lax.scan(adjoint_step, (plane_zero, plane_zero), block_starts)
    adjoint = jnp.stack([adjoint_re, adjoint_im], axis=1).astype(jnp.bfloat16)
    segments = adjoint.reshape(channel_count * part_count, rows_dev * columns // SEG, SEG)
    seg_count = segments.shape[1]
    capacity = max(2, 2 * seg_count // devices)
    owner_index = tile_owner[:, 0]
    matches = (owner_index[:, None] == jnp.arange(devices, dtype=jnp.int32)[None, :]).astype(
        jnp.int32
    )
    earlier = jnp.cumsum(matches, axis=0) - matches
    ranked = jnp.sum(earlier * matches, axis=1)
    position = owner_index * capacity + ranked
    outgoing = jnp.zeros((channel_count * part_count, devices * capacity, SEG), jnp.bfloat16)
    outgoing = outgoing.at[:, position].set(segments)
    labels = jnp.full((devices * capacity,), seg_count, jnp.int32).at[position].set(face_slot)
    arrived, slot_marks = (
        lax.all_to_all(
            outgoing.reshape(channel_count * part_count, devices, capacity, SEG),
            ("row", "tile"),
            split_axis=1,
            concat_axis=1,
            tiled=True,
        ),
        lax.all_to_all(
            labels.reshape(1, devices, capacity),
            ("row", "tile"),
            split_axis=1,
            concat_axis=1,
            tiled=True,
        ),
    )
    arrived = arrived.reshape(channel_count * part_count, devices * capacity, SEG).astype(
        jnp.float32
    )
    slot_marks = slot_marks.reshape(devices * capacity)
    faces = jnp.zeros((channel_count * part_count, seg_count, SEG), jnp.float32)
    faces = faces.at[:, slot_marks].add(arrived, mode="drop")
    return (intensity, faces.reshape(freq_count, comp_count, part_count, seg_count, SEG))


def solution(mesh):
    in_specs = (
        P(None, None, None, ("row", "tile"), None),
        P(),
        P(),
        P(None, "tile", "row"),
        P(None, "tile", "row"),
        P(("row", "tile"), None),
        P(("row", "tile")),
    )
    out_specs = (P(None, "tile", "row"), P(None, None, None, ("row", "tile"), None))
    return jax.shard_map(body, mesh=mesh, in_specs=in_specs, out_specs=out_specs, check_vma=False)
```

profile of v0, /device:TPU:0, one launch (start us, length us, event | category | flops | bytes accessed | tf_op | source)
XLA Modules:
  0.0 1410.0 jit_solution(18253644668635062543)
XLA Ops:
  9.0 300.6 %while.28 = (s32[]{:T(128)}, bf16[4,8,2,512,4]{3,1,4,2,0:T(8,128)(2,1)S(1)}, s32[4]{0:T(128)S(1)}, s32[2048]{0:T(1024)}, bf16[16,4,8192]{2,0,1:T(8,128)(2,1)S(1)}, /*index=5*/s32[]{:T(128)}, s32[]{:T(128)}, s32[]{:T(128)}) while((s32[]{:T(128)}, bf16[4,8,2,512,4]{3,1,4,2,0:T(8,128)(2,1)S(1)}, s32[4]{0:T(128)S(1)}, s32[2048]{0:T(1024)}, ...), condition=%wide.region_1.2_spmd.clone, body=%wide.region_0.1_spmd.clone.sunk | while | flops 1182990336 | bytes 36378764 | solution.py:57
  12.3 67.9 %multiply_convert_fusion.8 = (bf16[8192,1,512]{2,0,1:T(8,128)(2,1)S(1)}, bf16[8192,1,512]{2,0,1:T(8,128)(2,1)S(1)}) fusion(s32[512]{0:T(512)S(1)} %dynamic_slice.53), kind=kLoop, calls=%fused_computation.16.clone.1 | loop fusion | flops 75497472 | bytes 16779264 | tf_op jit(solution)/shard_map/while/body/eval_jaxpr/convert_element_type | solution.py:45
  80.3 3.4 fusion.115
  87.5 67.9 %multiply_convert_fusion.8 = (bf16[8192,1,512]{2,0,1:T(8,128)(2,1)S(1)}, bf16[8192,1,512]{2,0,1:T(8,128)(2,1)S(1)}) fusion(s32[512]{0:T(512)S(1)} %dynamic_slice.53), kind=kLoop, calls=%fused_computation.16.clone.1 | loop fusion | flops 75497472 | bytes 16779264 | tf_op jit(solution)/shard_map/while/body/eval_jaxpr/convert_element_type | solution.py:45
  155.4 3.4 fusion.115
  162.6 67.9 %multiply_convert_fusion.8 = (bf16[8192,1,512]{2,0,1:T(8,128)(2,1)S(1)}, bf16[8192,1,512]{2,0,1:T(8,128)(2,1)S(1)}) fusion(s32[512]{0:T(512)S(1)} %dynamic_slice.53), kind=kLoop, calls=%fused_computation.16.clone.1 | loop fusion | flops 75497472 | bytes 16779264 | tf_op jit(solution)/shard_map/while/body/eval_jaxpr/convert_element_type | solution.py:45
  230.6 3.4 fusion.115
  237.7 67.9 %multiply_convert_fusion.8 = (bf16[8192,1,512]{2,0,1:T(8,128)(2,1)S(1)}, bf16[8192,1,512]{2,0,1:T(8,128)(2,1)S(1)}) fusion(s32[512]{0:T(512)S(1)} %dynamic_slice.53), kind=kLoop, calls=%fused_computation.16.clone.1 | loop fusion | flops 75497472 | bytes 16779264 | tf_op jit(solution)/shard_map/while/body/eval_jaxpr/convert_element_type | solution.py:45
  305.7 3.4 fusion.115
  309.6 6.0 copy.43
  315.6 17.0 %reshape.427 = bf16[16,8,1024]{2,1,0:T(8,128)(2,1)S(1)} reshape(bf16[8,2,4,512,4]{4,3,2,1,0:T(8,128)(2,1)} %copy.43) | data formatting | bytes 524288 | tf_op jit(solution)/shard_map/reshape | solution.py:59
  333.5 7.3 all-to-all-start
  343.3 6.3 all-to-all-done
  349.7 3.1 copy.45
  352.8 5.2 copy.46
  358.0 2.4 convolution_bitcast_fusion.1
  360.4 2.4 convolution_bitcast_fusion
  362.8 11.7 pad_maximum_fusion
  375.0 233.4 %reduce-scatter.2.cloned.1.call-done = f32[2,4,2,256,512]{4,3,1,0,2:T(8,128)} async-done(((f32[2,4,2,256,2048]{4,3,1,0,2:T(8,128)}), f32[2,4,2,256,512]{4,3,1,0,2:T(8,128)}) %reduce-scatter.2.cloned.1.call-update) | async-done | bytes 8388624 | tf_op jit(solution)/shard_map/reduce_scatter | solution.py:80
  608.5 4.5 slice_add_fusion
  617.0 58.4 %all-gather.2.cloned.1.call-done = bf16[2,2,2,256,2048]{4,3,1,0,2:T(8,128)(2,1)} async-done(((bf16[2,2,2,256,512]{4,3,1,0,2:T(8,128)(2,1)}), bf16[2,2,2,256,2048]{4,3,1,0,2:T(8,128)(2,1)}) %all-gather.2.cloned.1.call-update) | async-done | bytes 8388624 | tf_op jit(solution)/shard_map/all_gather | solution.py:84
  675.4 6.0 fusion.87
  681.5 2.5 fusion.88
  684.2 4.5 copy.53
  688.7 4.4 copy.54
  693.2 5.5 all-to-all-start.2
  701.9 6.1 all-to-all-done.2
  708.0 3.1 all-to-all-start.1
  711.3 19.0 %reshape.433 = bf16[8,2,2048,4]{3,2,1,0:T(8,128)(2,1)} reshape(bf16[16,8,1024]{2,1,0:T(8,128)(2,1)S(1)} %copy.55) | data formatting | bytes 524288 | tf_op jit(solution)/shard_map/reshape | solution.py:105
  730.3 7.1 copy.56
  737.4 532.7 %while.29 = (s32[]{:T(128)}, f32[8,4,8192]{2,0,1:T(8,128)S(1)}, f32[8,4,8192]{2,0,1:T(8,128)}, s32[4]{0:T(128)S(1)}, bf16[8,2,2048,4]{2,0,3,1:T(8,128)(2,1)S(1)}...) while((s32[]{:T(128)}, f32[8,4,8192]{2,0,1:T(8,128)S(1)}, f32[8,4,8192]{2,0,1:T(8,128)}, ...), condition=%wide.region_9.10_spmd.clone, body=%wide.region_8.9_spmd.clone.sunk | while | flops 1209532416 | bytes 12722337 | solution.py:121
  740.9 62.6 %fusion.123 = f32[8,2,4,8192]{3,0,2,1:T(8,128)S(1)} fusion(s32[512]{0:T(512)S(1)} %dynamic_slice.57, bf16[8,2,2048,4]{2,0,3,1:T(8,128)(2,1)S(1)} %get-tuple-element.405, s32[]{:T(128)S(6)} %select_n.142), kind=kOutput, calls=%fused_computation.44.clone.3 | convolution fusion | flops 603979776 | bytes 2164740 | tf_op jit(solution)/shard_map/while/body/eval_jaxpr/qrvx,yv->qrxy/dot_general | solution.py:113
  803.5 63.4 %fusion.122 = f32[8,2,4,8192]{3,0,2,1:T(8,128)} fusion(s32[512]{0:T(512)S(1)} %dynamic_slice.57, bf16[8,2,2048,4]{2,0,3,1:T(8,128)(2,1)S(1)} %get-tuple-element.405, s32[]{:T(128)S(6)} %select_n.142), kind=kOutput, calls=%fused_computation.42.clone.3 | convolution fusion | flops 603979776 | bytes 2164740 | tf_op jit(solution)/shard_map/while/body/eval_jaxpr/qrvx,yv->qrxy/dot_general | solution.py:110
  866.9 3.5 fusion.124
  873.8 62.6 %fusion.123 = f32[8,2,4,8192]{3,0,2,1:T(8,128)S(1)} fusion(s32[512]{0:T(512)S(1)} %dynamic_slice.57, bf16[8,2,2048,4]{2,0,3,1:T(8,128)(2,1)S(1)} %get-tuple-element.405, s32[]{:T(128)S(6)} %select_n.142), kind=kOutput, calls=%fused_computation.44.clone.3 | convolution fusion | flops 603979776 | bytes 2164740 | tf_op jit(solution)/shard_map/while/body/eval_jaxpr/qrvx,yv->qrxy/dot_general | solution.py:113
  936.3 63.4 %fusion.122 = f32[8,2,4,8192]{3,0,2,1:T(8,128)} fusion(s32[512]{0:T(512)S(1)} %dynamic_slice.57, bf16[8,2,2048,4]{2,0,3,1:T(8,128)(2,1)S(1)} %get-tuple-element.405, s32[]{:T(128)S(6)} %select_n.142), kind=kOutput, calls=%fused_computation.42.clone.3 | convolution fusion | flops 603979776 | bytes 2164740 | tf_op jit(solution)/shard_map/while/body/eval_jaxpr/qrvx,yv->qrxy/dot_general | solution.py:110
  999.8 3.8 fusion.124
  1006.9 62.6 %fusion.123 = f32[8,2,4,8192]{3,0,2,1:T(8,128)S(1)} fusion(s32[512]{0:T(512)S(1)} %dynamic_slice.57, bf16[8,2,2048,4]{2,0,3,1:T(8,128)(2,1)S(1)} %get-tuple-element.405, s32[]{:T(128)S(6)} %select_n.142), kind=kOutput, calls=%fused_computation.44.clone.3 | convolution fusion | flops 603979776 | bytes 2164740 | tf_op jit(solution)/shard_map/while/body/eval_jaxpr/qrvx,yv->qrxy/dot_general | solution.py:113
  1069.5 63.4 %fusion.122 = f32[8,2,4,8192]{3,0,2,1:T(8,128)} fusion(s32[512]{0:T(512)S(1)} %dynamic_slice.57, bf16[8,2,2048,4]{2,0,3,1:T(8,128)(2,1)S(1)} %get-tuple-element.405, s32[]{:T(128)S(6)} %select_n.142), kind=kOutput, calls=%fused_computation.42.clone.3 | convolution fusion | flops 603979776 | bytes 2164740 | tf_op jit(solution)/shard_map/while/body/eval_jaxpr/qrvx,yv->qrxy/dot_general | solution.py:110
  1132.9 3.8 fusion.124
  1140.1 62.6 %fusion.123 = f32[8,2,4,8192]{3,0,2,1:T(8,128)S(1)} fusion(s32[512]{0:T(512)S(1)} %dynamic_slice.57, bf16[8,2,2048,4]{2,0,3,1:T(8,128)(2,1)S(1)} %get-tuple-element.405, s32[]{:T(128)S(6)} %select_n.142), kind=kOutput, calls=%fused_computation.44.clone.3 | convolution fusion | flops 603979776 | bytes 2164740 | tf_op jit(solution)/shard_map/while/body/eval_jaxpr/qrvx,yv->qrxy/dot_general | solution.py:113
  1202.6 63.4 %fusion.122 = f32[8,2,4,8192]{3,0,2,1:T(8,128)} fusion(s32[512]{0:T(512)S(1)} %dynamic_slice.57, bf16[8,2,2048,4]{2,0,3,1:T(8,128)(2,1)S(1)} %get-tuple-element.405, s32[]{:T(128)S(6)} %select_n.142), kind=kOutput, calls=%fused_computation.42.clone.3 | convolution fusion | flops 603979776 | bytes 2164740 | tf_op jit(solution)/shard_map/while/body/eval_jaxpr/qrvx,yv->qrxy/dot_general | solution.py:110
  1266.1 3.8 fusion.124
  1275.8 25.5 %scatter_fusion = bf16[16,512,128]{2,0,1:T(8,128)(2,1)} fusion(bf16[16,512,128]{2,0,1:T(8,128)(2,1)} %broadcast_in_dim.14, s32[256]{0:T(256)S(1)} %bitcast.193, bf16[256,16,128]{2,1,0:T(8,128)(2,1)S(1)} %copy.58), kind=kCustom, calls=%fused_computation.1 | custom fusion | bytes 3146752 | tf_op jit(solution)/shard_map/scatter | solution.py:134
  1301.3 5.8 all-to-all-start.3
  1309.2 48.0 %all-to-all-done.3 = bf16[16,32,16,128]{3,0,2,1:T(8,128)(2,1)S(1)} async-done(((bf16[16,32,16,128]{3,0,2,1:T(8,128)(2,1)}), bf16[16,32,16,128]{3,0,2,1:T(8,128)(2,1)S(1)}, u32[]{:S(2)}, u32[]{:S(2)}) %all-to-all-start.3) | async-done | bytes 2097184 | tf_op jit(solution)/shard_map/all_to_all | solution.py:137
  1357.2 2.4 convert_bitcast_fusion
  1359.8 41.0 %scatter_fusion.1 = f32[16,256,128]{2,0,1:T(8,128)S(1)} fusion(f32[16,256,128]{2,0,1:T(8,128)S(1)} %broadcast_in_dim.13, s32[512]{0:T(512)S(1)} %bitcast.191, f32[512,16,128]{2,1,0:T(8,128)} %convert_bitcast_fusion), kind=kCustom, calls=%fused_computation.2 | custom fusion | flops 1048576 | bytes 12584960 | tf_op jit(solution)/shard_map/scatter-add | solution.py:157
  (98 shorter events, 35.5 us)
Async XLA Ops:
  309.6 31.5 %copy-start.3 = (s32[2048]{0:T(1024)S(1)}, s32[2048]{0:T(1024)}, u32[]{:S(2)}) copy-start(s32[2048]{0:T(1024)} %param.12) | copy-start | bytes 24580
  333.5 16.2 %all-to-all-start = ((bf16[16,8,1024]{2,0,1:T(8,128)(2,1)}), bf16[16,8,1024]{2,0,1:T(8,128)(2,1)S(1)}, u32[]{:S(2)}, u32[]{:S(2)}) async-start(bf16[16,8,1024]{2,0,1:T(8,128)(2,1)} %copy.44), calls=%async_computation | async-start | bytes 524288 | tf_op jit(solution)/shard_map/all_to_all | solution.py:60
  340.8 267.7 %reduce-scatter.2.cloned.1.call-start = ((), (), s32[]{:S(2)}) async-start(), calls=%async_computation.5 | async-start | bytes 41943040 | tf_op jit(solution)/shard_map/reduce_scatter | solution.py:80
  374.5 240.0 %copy-start.1 = (f32[2,256,512]{2,1,0:T(8,128)S(1)}, f32[2,256,512]{2,1,0:T(8,128)}, u32[]{:S(2)}) copy-start(f32[2,256,512]{2,1,0:T(8,128)} %param.14) | copy-start | bytes 3145732
  374.5 240.0 %copy-start.2 = (f32[2,256,512]{2,1,0:T(8,128)S(1)}, f32[2,256,512]{2,1,0:T(8,128)}, u32[]{:S(2)}) copy-start(f32[2,256,512]{2,1,0:T(8,128)} %param.15) | copy-start | bytes 3145732
  374.5 300.9 %all-gather.2.cloned.1.call-start = ((), (), s32[]{:S(2)}) async-start(), calls=%async_computation.6 | async-start | bytes 10485760 | tf_op jit(solution)/shard_map/all_gather | solution.py:84
  613.5 1.0 copy-start
  675.4 6.1 slice-start
  675.4 6.1 slice-start.1
  684.0 14.6 %copy-start.4 = (s32[256,1]{0,1:T(1,128)S(1)}, s32[256,1]{0,1:T(1,128)}, u32[]{:S(2)}) copy-start(s32[256,1]{0,1:T(1,128)} %param.16) | copy-start | bytes 3076
  693.2 14.9 %all-to-all-start.2 = ((bf16[16,8,1024]{2,0,1:T(8,128)(2,1)}), bf16[16,8,1024]{2,0,1:T(8,128)(2,1)S(1)}, u32[]{:S(2)}, u32[]{:S(2)}) async-start(bf16[16,8,1024]{2,0,1:T(8,128)(2,1)} %copy.54), calls=%async_computation.3 | async-start | bytes 524288 | tf_op jit(solution)/shard_map/all_to_all | solution.py:104
  699.6 8.4 copy-start.5
  708.0 593.3 %all-to-all-start.1 = ((s32[1,32,16]{2,0,1:T(1,128)}), s32[1,32,16]{2,0,1:T(1,128)}, u32[]{:S(2)}, u32[]{:S(2)}) async-start(s32[1,32,16]{2,0,1:T(1,128)} %bitcast.20), calls=%async_computation.2 | async-start | bytes 32768 | tf_op jit(solution)/shard_map/all_to_all | solution.py:144
  1270.1 5.7 copy-start.6
  1301.3 55.9 %all-to-all-start.3 = ((bf16[16,32,16,128]{3,0,2,1:T(8,128)(2,1)}), bf16[16,32,16,128]{3,0,2,1:T(8,128)(2,1)S(1)}, u32[]{:S(2)}, u32[]{:S(2)}) async-start(bf16[16,32,16,128]{3,0,2,1:T(8,128)(2,1)} %bitcast.40), calls=%async_computation.4 | async-start | bytes 4194304 | tf_op jit(solution)/shard_map/all_to_all | solution.py:137
Sparse Core Ops, SparseCore 0:
  374.6 233.7 reduce-scatter.1
  617.1 58.2 all-gather.1
where the time goes:
time: 1420 us; the launch traced here: 1410 us
  matrix products  531 us (37%)
  other arithmetic  356 us (25%)
  waiting for transfers between devices  352 us (25%)
  local copies, waits for them, and re-layouts  118 us (8%)
  starting transfers between devices  22.4 us (2%)
  loops' own time  16.2 us (1%)
  between operations  14.8 us (1%)
    convert_element_type x4, other arithmetic, column_block(): return (cos_part.astype(jnp.bfloat16), sin_part.astype(jnp.bfloat16))  272 us
    dot_general x4, matrix products, adjoint_step(): jnp.einsum('qrvx,yv->qrxy', grad_block, cos_part, preferred_element_type=...  254 us
    dot_general x4, matrix products, adjoint_step(): jnp.einsum('qrvx,yv->qrxy', grad_block, sin_part, preferred_element_type=...  250 us
    reduce_scatter x1, waiting for transfers between devices, body(): lax.psum_scatter(fields, 'row', scatter_dimension=4, tiled=True)  233 us
    all_gather x1, waiting for transfers between devices, body(): portion = lax.all_gather(far_grad, 'row', axis=4, tiled=True)  58.4 us
    all_to_all x1, waiting for transfers between devices, body(): lax.all_to_all(outgoing.reshape(channel_count * part_count, devices, capa...  48 us
    scatter-add x1, other arithmetic, body(): faces = faces.at[:, slot_marks].add(arrived, mode='drop')  41 us
  transfers between devices with their start and end apart: 6, of which 5 were waited for; matrix products, arithmetic and copies ran while one was open for 42% of the time, Pallas kernels for 0%

commit v1 on v0

v1 whole, which is shorter than its diff:
```python
import functools
import math

import jax
import jax.numpy as jnp
from jax import lax
from jax.experimental import pallas as pl
from jax.experimental.pallas import tpu as pltpu
from jax.sharding import PartitionSpec as P

SEG = 128
CHUNK = 256
BF = jnp.bfloat16
F32 = jnp.float32


def cos_sin(turns, quarter, scale):
    bits = int(math.log2(quarter))
    turns = turns & (4 * quarter - 1)
    octant = (turns + quarter // 2) >> bits
    angle = (turns - (octant << bits)).astype(F32) * (math.pi / (2 * quarter))
    square = angle * angle
    sin_part = angle * scale + (angle * scale) * square * (
        -1.6666654611e-1 + square * (8.3321608736e-3 - square * 1.9515295891e-4)
    )
    cos_part = scale - square * (0.5 * scale) + (square * scale) * square * (
        4.166664568298827e-2 + square * (-1.388731625493765e-3 + square * 2.443315711809948e-5)
    )
    swap = (octant & 1) == 1
    cos_out = jnp.where(swap, sin_part, cos_part)
    sin_out = jnp.where(swap, cos_part, sin_part)
    cos_out = jnp.where(((octant + 1) & 2) == 2, -cos_out, cos_out)
    sin_out = jnp.where((octant & 2) == 2, -sin_out, sin_out)
    return cos_out, sin_out


def iota(shape, dim):
    return lax.broadcasted_iota(jnp.int32, shape, dim)


def forward_kernel(quarter, rows_dev, angle_ref, cur_ref, f_ref, w_ref, t_ref, lhs):
    columns = quarter
    points = rows_dev * columns // SEG
    width = angle_ref.shape[-1]

    @pl.when(pl.program_id(0) == 0)
    def _():
        for f in range(2):
            for p in range(2):
                rows = pl.ds((2 * f + p) * points, points)
                for c in range(2):
                    first, second = (0, 3) if p == 0 else (1, 2)
                    lhs[rows, c * SEG:(c + 1) * SEG] = cur_ref[f, first, c]
                    other = cur_ref[f, second, c]
                    if p == 1:
                        other = (-other.astype(F32)).astype(BF)
                    lhs[rows, (2 + c) * SEG:(3 + c) * SEG] = other

    angles = angle_ref[0]
    cos_b, sin_b = cos_sin(iota((SEG, width), 0) * angles, quarter, 1.0 / math.sqrt(columns))
    cos_b, sin_b = cos_b.astype(BF), sin_b.astype(BF)
    table = jnp.concatenate(
        [
            jnp.concatenate([cos_b, -sin_b], axis=1),
            jnp.concatenate([sin_b, cos_b], axis=1),
        ],
        axis=0,
    )
    w_ref[0] = table
    coarse = (iota((points, width), 0) // rows_dev) * SEG
    cos_a, sin_a = cos_sin(coarse * angles, quarter, 1.0)
    t_ref[0, 0] = cos_a
    t_ref[0, 1] = sin_a
    both = jnp.concatenate([table, table], axis=0)
    low = iota((8, width), 0) < 4
    for fp in range(4):
        grid_sum = jnp.dot(
            lhs[pl.ds(fp * points, points), :], both, preferred_element_type=F32
        )
        real, imag = grid_sum[:, :width], grid_sum[:, width:]
        out_re = jnp.sum((real * cos_a + imag * sin_a).reshape(points // 8, 8, width), axis=0)
        out_im = jnp.sum((imag * cos_a - real * sin_a).reshape(points // 8, 8, width), axis=0)
        out_re = out_re + pltpu.roll(out_re, 4, 0)
        out_im = out_im + pltpu.roll(out_im, 4, 0)
        out = jnp.where(low, out_re, out_im).astype(BF)
        for copy in range(f_ref.shape[0]):
            f_ref[copy, 0, fp] = out


def middle_kernel(quarter, rows_dev, angle_ref, got_ref, target_ref, weight_ref, int_ref, back_ref, table):
    devices = got_ref.shape[0]
    share_v = got_ref.shape[-1]
    share_u = angle_ref.shape[-1]
    depth = devices * 2 * rows_dev

    @pl.when(pl.program_id(0) == 0)
    def _():
        row = iota((depth, share_u), 0)
        x = (row // (2 * rows_dev)) * rows_dev + (row & (rows_dev - 1))
        is_imag = (row & rows_dev) == rows_dev
        scale = 1.0 / math.sqrt(rows_dev * devices)
        cos_x, sin_x = cos_sin(x * angle_ref[...], quarter, scale)
        table[:, :share_u] = jnp.where(is_imag, sin_x, cos_x).astype(BF)
        table[:, share_u:] = jnp.where(is_imag, cos_x, -sin_x).astype(BF)

    mixed = []
    for p in range(2):
        plane = got_ref[:, p].astype(F32).reshape(depth, share_v).astype(BF)
        mixed.append(
            lax.dot_general(plane, table[...], (((0,), (0,)), ((), ())), preferred_element_type=F32)
        )
    power = mixed[0] * mixed[0] + mixed[1] * mixed[1]
    intensity = power[:, :share_u] + power[:, share_u:]
    int_ref[0] = intensity
    factor = 4.0 * weight_ref[0] * (intensity - target_ref[0])
    factor = jnp.concatenate([factor, factor], axis=1)
    for p in range(2):
        far_grad = (factor * mixed[p]).astype(BF)
        back = lax.dot_general(
            table[...], far_grad, (((1,), (1,)), ((), ())), preferred_element_type=F32
        )
        back_ref[:, p] = back.reshape(devices, 2 * rows_dev, share_v).astype(BF)


def adjoint_kernel(devices, rows_dev, got_ref, w_ref, t_ref, owner_ref, slot_ref, out_ref, label_ref, total):
    points = t_ref.shape[2]
    width = t_ref.shape[3]
    segs = points // rows_dev
    slots = out_ref.shape[1]
    cap = slots // devices
    step = pl.program_id(0)

    @pl.when(step == 0)
    def _():
        total[...] = jnp.zeros_like(total)

    cos_a, sin_a = t_ref[0, 0], t_ref[0, 1]
    low = iota((8, width), 0) < 4
    parts = []
    for fp in range(4):
        plane = jnp.sum(got_ref[:, 0, fp].astype(F32), axis=0)
        turned = pltpu.roll(plane, 4, 0)
        real = jnp.where(low, plane, turned)
        imag = jnp.where(low, turned, plane)
        real = jnp.broadcast_to(real[None], (points // 8, 8, width)).reshape(points, width)
        imag = jnp.broadcast_to(imag[None], (points // 8, 8, width)).reshape(points, width)
        parts.append(
            jnp.concatenate(
                [
                    (cos_a * real - sin_a * imag).astype(BF),
                    (cos_a * imag + sin_a * real).astype(BF),
                ],
                axis=1,
            )
        )
    lhs = jnp.concatenate(parts, axis=0)
    total[...] += lax.dot_general(
        lhs, w_ref[0], (((1,), (1,)), ((), ())), preferred_element_type=F32
    )

    @pl.when(step == pl.num_programs(0) - 1)
    def _():
        point = iota((points, points), 1)
        point = (point & (rows_dev - 1)) * segs + (point // rows_dev)
        source = iota((points, points), 0)
        owner_col = owner_ref[...]
        owner_row = jnp.sum(jnp.where(source == point, owner_col, 0), axis=0, keepdims=True)
        same = jnp.where((source < point) & (owner_col == owner_row), 1, 0)
        place = owner_row * cap + jnp.sum(same, axis=0, keepdims=True)
        choose = jnp.where(iota((slots, points), 0) == place, 1.0, 0.0).astype(BF)
        for fp in range(4):
            block = total[fp * points:(fp + 1) * points, :].astype(BF)
            sent = jnp.dot(choose, block, preferred_element_type=F32).astype(BF)
            out_ref[2 * fp] = sent[:, :SEG]
            out_ref[2 * fp + 1] = sent[:, SEG:]
        slot_col = slot_ref[...]
        slot_row = jnp.sum(jnp.where(source == point, slot_col, 0), axis=0, keepdims=True)
        marks = jnp.where(iota((slots, points), 0) == place, slot_row + 1, 0)
        marks = jnp.sum(marks, axis=1, keepdims=True)
        label_ref[...] = marks


def faces_kernel(got_ref, label_ref, out_ref):
    faces = out_ref.shape[3]
    slots = got_ref.shape[1]
    hit = iota((faces, slots), 0) + 1 == label_ref[...]
    choose = jnp.where(hit, 1.0, 0.0).astype(BF)
    for f in range(2):
        for p in range(2):
            for c in range(2):
                found = jnp.dot(
                    choose, got_ref[4 * f + 2 * p + c], preferred_element_type=F32
                )
                if p == 0:
                    out_ref[f, 0, c] = found
                    out_ref[f, 3, c] = found
                else:
                    out_ref[f, 1, c] = found
                    out_ref[f, 2, c] = -found


def params():
    return pltpu.CompilerParams(
        dimension_semantics=("arbitrary",), vmem_limit_bytes=56 * 1024 * 1024
    )


def whole(shape):
    return pl.BlockSpec(shape, lambda i: (0,) * len(shape))


def body(currents, row_angles, column_angles, target, weight, tile_owner, face_slot):
    row_count = lax.axis_size("row")
    tile_count = lax.axis_size("tile")
    devices = row_count * tile_count
    freq_count, comp_count, part_count, rows_dev, columns = currents.shape
    far_rows = row_angles.shape[0]
    far_cols = column_angles.shape[0]
    share_v = far_cols // tile_count
    share_u = far_rows // row_count
    chunks = far_cols // CHUNK
    tiles = columns // SEG
    points = rows_dev * tiles
    both = ("row", "tile")

    cur = currents.reshape(freq_count, comp_count, part_count, rows_dev, tiles, SEG)
    cur = cur.transpose(0, 1, 2, 4, 3, 5).reshape(freq_count, comp_count, part_count, points, SEG)
    copies = row_count if share_v == CHUNK else 1
    plane, table, turn = pl.pallas_call(
        functools.partial(forward_kernel, columns, rows_dev),
        grid=(chunks,),
        in_specs=[
            pl.BlockSpec((1, 1, CHUNK), lambda i: (i, 0, 0)),
            whole(cur.shape),
        ],
        out_specs=[
            pl.BlockSpec((copies, 1, 4, 2 * rows_dev, CHUNK), lambda i: (0, i, 0, 0, 0)),
            pl.BlockSpec((1, 2 * SEG, 2 * CHUNK), lambda i: (i, 0, 0)),
            pl.BlockSpec((1, 2, points, CHUNK), lambda i: (i, 0, 0, 0)),
        ],
        out_shape=[
            jax.ShapeDtypeStruct((copies, chunks, 4, 2 * rows_dev, CHUNK), BF),
            jax.ShapeDtypeStruct((chunks, 2 * SEG, 2 * CHUNK), BF),
            jax.ShapeDtypeStruct((chunks, 2, points, CHUNK), F32),
        ],
        scratch_shapes=[pltpu.VMEM((4 * points, 4 * SEG), BF)],
        compiler_params=params(),
        name="columns",
    )(column_angles.reshape(chunks, 1, CHUNK), cur)

    if share_v != CHUNK:
        plane = plane.reshape(chunks, 4, 2 * rows_dev, CHUNK // share_v, share_v)
        plane = plane.transpose(0, 3, 1, 2, 4).reshape(1, tile_count, 4, 2 * rows_dev, share_v)
        plane = jnp.broadcast_to(plane, (row_count,) + plane.shape[1:])
    plane = plane.reshape(devices, 4, 2 * rows_dev, share_v)
    got = lax.all_to_all(plane, both, split_axis=0, concat_axis=0, tiled=True)

    own_angles = lax.dynamic_slice_in_dim(row_angles, lax.axis_index("row") * share_u, share_u)
    pair = pl.BlockSpec((devices, 2, 2 * rows_dev, share_v), lambda i: (0, i, 0, 0))
    far = pl.BlockSpec((1, share_v, share_u), lambda i: (i, 0, 0))
    intensity, back = pl.pallas_call(
        functools.partial(middle_kernel, columns, rows_dev),
        grid=(freq_count,),
        in_specs=[whole((1, share_u)), pair, far, far],
        out_specs=[far, pair],
        out_shape=[
            jax.ShapeDtypeStruct((freq_count, share_v, share_u), F32),
            jax.ShapeDtypeStruct((devices, 4, 2 * rows_dev, share_v), BF),
        ],
        scratch_shapes=[pltpu.VMEM((devices * 2 * rows_dev, 2 * share_u), BF)],
        compiler_params=params(),
        name="objective",
    )(own_angles.reshape(1, share_u), got, target, weight)

    back = lax.all_to_all(back, both, split_axis=0, concat_axis=0, tiled=True)
    back = back.reshape(row_count, tile_count, 4, 2 * rows_dev, share_v)
    if share_v != CHUNK:
        back = back.reshape(row_count, chunks, CHUNK // share_v, 4, 2 * rows_dev, share_v)
        back = back.transpose(0, 1, 3, 4, 2, 5).reshape(row_count, chunks, 4, 2 * rows_dev, CHUNK)

    seg_count = rows_dev * tiles
    slots = 2 * seg_count
    cap = slots // devices
    outgoing, labels = pl.pallas_call(
        functools.partial(adjoint_kernel, devices, rows_dev),
        grid=(chunks,),
        in_specs=[
            pl.BlockSpec((row_count, 1, 4, 2 * rows_dev, CHUNK), lambda i: (0, i, 0, 0, 0)),
            pl.BlockSpec((1, 2 * SEG, 2 * CHUNK), lambda i: (i, 0, 0)),
            pl.BlockSpec((1, 2, points, CHUNK), lambda i: (i, 0, 0, 0)),
            whole((seg_count, 1)),
            whole((seg_count, 1)),
        ],
        out_specs=[whole((8, slots, SEG)), whole((slots, 1))],
        out_shape=[
            jax.ShapeDtypeStruct((8, slots, SEG), BF),
            jax.ShapeDtypeStruct((slots, 1), jnp.int32),
        ],
        scratch_shapes=[pltpu.VMEM((4 * points, 2 * SEG), F32)],
        compiler_params=params(),
        name="adjoint",
    )(back, table, turn, tile_owner, face_slot.reshape(seg_count, 1))

    arrived = lax.all_to_all(
        outgoing.reshape(8, devices, cap, SEG), both, split_axis=1, concat_axis=1, tiled=True
    )
    marks = lax.all_to_all(
        labels.reshape(devices, cap), both, split_axis=0, concat_axis=0, tiled=True
    )
    out_shape = (freq_count, comp_count, part_count, seg_count, SEG)
    faces = pl.pallas_call(
        faces_kernel,
        grid=(1,),
        in_specs=[whole((8, slots, SEG)), whole((1, slots))],
        out_specs=whole(out_shape),
        out_shape=jax.ShapeDtypeStruct(out_shape, F32),
        compiler_params=params(),
        name="faces",
    )(arrived.reshape(8, slots, SEG), marks.reshape(1, slots))
    return (intensity, faces)


def solution(mesh):
    in_specs = (
        P(None, None, None, ("row", "tile"), None),
        P(),
        P(),
        P(None, "tile", "row"),
        P(None, "tile", "row"),
        P(("row", "tile"), None),
        P(("row", "tile")),
    )
    out_specs = (P(None, "tile", "row"), P(None, None, None, ("row", "tile"), None))
    return jax.shard_map(body, mesh=mesh, in_specs=in_specs, out_specs=out_specs, check_vma=False)
```

time: 1420 us -> 117 us (0.08)
  matrix products: 531 us -> 0 us
  other arithmetic: 356 us -> 1.76 us
  waiting for transfers between devices: 352 us -> 60 us
  local copies, waits for them, and re-layouts: 118 us -> 10.1 us
  Pallas kernels: 0 us -> 28.9 us
  loops' own time: 16.2 us -> 0 us
    dot_general x16 -> x0, matrix products: 531 us -> none  [the longest x4 254 us: adjoint_step(): jnp.einsum('qrvx,yv->qrxy', grad_block, cos_part, preferred_element_type=...]
    convert_element_type x8 -> x0, other arithmetic: 277 us -> none  [the longest x4 272 us: column_block(): return (cos_part.astype(jnp.bfloat16), sin_part.astype(jnp.bfloat16))]
    reduce_scatter x1 -> x0, waiting for transfers between devices: 233 us -> none  [body(): lax.psum_scatter(fields, 'row', scatter_dimension=4, tiled=True)]
    all_gather x1 -> x0, waiting for transfers between devices: 58.4 us -> none  [body(): portion = lax.all_gather(far_grad, 'row', axis=4, tiled=True)]
    scatter-add x1 -> x0, other arithmetic: 41 us -> none  [body(): faces = faces.at[:, slot_marks].add(arrived, mode='drop')]
    reshape x10 -> x3, local copies, waits for them, and re-layouts: 40.1 us -> 3.93 us  [the longest x1 2.49 us: body(): outgoing.reshape(8, devices, cap, SEG)]
    pallas_call x0 -> x4, Pallas kernels: none -> 28.9 us  [the longest x1 11.5 us: body(): pl.pallas_call(functools.partial(forward_kernel, columns, rows_dev), grid...]
    scatter x2 -> x0, local copies, waits for them, and re-layouts: 27.1 us -> none  [the longest x1 25.5 us: body(): outgoing = outgoing.at[:, position].set(segments)]
  transfers between devices with their start and end apart: 6 -> 4, of which waited for: 5 -> 4; matrix products, arithmetic and copies ran while one was open for 42% -> 6% of each run, Pallas kernels for 0% -> 0%
where the time goes in v1:
time: 117 us
  waiting for transfers between devices  60 us (51%)
  Pallas kernels  28.9 us (25%)
  starting transfers between devices  15.1 us (13%)
  local copies, waits for them, and re-layouts  10.1 us (9%)
  other arithmetic  1.76 us (2%)
    all_to_all x1, waiting for transfers between devices, body(): lax.all_to_all(outgoing.reshape(8, devices, cap, SEG), both, split_axis=1...  25.7 us
    all_to_all x1, waiting for transfers between devices, body(): got = lax.all_to_all(plane, both, split_axis=0, concat_axis=0, tiled=True)  15 us
    all_to_all x1, waiting for transfers between devices, body(): back = lax.all_to_all(back, both, split_axis=0, concat_axis=0, tiled=True)  14.8 us
    pallas_call x1, Pallas kernels, body(): pl.pallas_call(functools.partial(forward_kernel, columns, rows_dev), grid...  11.5 us
    pallas_call x1, Pallas kernels, body(): pl.pallas_call(functools.partial(adjoint_kernel, devices, rows_dev), grid...  9.17 us
    all_to_all x1, starting transfers between devices, body(): got = lax.all_to_all(plane, both, split_axis=0, concat_axis=0, tiled=True)  7.32 us
    pallas_call x1, Pallas kernels, body(): pl.pallas_call(functools.partial(middle_kernel, columns, rows_dev), grid=...  5 us
    all_to_all x1, waiting for transfers between devices, body(): lax.all_to_all(labels.reshape(devices, cap), both, split_axis=0, concat_a...  4.62 us
  transfers between devices with their start and end apart: 4, of which 4 were waited for; matrix products, arithmetic and copies ran while one was open for 6% of the time, Pallas kernels for 0%

profile of v1, /device:TPU:0, one launch (start us, length us, event | category | flops | bytes accessed | tf_op | source)
XLA Modules:
  0.0 116.6 jit_solution(478300180810895240)
XLA Ops:
  0.6 11.5 %columns.1 = (bf16[4,8,4,8,256]{4,3,2,1,0:T(8,128)(2,1)}, bf16[8,256,512]{2,1,0:T(8,128)(2,1)}, f32[8,2,256,256]{3,2,1,0:T(8,128)}) custom-call(s32[8,1,256]{2,1,0:T(1,128)} %bitcast.18, bf16[2,4,2,256,128]{4,3,2,1,0:T(8,128)(2,1)} %bitcast.15), custom_call_target="tpu_custom_call" | custom-call | tf_op jit(solution)/shard_map/columns/pallas_call | solution.py:229
  12.1 7.3 %all-to-all-start = ((bf16[32,4,8,256]{3,2,1,0:T(8,128)(2,1)}), bf16[32,4,8,256]{3,2,1,0:T(8,128)(2,1)S(1)}, u32[]{:S(2)}, u32[]{:S(2)}) async-start(bf16[32,4,8,256]{3,2,1,0:T(8,128)(2,1)} %bitcast.17), calls=%async_computation | async-start | bytes 1048576 | tf_op jit(solution)/shard_map/all_to_all | solution.py:256
  19.5 0.0 copy-start.2
  19.5 0.0 copy-start.3
  19.5 1.4 %dynamic_slice.3 = s32[512]{0:T(512)} dynamic-slice(s32[2048]{0:T(1024)} %param.8, s32[]{:T(128)S(6)} %select_n.3), dynamic_slice_sizes={512} | dynamic-slice | bytes 4100 | tf_op jit(solution)/shard_map/dynamic_slice | solution.py:258
  20.8 15.0 %all-to-all-done.got_ref = bf16[32,4,8,256]{3,2,1,0:T(8,128)(2,1)S(1)} async-done(((bf16[32,4,8,256]{3,2,1,0:T(8,128)(2,1)}), bf16[32,4,8,256]{3,2,1,0:T(8,128)(2,1)S(1)}, u32[]{:S(2)}, u32[]{:S(2)}) %all-to-all-start) | async-done | bytes 524320 | tf_op jit(solution)/shard_map/all_to_all | solution.py:256
  35.8 0.0 copy-start.1
  35.8 0.8 copy-done.1
  36.6 5.0 %objective.1 = (f32[2,256,512]{2,1,0:T(8,128)}, bf16[32,4,8,256]{3,2,1,0:T(8,128)(2,1)}) custom-call(s32[1,512]{1,0:T(1,128)} %bitcast.19, bf16[32,4,8,256]{3,2,1,0:T(8,128)(2,1)} %copy-done.1, f32[2,256,512]{2,1,0:T(8,128)} %target_ref.1, f32[2,256,512]{2,1,0:T(8,128)} %weight_ref.1), custom_call_target="tpu_custom_call" | custom-call | tf_op jit(solution)/shard_map/objective/pallas_call | solution.py:261
  41.6 2.6 %all-to-all-start.1 = ((bf16[32,4,8,256]{3,2,1,0:T(8,128)(2,1)}), bf16[32,4,8,256]{3,2,1,0:T(8,128)(2,1)S(1)}, u32[]{:S(2)}, u32[]{:S(2)}) async-start(bf16[32,4,8,256]{3,2,1,0:T(8,128)(2,1)} %get-tuple-element.11), calls=%async_computation.1 | async-start | bytes 1048576 | tf_op jit(solution)/shard_map/all_to_all | solution.py:275
  44.2 0.0 copy-done.2
  44.2 0.8 copy.15.owner_ref
  45.0 0.0 copy-done.3
  45.0 0.8 copy.16.slot_ref
  45.8 14.8 %all-to-all-done.1 = bf16[32,4,8,256]{3,2,1,0:T(8,128)(2,1)S(1)} async-done(((bf16[32,4,8,256]{3,2,1,0:T(8,128)(2,1)}), bf16[32,4,8,256]{3,2,1,0:T(8,128)(2,1)S(1)}, u32[]{:S(2)}, u32[]{:S(2)}) %all-to-all-start.1) | async-done | bytes 524320 | tf_op jit(solution)/shard_map/all_to_all | solution.py:275
  60.6 0.0 copy-start
  60.6 0.8 copy-done
  61.4 9.2 %adjoint.1 = (bf16[8,512,128]{2,1,0:T(8,128)(2,1)}, s32[512,1]{1,0:T(8,128)}) custom-call(bf16[4,8,4,8,256]{4,3,2,1,0:T(8,128)(2,1)} %bitcast.14, bf16[8,256,512]{2,1,0:T(8,128)(2,1)} %get-tuple-element.12.w_ref, f32[8,2,256,256]{3,2,1,0:T(8,128)} %get-tuple-element.13.t_ref, s32[256,1]{1,0:T(8,128)} %copy.15.owner_ref, s32[256,1]{1,0:T(8,128)} %copy.16.slot_ref), custom_call_target="tpu_custom_call" | custom-call | tf_op jit(solution)/shard_map/adjoint/pallas_call | solution.py:284
  70.6 1.1 reduce
  71.7 0.7 all_to_all.18
  72.3 2.5 %all-to-all-start.3 = ((s32[32,1,16]{2,1,0:T(1,128)}), s32[32,1,16]{2,1,0:T(1,128)S(1)}, u32[]{:S(2)}, u32[]{:S(2)}) async-start(s32[32,1,16]{2,1,0:T(1,128)} %bitcast.10), calls=%async_computation.3 | async-start | bytes 32768 | tf_op jit(solution)/shard_map/all_to_all | solution.py:307
  74.9 2.5 %copy.17 = bf16[8,32,16,128]{3,2,0,1:T(8,128)(2,1)} copy(bf16[8,32,16,128]{3,2,1,0:T(8,128)(2,1)} %bitcast.16) | data formatting | bytes 2097152 | tf_op jit(solution)/shard_map/reshape | solution.py:305
  77.4 4.6 %all-to-all-done.3 = s32[32,1,16]{2,1,0:T(1,128)S(1)} async-done(((s32[32,1,16]{2,1,0:T(1,128)}), s32[32,1,16]{2,1,0:T(1,128)S(1)}, u32[]{:S(2)}, u32[]{:S(2)}) %all-to-all-start.3) | async-done | bytes 2080 | tf_op jit(solution)/shard_map/all_to_all | solution.py:307
  82.0 2.6 %all-to-all-start.2 = ((bf16[8,32,16,128]{3,2,0,1:T(8,128)(2,1)}), bf16[8,32,16,128]{3,2,0,1:T(8,128)(2,1)S(1)}, u32[]{:S(2)}, u32[]{:S(2)}) async-start(bf16[8,32,16,128]{3,2,0,1:T(8,128)(2,1)} %copy.17), calls=%async_computation.2 | async-start | bytes 2097152 | tf_op jit(solution)/shard_map/all_to_all | solution.py:304
  84.7 0.6 broadcast.4
  85.2 0.7 reduce.4
  85.9 0.6 reshape.48.label_ref
  86.5 25.7 %all-to-all-done.2 = bf16[8,32,16,128]{3,2,0,1:T(8,128)(2,1)S(1)} async-done(((bf16[8,32,16,128]{3,2,0,1:T(8,128)(2,1)}), bf16[8,32,16,128]{3,2,0,1:T(8,128)(2,1)S(1)}, u32[]{:S(2)}, u32[]{:S(2)}) %all-to-all-start.2) | async-done | bytes 1048608 | tf_op jit(solution)/shard_map/all_to_all | solution.py:304
  112.2 1.2 copy.18
  113.4 3.2 %faces.1 = f32[2,4,2,256,128]{4,3,2,1,0:T(8,128)} custom-call(bf16[8,512,128]{2,1,0:T(8,128)(2,1)} %bitcast.13, s32[1,512]{1,0:T(1,128)} %reshape.48.label_ref), custom_call_target="tpu_custom_call" | custom-call | tf_op jit(solution)/shard_map/faces/pallas_call | solution.py:311
Async XLA Ops:
  12.1 23.7 %all-to-all-start = ((bf16[32,4,8,256]{3,2,1,0:T(8,128)(2,1)}), bf16[32,4,8,256]{3,2,1,0:T(8,128)(2,1)S(1)}, u32[]{:S(2)}, u32[]{:S(2)}) async-start(bf16[32,4,8,256]{3,2,1,0:T(8,128)(2,1)} %bitcast.17), calls=%async_computation | async-start | bytes 1048576 | tf_op jit(solution)/shard_map/all_to_all | solution.py:256
  19.5 24.8 %copy-start.2 = (s32[256,1]{0,1:T(1,128)S(1)}, s32[256,1]{0,1:T(1,128)}, u32[]{:S(2)}) copy-start(s32[256,1]{0,1:T(1,128)} %param.12) | copy-start | bytes 3076
  19.5 25.6 %copy-start.3 = (s32[256]{0:T(256)S(1)}, s32[256]{0:T(256)}, u32[]{:S(2)}) copy-start(s32[256]{0:T(256)} %param.13) | copy-start | bytes 3076
  35.8 0.8 copy-start.1
  41.6 19.0 %all-to-all-start.1 = ((bf16[32,4,8,256]{3,2,1,0:T(8,128)(2,1)}), bf16[32,4,8,256]{3,2,1,0:T(8,128)(2,1)S(1)}, u32[]{:S(2)}, u32[]{:S(2)}) async-start(bf16[32,4,8,256]{3,2,1,0:T(8,128)(2,1)} %get-tuple-element.11), calls=%async_computation.1 | async-start | bytes 1048576 | tf_op jit(solution)/shard_map/all_to_all | solution.py:275
  60.6 0.8 copy-start
  72.3 9.7 %all-to-all-start.3 = ((s32[32,1,16]{2,1,0:T(1,128)}), s32[32,1,16]{2,1,0:T(1,128)S(1)}, u32[]{:S(2)}, u32[]{:S(2)}) async-start(s32[32,1,16]{2,1,0:T(1,128)} %bitcast.10), calls=%async_computation.3 | async-start | bytes 32768 | tf_op jit(solution)/shard_map/all_to_all | solution.py:307
  82.0 30.2 %all-to-all-start.2 = ((bf16[8,32,16,128]{3,2,0,1:T(8,128)(2,1)}), bf16[8,32,16,128]{3,2,0,1:T(8,128)(2,1)S(1)}, u32[]{:S(2)}, u32[]{:S(2)}) async-start(bf16[8,32,16,128]{3,2,0,1:T(8,128)(2,1)} %copy.17), calls=%async_computation.2 | async-start | bytes 2097152 | tf_op jit(solution)/shard_map/all_to_all | solution.py:304

commit v2 on v1

v2 whole, which is shorter than its diff:
```python
import functools
import math

import jax
import jax.numpy as jnp
from jax import lax
from jax.experimental import pallas as pl
from jax.experimental.pallas import tpu as pltpu
from jax.sharding import PartitionSpec as P

SEG = 128
CHUNK = 256
PACK = 16
BF = jnp.bfloat16
F32 = jnp.float32


def cos_sin(turns, quarter, scale):
    bits = int(math.log2(quarter))
    turns = turns & (4 * quarter - 1)
    octant = (turns + quarter // 2) >> bits
    angle = (turns - (octant << bits)).astype(F32) * (math.pi / (2 * quarter))
    square = angle * angle
    sin_part = angle * scale + (angle * scale) * square * (
        -1.6666654611e-1 + square * (8.3321608736e-3 - square * 1.9515295891e-4)
    )
    cos_part = scale - square * (0.5 * scale) + (square * scale) * square * (
        4.166664568298827e-2 + square * (-1.388731625493765e-3 + square * 2.443315711809948e-5)
    )
    swap = (octant & 1) == 1
    cos_out = jnp.where(swap, sin_part, cos_part)
    sin_out = jnp.where(swap, cos_part, sin_part)
    cos_out = jnp.where(((octant + 1) & 2) == 2, -cos_out, cos_out)
    sin_out = jnp.where((octant & 2) == 2, -sin_out, sin_out)
    return cos_out, sin_out


def iota(shape, dim):
    return lax.broadcasted_iota(jnp.int32, shape, dim)


def turned(cos_0, sin_0, cos_1, sin_1):
    rows, width = cos_0.shape
    cos_out, sin_out = [], []
    for j in range(cos_1.shape[0]):
        cos_j = jnp.broadcast_to(cos_1[j:j + 1], (rows, width))
        sin_j = jnp.broadcast_to(sin_1[j:j + 1], (rows, width))
        cos_out.append(cos_0 * cos_j - sin_0 * sin_j)
        sin_out.append(sin_0 * cos_j + cos_0 * sin_j)
    return jnp.concatenate(cos_out, axis=0), jnp.concatenate(sin_out, axis=0)


def fine_table(quarter, angles):
    width = angles.shape[-1]
    steps = SEG // 8
    step = iota((2 * steps, width), 0)
    start = (step // steps) * (quarter // 2) + (step & (steps - 1)) * 8
    cos_0, sin_0 = cos_sin(iota((8, width), 0) * angles, quarter, 1.0 / math.sqrt(quarter))
    cos_1, sin_1 = cos_sin(start * angles, quarter, 1.0)
    return turned(cos_0, sin_0, cos_1, sin_1)


def coarse_table(quarter, rows_dev, angles):
    width = angles.shape[-1]
    tiles = quarter // SEG // 2
    group = 8 // rows_dev
    cos_0, sin_0 = cos_sin((iota((8, width), 0) // rows_dev) * SEG * angles, quarter, 1.0)
    start = iota((tiles // group, width), 0) * (group * SEG)
    cos_1, sin_1 = cos_sin(start * angles, quarter, 1.0)
    return turned(cos_0, sin_0, cos_1, sin_1)


def rotation(cos_part, sin_part):
    cos_part, sin_part = cos_part.astype(BF), sin_part.astype(BF)
    return jnp.concatenate(
        [
            jnp.concatenate([cos_part, -sin_part], axis=1),
            jnp.concatenate([sin_part, cos_part], axis=1),
        ],
        axis=0,
    )


def forward_kernel(quarter, rows_dev, angle_ref, cur_ref, f_ref, lhs):
    points = rows_dev * quarter // SEG // 2
    width = angle_ref.shape[-1]

    @pl.when(pl.program_id(0) == 0)
    def _():
        for f in range(2):
            for c in range(2):
                for half in range(2):
                    part = pl.ds(half * points, points)
                    spot = (2 * c + half) * SEG
                    j = [cur_ref[f, k, c, part, :].astype(F32) for k in range(4)]
                    lhs[2 * f * points:(2 * f + 1) * points, spot:spot + SEG] = (j[0] + j[3]).astype(BF)
                    lhs[(2 * f + 1) * points:(2 * f + 2) * points, spot:spot + SEG] = (j[1] - j[2]).astype(BF)

    angles = angle_ref[0]
    table = rotation(*fine_table(quarter, angles))
    cos_a, sin_a = coarse_table(quarter, rows_dev, angles)
    low = iota((8, width), 0) < 4
    for fp in range(4):
        grid_sum = jnp.dot(
            lhs[pl.ds(fp * points, points), :], table, preferred_element_type=F32
        )
        real, imag = grid_sum[:, :width], grid_sum[:, width:]
        out_re = jnp.sum((real * cos_a + imag * sin_a).reshape(points // 8, 8, width), axis=0)
        out_im = jnp.sum((imag * cos_a - real * sin_a).reshape(points // 8, 8, width), axis=0)
        out_re = out_re + pltpu.roll(out_re, 4, 0)
        out_im = out_im + pltpu.roll(out_im, 4, 0)
        out = jnp.where(low, out_re, out_im).astype(BF)
        for copy in range(f_ref.shape[0]):
            f_ref[copy, 0, fp] = out


def prepare_kernel(
    quarter, rows_dev, devices, angle_ref, row_ref, owner_ref, slot_ref,
    w_ref, t_ref, r_ref, choose_ref, mark_ref,
):
    points = owner_ref.shape[0]
    slots, units = choose_ref.shape[0], mark_ref.shape[0]
    depth, share_u = r_ref.shape[0], row_ref.shape[1]
    angles = angle_ref[0]
    w_ref[0] = rotation(*fine_table(quarter, angles))
    t_ref[0, 0], t_ref[0, 1] = coarse_table(quarter, rows_dev, angles)

    @pl.when(pl.program_id(0) == 0)
    def _():
        row = iota((depth, share_u), 0)
        x = (row // (2 * rows_dev)) * rows_dev + (row & (rows_dev - 1))
        is_imag = (row & rows_dev) == rows_dev
        scale = 1.0 / math.sqrt(rows_dev * devices)
        cos_x, sin_x = cos_sin(x * row_ref[...], quarter, scale)
        r_ref[:, :share_u] = jnp.where(is_imag, sin_x, cos_x).astype(BF)
        r_ref[:, share_u:] = jnp.where(is_imag, cos_x, -sin_x).astype(BF)

    @pl.when(pl.program_id(0) == 1)
    def _():
        segs = points // rows_dev
        cap = slots // devices
        point = iota((points, points), 1)
        point = (point & (rows_dev - 1)) * segs + (point // rows_dev)
        source = iota((points, points), 0)
        owner_col = owner_ref[...]
        owner_row = jnp.sum(jnp.where(source == point, owner_col, 0), axis=0, keepdims=True)
        same = jnp.where((source < point) & (owner_col == owner_row), 1, 0)
        place = owner_row * cap + jnp.sum(same, axis=0, keepdims=True)
        hit = iota((slots, points), 0) == place
        choose_ref[...] = jnp.where(hit, 1.0, 0.0).astype(BF)
        slot_col = slot_ref[...]
        slot_row = jnp.sum(jnp.where(source == point, slot_col, 0), axis=0, keepdims=True)
        marks = jnp.sum(jnp.where(hit, slot_row + 1, 0), axis=1, keepdims=True)
        marks = jnp.broadcast_to(marks, (slots, SEG)).reshape(units, 2, PACK // 2, SEG)
        marks = jnp.where(iota((PACK // 2, SEG), 1) < SEG // 2, marks[:, 0], marks[:, 1])
        mark_ref[...] = marks.astype(F32).astype(BF)


def middle_kernel(table, got_ref, target_ref, weight_ref, int_ref, back_ref):
    devices, pairs, rows, share_v = got_ref.shape
    depth = devices * rows
    share_u = table.shape[1] // 2

    mixed = []
    for p in range(2):
        plane = got_ref[:, p].astype(F32).reshape(depth, share_v).astype(BF)
        mixed.append(
            lax.dot_general(plane, table[...], (((0,), (0,)), ((), ())), preferred_element_type=F32)
        )
    power = mixed[0] * mixed[0] + mixed[1] * mixed[1]
    intensity = power[:, :share_u] + power[:, share_u:]
    int_ref[0] = intensity
    factor = 4.0 * weight_ref[0] * (intensity - target_ref[0])
    factor = jnp.concatenate([factor, factor], axis=1)
    for p in range(2):
        far_grad = (factor * mixed[p]).astype(BF)
        back = lax.dot_general(
            table[...], far_grad, (((1,), (1,)), ((), ())), preferred_element_type=F32
        )
        back_ref[:, p] = back.reshape(devices, rows, share_v).astype(BF)


def adjoint_kernel(got_ref, w_ref, t_ref, choose_ref, mark_ref, out_ref, total):
    points, width = t_ref.shape[2], t_ref.shape[3]
    units = out_ref.shape[0]
    step = pl.program_id(0)

    @pl.when(step == 0)
    def _():
        total[...] = jnp.zeros_like(total)

    cos_a, sin_a = t_ref[0, 0], t_ref[0, 1]
    low = iota((8, width), 0) < 4
    parts = []
    for fp in range(4):
        plane = jnp.sum(got_ref[:, 0, fp].astype(F32), axis=0)
        other = pltpu.roll(plane, 4, 0)
        real = jnp.where(low, plane, other)
        imag = jnp.where(low, other, plane)
        real = jnp.broadcast_to(real[None], (points // 8, 8, width)).reshape(points, width)
        imag = jnp.broadcast_to(imag[None], (points // 8, 8, width)).reshape(points, width)
        parts.append(
            jnp.concatenate(
                [
                    (cos_a * real - sin_a * imag).astype(BF),
                    (cos_a * imag + sin_a * real).astype(BF),
                ],
                axis=1,
            )
        )
    lhs = jnp.concatenate(parts, axis=0)
    total[...] += lax.dot_general(
        lhs, w_ref[0], (((1,), (1,)), ((), ())), preferred_element_type=F32
    )

    @pl.when(step == pl.num_programs(0) - 1)
    def _():
        for fp in range(4):
            block = total[fp * points:(fp + 1) * points, :].astype(BF)
            halves = []
            for half in range(2):
                spots = [(2 * c + half) * SEG for c in range(2)]
                halves.append(jnp.concatenate([block[:, i:i + SEG] for i in spots], axis=1))
            block = jnp.concatenate(halves, axis=0)
            sent = jnp.dot(choose_ref[...], block, preferred_element_type=F32).astype(BF)
            sent = sent.reshape(units, PACK, 2 * SEG)
            for c in range(2):
                rows = pl.ds((2 * fp + c) * PACK, PACK)
                out_ref[:, rows, :] = sent[:, :, c * SEG:(c + 1) * SEG]
        out_ref[:, 8 * PACK:, :] = mark_ref[...]


def faces_kernel(got_ref, out_ref):
    faces = out_ref.shape[3]
    units = got_ref.shape[0]
    slots = units * PACK
    marks = got_ref[:, 8 * PACK:, :].astype(F32)
    marks = jnp.concatenate([marks[:, :, :1], marks[:, :, SEG // 2:SEG // 2 + 1]], axis=1)
    marks = jnp.broadcast_to(marks.reshape(slots, 1), (slots, faces))
    hit = iota((slots, faces), 1) + 1 == marks.astype(jnp.int32)
    choose = jnp.where(hit, 1.0, 0.0).astype(BF)
    for f in range(2):
        for p in range(2):
            for c in range(2):
                rows = pl.ds((4 * f + 2 * p + c) * PACK, PACK)
                block = got_ref[:, rows, :].reshape(slots, SEG)
                found = lax.dot_general(
                    choose, block, (((0,), (0,)), ((), ())), preferred_element_type=F32
                )
                if p == 0:
                    out_ref[f, 0, c] = found
                    out_ref[f, 3, c] = found
                else:
                    out_ref[f, 1, c] = found
                    out_ref[f, 2, c] = -found


def exchange_small(outgoing, axes, devices, cap):
    units = outgoing.shape[0]
    rows = outgoing[:, :8 * PACK].reshape(units, 8, PACK, SEG).transpose(1, 0, 2, 3)
    rows = rows.reshape(8, devices, cap, SEG)
    marks = outgoing[:, 8 * PACK:, ::SEG // 2].transpose(0, 2, 1).reshape(devices, cap)
    rows = lax.all_to_all(rows, axes, split_axis=1, concat_axis=1, tiled=True)
    marks = lax.all_to_all(marks, axes, split_axis=0, concat_axis=0, tiled=True)
    rows = rows.reshape(8, units, PACK, SEG).transpose(1, 0, 2, 3).reshape(units, 8 * PACK, SEG)
    marks = marks.reshape(units, 2, PACK // 2).transpose(0, 2, 1)
    marks = jnp.repeat(marks, SEG // 2, axis=2)
    return jnp.concatenate([rows, marks], axis=1)


def params():
    return pltpu.CompilerParams(
        dimension_semantics=("arbitrary",), vmem_limit_bytes=24 * 1024 * 1024
    )


def cost(flops, moved):
    return pl.CostEstimate(flops=int(flops), bytes_accessed=int(moved), transcendentals=0)


def whole(shape):
    return pl.BlockSpec(shape, lambda i: (0,) * len(shape))


def body(currents, row_angles, column_angles, target, weight, tile_owner, face_slot):
    row_count = lax.axis_size("row")
    tile_count = lax.axis_size("tile")
    devices = row_count * tile_count
    freq_count, comp_count, part_count, rows_dev, columns = currents.shape
    far_rows = row_angles.shape[0]
    far_cols = column_angles.shape[0]
    share_v = far_cols // tile_count
    share_u = far_rows // row_count
    chunks = far_cols // CHUNK
    tiles = columns // SEG
    points = rows_dev * tiles
    both = ("row", "tile")

    half = points // 2
    seg_count = points
    slots = 2 * seg_count
    cap = slots // devices
    units = slots // PACK
    held = 8 * PACK + PACK // 2
    depth = devices * 2 * rows_dev
    angles = column_angles.reshape(chunks, 1, CHUNK)
    angle_spec = pl.BlockSpec((1, 1, CHUNK), lambda i: (i, 0, 0))
    table_spec = pl.BlockSpec((1, 4 * SEG, 2 * CHUNK), lambda i: (i, 0, 0))
    turn_spec = pl.BlockSpec((1, 2, half, CHUNK), lambda i: (i, 0, 0, 0))

    cur = currents.reshape(freq_count, comp_count, part_count, rows_dev, tiles, SEG)
    cur = cur.transpose(0, 1, 2, 4, 3, 5).reshape(freq_count, comp_count, part_count, points, SEG)
    copies = row_count if share_v == CHUNK else 1
    plane = pl.pallas_call(
        functools.partial(forward_kernel, columns, rows_dev),
        grid=(chunks,),
        in_specs=[angle_spec, whole(cur.shape)],
        out_specs=pl.BlockSpec((copies, 1, 4, 2 * rows_dev, CHUNK), lambda i: (0, i, 0, 0, 0)),
        out_shape=jax.ShapeDtypeStruct((copies, chunks, 4, 2 * rows_dev, CHUNK), BF),
        scratch_shapes=[pltpu.VMEM((4 * half, 4 * SEG), BF)],
        compiler_params=params(),
        cost_estimate=cost(4.3e9, 1.6e6),
        name="columns",
    )(angles, cur)

    if share_v != CHUNK:
        plane = plane.reshape(chunks, 4, 2 * rows_dev, CHUNK // share_v, share_v)
        plane = plane.transpose(0, 3, 1, 2, 4).reshape(1, tile_count, 4, 2 * rows_dev, share_v)
        plane = jnp.broadcast_to(plane, (row_count,) + plane.shape[1:])
    plane = plane.reshape(devices, 4, 2 * rows_dev, share_v)
    own_angles = lax.dynamic_slice_in_dim(row_angles, lax.axis_index("row") * share_u, share_u)
    angles, own_angles, owner, slot, plane = lax.optimization_barrier(
        (angles, own_angles, tile_owner, face_slot.reshape(seg_count, 1), plane)
    )
    table, turn, row_table, choose, mark = pl.pallas_call(
        functools.partial(prepare_kernel, columns, rows_dev, devices),
        grid=(chunks,),
        in_specs=[angle_spec, whole((1, share_u)), whole((seg_count, 1)), whole((seg_count, 1))],
        out_specs=[
            table_spec,
            turn_spec,
            whole((depth, 2 * share_u)),
            whole((slots, points)),
            whole((units, PACK // 2, SEG)),
        ],
        out_shape=[
            jax.ShapeDtypeStruct((chunks, 4 * SEG, 2 * CHUNK), BF),
            jax.ShapeDtypeStruct((chunks, 2, half, CHUNK), F32),
            jax.ShapeDtypeStruct((depth, 2 * share_u), BF),
            jax.ShapeDtypeStruct((slots, points), BF),
            jax.ShapeDtypeStruct((units, PACK // 2, SEG), BF),
        ],
        compiler_params=params(),
        cost_estimate=cost(4e9, 8e6),
        name="prepare",
    )(angles, own_angles.reshape(1, share_u), owner, slot)
    got = lax.all_to_all(plane, both, split_axis=0, concat_axis=0, tiled=True)

    pair = pl.BlockSpec((devices, 2, 2 * rows_dev, share_v), lambda i: (0, i, 0, 0))
    far = pl.BlockSpec((1, share_v, share_u), lambda i: (i, 0, 0))
    intensity, back = pl.pallas_call(
        middle_kernel,
        grid=(freq_count,),
        in_specs=[whole((depth, 2 * share_u)), pair, far, far],
        out_specs=[far, pair],
        out_shape=[
            jax.ShapeDtypeStruct((freq_count, share_v, share_u), F32),
            jax.ShapeDtypeStruct((devices, 4, 2 * rows_dev, share_v), BF),
        ],
        compiler_params=params(),
        cost_estimate=cost(1.1e9, 5e6),
        name="objective",
    )(row_table, got, target, weight)

    back = lax.all_to_all(back, both, split_axis=0, concat_axis=0, tiled=True)
    back = back.reshape(row_count, tile_count, 4, 2 * rows_dev, share_v)
    if share_v != CHUNK:
        back = back.reshape(row_count, chunks, CHUNK // share_v, 4, 2 * rows_dev, share_v)
        back = back.transpose(0, 1, 3, 4, 2, 5).reshape(row_count, chunks, 4, 2 * rows_dev, CHUNK)

    outgoing = pl.pallas_call(
        adjoint_kernel,
        grid=(chunks,),
        in_specs=[
            pl.BlockSpec((row_count, 1, 4, 2 * rows_dev, CHUNK), lambda i: (0, i, 0, 0, 0)),
            table_spec,
            turn_spec,
            whole((slots, points)),
            whole((units, PACK // 2, SEG)),
        ],
        out_specs=whole((units, held, SEG)),
        out_shape=jax.ShapeDtypeStruct((units, held, SEG), BF),
        scratch_shapes=[pltpu.VMEM((4 * half, 4 * SEG), F32)],
        compiler_params=params(),
        cost_estimate=cost(4.3e9, 8e6),
        name="adjoint",
    )(back, table, turn, choose, mark)

    if cap == PACK:
        arrived = lax.all_to_all(outgoing, both, split_axis=0, concat_axis=0, tiled=True)
    else:
        arrived = exchange_small(outgoing, both, devices, cap)
    out_shape = (freq_count, comp_count, part_count, seg_count, SEG)
    faces = pl.pallas_call(
        faces_kernel,
        grid=(1,),
        in_specs=[whole((units, held, SEG))],
        out_specs=whole(out_shape),
        out_shape=jax.ShapeDtypeStruct(out_shape, F32),
        compiler_params=params(),
        name="faces",
    )(arrived)
    return (intensity, faces)


def solution(mesh):
    in_specs = (
        P(None, None, None, ("row", "tile"), None),
        P(),
        P(),
        P(None, "tile", "row"),
        P(None, "tile", "row"),
        P(("row", "tile"), None),
        P(("row", "tile")),
    )
    out_specs = (P(None, "tile", "row"), P(None, None, None, ("row", "tile"), None))
    return jax.shard_map(body, mesh=mesh, in_specs=in_specs, out_specs=out_specs, check_vma=False)
```

time: 117 us -> 93.6 us (0.80)
  waiting for transfers between devices: 60 us -> 8.91 us
  blocking collectives: 0 us -> 49.7 us
  Pallas kernels: 28.9 us -> 18 us
  starting transfers between devices: 15.1 us -> 7.32 us
  other arithmetic: 1.76 us -> 0 us
  local copies, waits for them, and re-layouts: 10.1 us -> 8.55 us
    all_to_all x0 -> x2, blocking collectives: none -> 49.7 us  [the longest x1 31.2 us: body(): lax.all_to_all(outgoing, both, split_axis=0, concat_axis=0, tiled=True)]
    all_to_all x3 -> x0, waiting for transfers between devices: 45.1 us -> none  [the longest x1 25.7 us: body(): lax.all_to_all(outgoing.reshape(8, devices, cap, SEG), both, split_axis=1...]
    all_to_all x3 -> x0, starting transfers between devices: 7.79 us -> none  [the longest x1 2.65 us: body(): lax.all_to_all(outgoing.reshape(8, devices, cap, SEG), both, split_axis=1...]
    all_to_all x1, waiting for transfers between devices: 15 us -> 8.91 us  [body(): got = lax.all_to_all(plane, both, split_axis=0, concat_axis=0, tiled=True)]
    pallas_call x1, Pallas kernels: 11.5 us -> 5.53 us  [body(): pl.pallas_call(functools.partial(forward_kernel, columns, rows_dev), grid...]
    unnamed x9 -> x26, local copies, waits for them, and re-layouts: 2.42 us -> 7.52 us
    pallas_call x3 -> x4, Pallas kernels: 17.4 us -> 12.5 us  [the longest x1 4.48 us: body(): pl.pallas_call(adjoint_kernel, grid=(chunks,), in_specs=[pl.BlockSpec((ro...]
    reshape x3 -> x0, local copies, waits for them, and re-layouts: 3.93 us -> none  [the longest x1 2.49 us: body(): outgoing.reshape(8, devices, cap, SEG)]
  transfers between devices with their start and end apart: 4 -> 1, of which waited for: 4 -> 1; matrix products, arithmetic and copies ran while one was open for 6% -> 0% of each run, Pallas kernels for 0% -> 3%
where the time goes in v2:
time: 93.6 us; the launch traced here: 93.2 us
  blocking collectives  49.7 us (53%)
  Pallas kernels  18 us (19%)
  waiting for transfers between devices  8.91 us (10%)
  local copies, waits for them, and re-layouts  8.55 us (9%)
  starting transfers between devices  7.32 us (8%)
    all_to_all x1, blocking collectives, body(): lax.all_to_all(outgoing, both, split_axis=0, concat_axis=0, tiled=True)  31.2 us
    all_to_all x1, blocking collectives, body(): back = lax.all_to_all(back, both, split_axis=0, concat_axis=0, tiled=True)  18.4 us
    all_to_all x1, waiting for transfers between devices, body(): got = lax.all_to_all(plane, both, split_axis=0, concat_axis=0, tiled=True)  8.91 us
    unnamed x26, local copies, waits for them, and re-layouts  7.52 us
    all_to_all x1, starting transfers between devices, body(): got = lax.all_to_all(plane, both, split_axis=0, concat_axis=0, tiled=True)  7.32 us
    pallas_call x1, Pallas kernels, body(): pl.pallas_call(functools.partial(forward_kernel, columns, rows_dev), grid...  5.53 us
    pallas_call x1, Pallas kernels, body(): pl.pallas_call(adjoint_kernel, grid=(chunks,), in_specs=[pl.BlockSpec((ro...  4.48 us
    pallas_call x1, Pallas kernels, body(): pl.pallas_call(functools.partial(prepare_kernel, columns, rows_dev, devic...  3.11 us
  transfers between devices with their start and end apart: 1, of which 1 were waited for; matrix products, arithmetic and copies ran while one was open for 0% of the time, Pallas kernels for 3%

profile of v2, /device:TPU:0, one launch (start us, length us, event | category | flops | bytes accessed | tf_op | source)
XLA Modules:
  0.0 93.2 jit_solution(10163307119769697114)
XLA Ops:
  0.6 0.8 dynamic_slice.3
  1.4 0.0 copy-start
  1.4 1.2 %copy-done = bf16[2,4,2,4,8192]{4,3,2,1,0:T(4,128)(2,1)S(1)} copy-done((bf16[2,4,2,4,8192]{4,3,2,1,0:T(4,128)(2,1)S(1)}, bf16[2,4,2,4,8192]{4,3,2,1,0:T(4,128)(2,1)}, u32[]{:S(2)}) %copy-start) | copy-done | bytes 1048600
  2.6 0.0 copy-start.3
  2.6 0.7 copy-done.3
  3.3 0.0 copy-start.11
  3.3 0.0 copy-start.12
  3.3 0.0 copy-start.4
  3.3 5.5 %columns.1 = bf16[4,8,4,8,256]{4,3,2,1,0:T(8,128)(2,1)} custom-call(s32[8,1,256]{2,1,0:T(1,128)S(1)} %bitcast.13, bf16[2,4,2,256,128]{4,3,2,1,0:T(8,128)(2,1)S(1)} %bitcast.12), custom_call_target="tpu_custom_call" | custom-call | flops 4300000256 | bytes 1600000 | tf_op jit(solution)/shard_map/columns/pallas_call | solution.py:314
  8.9 7.3 %all-to-all-start = ((bf16[32,4,8,256]{3,2,1,0:T(8,128)(2,1)}), bf16[32,4,8,256]{3,2,1,0:T(8,128)(2,1)S(1)}, u32[]{:S(2)}, u32[]{:S(2)}) async-start(bf16[32,4,8,256]{3,2,1,0:T(8,128)(2,1)} %bitcast.5), calls=%async_computation | async-start | bytes 1048576 | tf_op jit(solution)/shard_map/all_to_all | solution.py:357
  16.2 0.0 copy-done.11
  16.2 0.1 copy.12.owner_ref
  16.3 0.0 copy-done.12
  16.3 0.1 copy.13.slot_ref
  16.5 0.0 copy-done.4
  16.5 0.0 copy-start.1
  16.5 0.0 copy-start.2
  16.5 3.1 %prepare.1 = (bf16[8,512,512]{2,1,0:T(8,128)(2,1)S(1)}, f32[8,2,128,256]{3,2,1,0:T(8,128)S(1)}, bf16[256,1024]{1,0:T(8,128)(2,1)S(1)}, bf16[512,256]{1,0:T(8,128)(2,1)S(1)}, bf16[32,8,128]{2,1,0:T(8,128)(2,1)S(1)}) custom-call(s32[8,1,256]{2,1,0:T(1,128)S(1)} %bitcast.14, s32[1,512]{1,0:T(1,128)S(1)} %bitcast.11, s32[256,1]{1,0:T(8,128)S(1)} %copy.12.owner_ref, ...), custom_call_target="tpu_custom_call" | custom-call | flops 4000000000 | bytes 8000000 | tf_op jit(solution)/shard_map/prepare/pallas_call | solution.py:335
  19.6 0.0 copy-start.5
  19.6 2.0 %copy-done.5 = bf16[8,512,512]{2,1,0:T(8,128)(2,1)} copy-done((bf16[8,512,512]{2,1,0:T(8,128)(2,1)}, bf16[8,512,512]{2,1,0:T(8,128)(2,1)S(1)}, u32[]{:S(2)}) %copy-start.5) | copy-done | bytes 4194328
  21.6 0.0 copy-start.7
  21.6 1.3 %copy-done.7 = f32[8,2,128,256]{3,2,1,0:T(8,128)} copy-done((f32[8,2,128,256]{3,2,1,0:T(8,128)}, f32[8,2,128,256]{3,2,1,0:T(8,128)S(1)}, u32[]{:S(2)}) %copy-start.7) | copy-done | bytes 2097176
  22.9 0.0 copy-start.9
  22.9 0.7 copy-done.9
  23.6 8.9 %all-to-all-done.got_ref = bf16[32,4,8,256]{3,2,1,0:T(8,128)(2,1)S(1)} async-done(((bf16[32,4,8,256]{3,2,1,0:T(8,128)(2,1)}), bf16[32,4,8,256]{3,2,1,0:T(8,128)(2,1)S(1)}, u32[]{:S(2)}, u32[]{:S(2)}) %all-to-all-start) | async-done | bytes 524320 | tf_op jit(solution)/shard_map/all_to_all | solution.py:357
  32.5 0.0 copy-done.1
  32.5 0.0 copy-done.2
  32.5 0.0 copy-start.6
  32.5 0.0 copy-start.10
  32.5 2.6 %objective.1 = (f32[2,256,512]{2,1,0:T(8,128)}, bf16[32,4,8,256]{3,2,1,0:T(8,128)(2,1)S(1)}) custom-call(bf16[256,1024]{1,0:T(8,128)(2,1)S(1)} %get-tuple-element.18.table, bf16[32,4,8,256]{3,2,1,0:T(8,128)(2,1)S(1)} %all-to-all-done.got_ref, f32[2,256,512]{2,1,0:T(8,128)S(1)} %copy-done.1, f32[2,256,512]{2,1,0:T(8,128)S(1)} %copy-done.2), custom_call_target="tpu_custom_call" | custom-call | flops 1100000000 | bytes 5000000 | tf_op jit(solution)/shard_map/objective/pallas_call | solution.py:361
  35.2 18.4 %all_to_all.15 = bf16[32,4,8,256]{3,2,1,0:T(8,128)(2,1)S(1)} all-to-all(bf16[32,4,8,256]{3,2,1,0:T(8,128)(2,1)S(1)} %get-tuple-element.21), channel_id=1, replica_groups=mesh['row'=4,'tile'=8] {'row','tile'}, dimensions={0} | all-to-all | bytes 1048576 | tf_op jit(solution)/shard_map/all_to_all | solution.py:375
  53.6 0.0 copy-done.6
  53.6 0.0 copy-done.10
  53.6 0.0 copy-start.8
  53.6 1.6 %copy-done.8 = f32[8,2,128,256]{3,2,1,0:T(8,128)S(1)} copy-done((f32[8,2,128,256]{3,2,1,0:T(8,128)S(1)}, f32[8,2,128,256]{3,2,1,0:T(8,128)}, u32[]{:S(2)}) %copy-start.8) | copy-done | bytes 2097176
  55.2 4.5 %adjoint.1 = bf16[32,136,128]{2,1,0:T(8,128)(2,1)S(1)} custom-call(bf16[4,8,4,8,256]{4,3,2,1,0:T(8,128)(2,1)S(1)} %bitcast.10, bf16[8,512,512]{2,1,0:T(8,128)(2,1)S(1)} %copy-done.6, f32[8,2,128,256]{3,2,1,0:T(8,128)S(1)} %copy-done.8, bf16[512,256]{1,0:T(8,128)(2,1)S(1)} %copy-done.10, bf16[32,8,128]{2,1,0:T(8,128)(2,1)S(1)} %get-tuple-element.25.mark_ref), custom_call_target="tpu_custom_call" | custom-call | flops 4300000256 | bytes 8000000 | tf_op jit(solution)/shard_map/adjoint/pallas_call | solution.py:381
  59.7 31.2 %all_to_all.16.got_ref = bf16[32,136,128]{2,1,0:T(8,128)(2,1)S(1)} all-to-all(bf16[32,136,128]{2,1,0:T(8,128)(2,1)S(1)} %adjoint.1), channel_id=1, replica_groups=mesh['row'=4,'tile'=8] {'row','tile'}, dimensions={0} | all-to-all | bytes 2228224 | tf_op jit(solution)/shard_map/all_to_all | solution.py:400
  90.9 2.3 %faces.1 = f32[2,4,2,256,128]{4,3,2,1,0:T(8,128)} custom-call(bf16[32,136,128]{2,1,0:T(8,128)(2,1)S(1)} %all_to_all.16.got_ref), custom_call_target="tpu_custom_call" | custom-call | tf_op jit(solution)/shard_map/faces/pallas_call | solution.py:404
Async XLA Ops:
  1.4 1.2 %copy-start = (bf16[2,4,2,4,8192]{4,3,2,1,0:T(4,128)(2,1)S(1)}, bf16[2,4,2,4,8192]{4,3,2,1,0:T(4,128)(2,1)}, u32[]{:S(2)}) copy-start(bf16[2,4,2,4,8192]{4,3,2,1,0:T(4,128)(2,1)} %param.7) | copy-start | bytes 3145732
  2.6 0.7 copy-start.3
  3.3 12.9 %copy-start.11 = (s32[256,1]{0,1:T(1,128)S(1)}, s32[256,1]{0,1:T(1,128)}, u32[]{:S(2)}) copy-start(s32[256,1]{0,1:T(1,128)} %param.12) | copy-start | bytes 3076
  3.3 13.0 %copy-start.12 = (s32[256]{0:T(256)S(1)}, s32[256]{0:T(256)}, u32[]{:S(2)}) copy-start(s32[256]{0:T(256)} %param.13) | copy-start | bytes 3076
  3.3 13.2 %copy-start.4 = (s32[2048]{0:T(1024)S(1)}, s32[2048]{0:T(1024)}, u32[]{:S(2)}) copy-start(s32[2048]{0:T(1024)} %param.9) | copy-start | bytes 24580
  8.9 23.7 %all-to-all-start = ((bf16[32,4,8,256]{3,2,1,0:T(8,128)(2,1)}), bf16[32,4,8,256]{3,2,1,0:T(8,128)(2,1)S(1)}, u32[]{:S(2)}, u32[]{:S(2)}) async-start(bf16[32,4,8,256]{3,2,1,0:T(8,128)(2,1)} %bitcast.5), calls=%async_computation | async-start | bytes 1048576 | tf_op jit(solution)/shard_map/all_to_all | solution.py:357
  16.5 16.0 %copy-start.1 = (f32[2,256,512]{2,1,0:T(8,128)S(1)}, f32[2,256,512]{2,1,0:T(8,128)}, u32[]{:S(2)}) copy-start(f32[2,256,512]{2,1,0:T(8,128)} %target_ref.1) | copy-start | bytes 3145732
  16.5 16.0 %copy-start.2 = (f32[2,256,512]{2,1,0:T(8,128)S(1)}, f32[2,256,512]{2,1,0:T(8,128)}, u32[]{:S(2)}) copy-start(f32[2,256,512]{2,1,0:T(8,128)} %weight_ref.1) | copy-start | bytes 3145732
  19.6 2.0 %copy-start.5 = (bf16[8,512,512]{2,1,0:T(8,128)(2,1)}, bf16[8,512,512]{2,1,0:T(8,128)(2,1)S(1)}, u32[]{:S(2)}) copy-start(bf16[8,512,512]{2,1,0:T(8,128)(2,1)S(1)} %get-tuple-element.22.w_ref) | copy-start | bytes 12582916
  21.6 1.3 %copy-start.7 = (f32[8,2,128,256]{3,2,1,0:T(8,128)}, f32[8,2,128,256]{3,2,1,0:T(8,128)S(1)}, u32[]{:S(2)}) copy-start(f32[8,2,128,256]{3,2,1,0:T(8,128)S(1)} %get-tuple-element.23.t_ref) | copy-start | bytes 6291460
  22.9 0.7 copy-start.9
  32.5 21.1 %copy-start.6 = (bf16[8,512,512]{2,1,0:T(8,128)(2,1)S(1)}, bf16[8,512,512]{2,1,0:T(8,128)(2,1)}, u32[]{:S(2)}) copy-start(bf16[8,512,512]{2,1,0:T(8,128)(2,1)} %copy-done.5) | copy-start | bytes 12582916
  32.5 21.1 %copy-start.10 = (bf16[512,256]{1,0:T(8,128)(2,1)S(1)}, bf16[512,256]{1,0:T(8,128)(2,1)}, u32[]{:S(2)}) copy-start(bf16[512,256]{1,0:T(8,128)(2,1)} %copy-done.9) | copy-start | bytes 786436
  53.6 1.6 %copy-start.8 = (f32[8,2,128,256]{3,2,1,0:T(8,128)S(1)}, f32[8,2,128,256]{3,2,1,0:T(8,128)}, u32[]{:S(2)}) copy-start(f32[8,2,128,256]{3,2,1,0:T(8,128)} %copy-done.7) | copy-start | bytes 6291460

commit v3 on v2

v3 whole, which is shorter than its diff:
```python
import functools
import math

import jax
import jax.numpy as jnp
from jax import lax
from jax.experimental import pallas as pl
from jax.experimental.pallas import tpu as pltpu
from jax.sharding import PartitionSpec as P

SEG = 128
CHUNK = 256
PACK = 16
BOTH = ("row", "tile")
BF = jnp.bfloat16
F32 = jnp.float32


def cos_sin(turns, quarter, scale):
    bits = int(math.log2(quarter))
    turns = turns & (4 * quarter - 1)
    octant = (turns + quarter // 2) >> bits
    angle = (turns - (octant << bits)).astype(F32) * (math.pi / (2 * quarter))
    square = angle * angle
    sin_part = angle * scale + (angle * scale) * square * (
        -1.6666654611e-1 + square * (8.3321608736e-3 - square * 1.9515295891e-4)
    )
    cos_part = scale - square * (0.5 * scale) + (square * scale) * square * (
        4.166664568298827e-2 + square * (-1.388731625493765e-3 + square * 2.443315711809948e-5)
    )
    swap = (octant & 1) == 1
    cos_out = jnp.where(swap, sin_part, cos_part)
    sin_out = jnp.where(swap, cos_part, sin_part)
    cos_out = jnp.where(((octant + 1) & 2) == 2, -cos_out, cos_out)
    sin_out = jnp.where((octant & 2) == 2, -sin_out, sin_out)
    return cos_out, sin_out


def iota(shape, dim):
    return lax.broadcasted_iota(jnp.int32, shape, dim)


def turned(cos_0, sin_0, cos_1, sin_1):
    rows, width = cos_0.shape
    cos_out, sin_out = [], []
    for j in range(cos_1.shape[0]):
        cos_j = jnp.broadcast_to(cos_1[j:j + 1], (rows, width))
        sin_j = jnp.broadcast_to(sin_1[j:j + 1], (rows, width))
        cos_out.append(cos_0 * cos_j - sin_0 * sin_j)
        sin_out.append(sin_0 * cos_j + cos_0 * sin_j)
    return jnp.concatenate(cos_out, axis=0), jnp.concatenate(sin_out, axis=0)


def fine_table(quarter, angles):
    width = angles.shape[-1]
    steps = SEG // 8
    step = iota((2 * steps, width), 0)
    start = (step // steps) * (quarter // 2) + (step & (steps - 1)) * 8
    cos_0, sin_0 = cos_sin(iota((8, width), 0) * angles, quarter, 1.0 / math.sqrt(quarter))
    cos_1, sin_1 = cos_sin(start * angles, quarter, 1.0)
    return turned(cos_0, sin_0, cos_1, sin_1)


def coarse_table(quarter, rows_dev, angles):
    width = angles.shape[-1]
    tiles = quarter // SEG // 2
    group = 8 // rows_dev
    cos_0, sin_0 = cos_sin((iota((8, width), 0) // rows_dev) * SEG * angles, quarter, 1.0)
    start = iota((tiles // group, width), 0) * (group * SEG)
    cos_1, sin_1 = cos_sin(start * angles, quarter, 1.0)
    return turned(cos_0, sin_0, cos_1, sin_1)


def rotation(cos_part, sin_part):
    cos_part, sin_part = cos_part.astype(BF), sin_part.astype(BF)
    return jnp.concatenate(
        [
            jnp.concatenate([cos_part, -sin_part], axis=1),
            jnp.concatenate([sin_part, cos_part], axis=1),
        ],
        axis=0,
    )


def forward_kernel(quarter, rows_dev, angle_ref, cur_hbm, f_ref, cur_ref, lhs, sem):
    points = rows_dev * quarter // SEG // 2
    width = angle_ref.shape[-1]
    load = pltpu.make_async_copy(cur_hbm, cur_ref, sem)

    @pl.when(pl.program_id(0) == 0)
    def _():
        load.start()

    angles = angle_ref[0]
    table = rotation(*fine_table(quarter, angles))
    cos_a, sin_a = coarse_table(quarter, rows_dev, angles)

    @pl.when(pl.program_id(0) == 0)
    def _():
        load.wait()
        for f in range(2):
            for c in range(2):
                for half in range(2):
                    part = pl.ds(half * points, points)
                    spot = (2 * c + half) * SEG
                    j = [cur_ref[f, k, c, part, :].astype(F32) for k in range(4)]
                    lhs[2 * f * points:(2 * f + 1) * points, spot:spot + SEG] = (j[0] + j[3]).astype(BF)
                    lhs[(2 * f + 1) * points:(2 * f + 2) * points, spot:spot + SEG] = (j[1] - j[2]).astype(BF)

    low = iota((8, width), 0) < 4
    for fp in range(4):
        grid_sum = jnp.dot(
            lhs[pl.ds(fp * points, points), :], table, preferred_element_type=F32
        )
        real, imag = grid_sum[:, :width], grid_sum[:, width:]
        out_re = jnp.sum((real * cos_a + imag * sin_a).reshape(points // 8, 8, width), axis=0)
        out_im = jnp.sum((imag * cos_a - real * sin_a).reshape(points // 8, 8, width), axis=0)
        out_re = out_re + pltpu.roll(out_re, 4, 0)
        out_im = out_im + pltpu.roll(out_im, 4, 0)
        out = jnp.where(low, out_re, out_im).astype(BF)
        for copy in range(f_ref.shape[0]):
            f_ref[copy, 0, fp] = out


def row_kernel(quarter, rows_dev, row_count, tile_count, row_ref, r_ref):
    depth, share_u = r_ref.shape[0], row_ref.shape[1]
    core = lax.axis_index("row") & 1
    row = iota((depth, share_u), 0)
    unit = row // (2 * rows_dev)
    far = unit // (depth // (4 * rows_dev))
    unit = unit - far * (depth // (4 * rows_dev))
    group = (unit // tile_count) * 2 + jnp.where(far == 1, 1 - core, core)
    x = (group * tile_count + unit % tile_count) * rows_dev + row % rows_dev
    is_imag = row % (2 * rows_dev) >= rows_dev
    scale = 1.0 / math.sqrt(rows_dev * row_count * tile_count)
    cos_x, sin_x = cos_sin(x * row_ref[...], quarter, scale)
    r_ref[:, :share_u] = jnp.where(is_imag, sin_x, cos_x).astype(BF)
    r_ref[:, share_u:] = jnp.where(is_imag, cos_x, -sin_x).astype(BF)


def prepare_kernel(quarter, rows_dev, tile_count, cap, angle_ref, code_ref, w_ref, v_ref, t_ref, choose_ref, mark_ref):
    points = code_ref.shape[0]
    slots, units = choose_ref.shape[1], mark_ref.shape[0]
    angles = angle_ref[0]
    table = rotation(*fine_table(quarter, angles))
    w_ref[0], v_ref[0] = table[:, :CHUNK], table[:, CHUNK:]
    t_ref[0, 0], t_ref[0, 1] = coarse_table(quarter, rows_dev, angles)

    @pl.when(pl.program_id(0) == 0)
    def _():
        segs = points // rows_dev
        half = tile_count // 2
        mine = lax.axis_index("tile") // half
        point = iota((points, points), 1)
        point = (point % rows_dev) * segs + (point // rows_dev)
        source = iota((points, points), 0)
        lane = iota((PACK // 2, SEG), 1) // (SEG // 4)
        marked = jnp.zeros((units, PACK // 2, SEG), jnp.int32)
        for side in range(2):
            code_col = code_ref[:, side:side + 1]
            code_row = jnp.sum(jnp.where(source == point, code_col, 0), axis=0, keepdims=True)
            owner_col, owner_row = code_col // points, code_row // points
            same = jnp.where((source < point) & (owner_col == owner_row), 1, 0)
            rank = jnp.sum(same, axis=0, keepdims=True)
            tile = owner_row % tile_count
            place = ((owner_row // tile_count) * half + tile % half) * cap + rank
            place = jnp.where(tile // half == mine, place, -1)
            hit = iota((slots, points), 0) == place
            choose_ref[side] = jnp.where(hit, 1.0, 0.0).astype(BF)
            marks = jnp.sum(jnp.where(hit, code_row % points + 1, 0), axis=1, keepdims=True)
            marks = jnp.broadcast_to(marks, (slots, SEG)).reshape(units, 2, PACK // 2, SEG)
            for part in range(2):
                marked = jnp.where(lane == 2 * side + part, marks[:, part], marked)
        mark_ref[...] = marked.astype(F32).astype(BF)


def middle_kernel(table, own_ref, far_ref, target_ref, weight_ref, int_ref, back_ref, over_ref):
    count, pairs, rows, share_v = own_ref.shape
    depth = 2 * count * rows
    share_u = table.shape[1] // 2

    mixed = []
    for p in range(2):
        plane = jnp.concatenate([own_ref[:, p], far_ref[:, p]], axis=0)
        plane = plane.astype(F32).reshape(depth, share_v).astype(BF)
        mixed.append(
            lax.dot_general(plane, table[...], (((0,), (0,)), ((), ())), preferred_element_type=F32)
        )
    power = mixed[0] * mixed[0] + mixed[1] * mixed[1]
    intensity = power[:, :share_u] + power[:, share_u:]
    int_ref[0] = intensity
    factor = 4.0 * weight_ref[0] * (intensity - target_ref[0])
    factor = jnp.concatenate([factor, factor], axis=1)
    for p in range(2):
        far_grad = (factor * mixed[p]).astype(BF)
        back = lax.dot_general(
            table[...], far_grad, (((1,), (1,)), ((), ())), preferred_element_type=F32
        )
        back = back.reshape(2 * count, rows, share_v).astype(BF)
        back_ref[:, p] = back[:count]
        over_ref[:, p] = back[count:]


def fold_kernel(own_ref, got_ref, out_ref):
    for side in range(2):
        total = own_ref[:, side].astype(F32) + got_ref[:, side].astype(F32)
        total = total.astype(BF)
        out_ref[:, side, :, 0] = total
        out_ref[:, 1 - side, :, 1] = total


def adjoint_kernel(got_ref, w_ref, v_ref, t_ref, choose_ref, mark_ref, out_ref, total):
    points, width = t_ref.shape[2], t_ref.shape[3]
    units = out_ref.shape[0]
    step = pl.program_id(0)

    @pl.when(step == 0)
    def _():
        total[...] = jnp.zeros_like(total)

    cos_a, sin_a = t_ref[0, 0], t_ref[0, 1]
    low = iota((8, width), 0) < 4
    parts = []
    for side, fp in [(i, j) for i in range(2) for j in range(4)]:
        plane = jnp.sum(got_ref[:, 0, side, fp].astype(F32), axis=0)
        other = pltpu.roll(plane, 4, 0)
        real = jnp.where(low, plane, other)
        imag = jnp.where(low, other, plane)
        real = jnp.broadcast_to(real[None], (points // 8, 8, width)).reshape(points, width)
        imag = jnp.broadcast_to(imag[None], (points // 8, 8, width)).reshape(points, width)
        parts.append(
            jnp.concatenate(
                [
                    (cos_a * real - sin_a * imag).astype(BF),
                    (cos_a * imag + sin_a * real).astype(BF),
                ],
                axis=1,
            )
        )
    lhs = jnp.concatenate(parts, axis=0)
    total[...] += lax.dot_general(
        lhs, jnp.concatenate([w_ref[0], v_ref[0]], axis=1), (((1,), (1,)), ((), ())),
        preferred_element_type=F32,
    )

    @pl.when(step == pl.num_programs(0) - 1)
    def _():
        for side, fp in [(i, j) for i in range(2) for j in range(4)]:
            start = (4 * side + fp) * points
            block = total[start:start + points, :].astype(BF)
            halves = []
            for half in range(2):
                spots = [(2 * c + half) * SEG for c in range(2)]
                halves.append(jnp.concatenate([block[:, i:i + SEG] for i in spots], axis=1))
            block = jnp.concatenate(halves, axis=0)
            sent = jnp.dot(choose_ref[side], block, preferred_element_type=F32).astype(BF)
            sent = sent.reshape(units, PACK, 2 * SEG)
            for c in range(2):
                rows = pl.ds((8 * side + 2 * fp + c) * PACK, PACK)
                out_ref[:, rows, :] = sent[:, :, c * SEG:(c + 1) * SEG]
        out_ref[:, 16 * PACK:, :] = mark_ref[...]


def faces_kernel(got_ref, out_ref):
    faces = out_ref.shape[3]
    units = got_ref.shape[0]
    slots = units * PACK
    marks = got_ref[:, 16 * PACK:, :].astype(F32)
    hits = []
    for side in range(2):
        spots = [(2 * side + part) * (SEG // 4) for part in range(2)]
        mark = jnp.concatenate([marks[:, :, i:i + 1] for i in spots], axis=1)
        mark = jnp.broadcast_to(mark.reshape(slots, 1), (slots, faces)).astype(jnp.int32)
        hits.append(jnp.where(iota((slots, faces), 1) + 1 == mark, 1.0, 0.0).astype(BF))
    choose = jnp.concatenate(hits, axis=0)
    for f in range(2):
        for p in range(2):
            for c in range(2):
                blocks = []
                for side in range(2):
                    rows = pl.ds((8 * side + 4 * f + 2 * p + c) * PACK, PACK)
                    blocks.append(got_ref[:, rows, :].reshape(slots, SEG))
                found = lax.dot_general(
                    choose, jnp.concatenate(blocks, axis=0), (((0,), (0,)), ((), ())),
                    preferred_element_type=F32,
                )
                if p == 0:
                    out_ref[f, 0, c] = found
                    out_ref[f, 3, c] = found
                else:
                    out_ref[f, 1, c] = found
                    out_ref[f, 2, c] = -found


def exchange_small(outgoing, groups, cap):
    units = outgoing.shape[0]
    peers = units * PACK // cap
    swap = functools.partial(
        lax.all_to_all, axis_name=BOTH, split_axis=1, concat_axis=1, tiled=True, axis_index_groups=groups
    )
    rows = outgoing[:, :16 * PACK].reshape(units, 16, PACK, SEG).transpose(1, 0, 2, 3)
    rows = swap(rows.reshape(16, peers, cap, SEG))
    rows = rows.reshape(16, units, PACK, SEG).transpose(1, 0, 2, 3).reshape(units, 16 * PACK, SEG)
    marks = outgoing[:, 16 * PACK:, ::SEG // 4].reshape(units, PACK // 2, 2, 2).transpose(2, 0, 3, 1)
    marks = swap(marks.reshape(2, peers, cap)).reshape(2, units, 2, PACK // 2)
    marks = marks.transpose(1, 3, 0, 2).reshape(units, PACK // 2, 4)
    return jnp.concatenate([rows, jnp.repeat(marks, SEG // 4, axis=2)], axis=1)


def params(mib=24):
    return pltpu.CompilerParams(
        dimension_semantics=("arbitrary",), vmem_limit_bytes=mib * 1024 * 1024
    )


def cost(flops, moved):
    return pl.CostEstimate(flops=int(flops), bytes_accessed=int(moved), transcendentals=0)


def whole(shape):
    return pl.BlockSpec(shape, lambda i: (0,) * len(shape))


def body(currents, row_angles, column_angles, target, weight, tile_owner, face_slot):
    row_count = lax.axis_size("row")
    tile_count = lax.axis_size("tile")
    devices = row_count * tile_count
    freq_count, comp_count, part_count, rows_dev, columns = currents.shape
    far_rows = row_angles.shape[0]
    far_cols = column_angles.shape[0]
    share_v = far_cols // tile_count
    share_u = far_rows // row_count
    chunks = far_cols // CHUNK
    tiles = columns // SEG
    points = rows_dev * tiles
    half = points // 2
    cap = 2 * points // devices
    slots = points
    units = slots // PACK
    held = 16 * PACK + PACK // 2
    pairs = row_count // 2
    peers = pairs * tile_count
    wide = 2 * rows_dev
    depth = devices * wide
    tile_half = tile_count // 2
    core_groups = [
        [(2 * x + core) * tile_count + t for x in range(pairs) for t in range(tile_count)]
        for core in range(2)
    ]
    half_groups = [
        [r * tile_count + side * tile_half + t for r in range(row_count) for t in range(tile_half)]
        for side in range(2)
    ]
    core_swap = [(i, i ^ 1) for i in range(row_count)]
    mirror = [(i, (i + tile_half) % tile_count) for i in range(tile_count)]
    angles = column_angles.reshape(chunks, 1, CHUNK)
    angle_spec = pl.BlockSpec((1, 1, CHUNK), lambda i: (i, 0, 0))
    table_spec = pl.BlockSpec((1, 4 * SEG, CHUNK), lambda i: (i, 0, 0))
    turn_spec = pl.BlockSpec((1, 2, half, CHUNK), lambda i: (i, 0, 0, 0))

    cur = currents.reshape(freq_count, comp_count, part_count, rows_dev, tiles, SEG)
    cur = cur.transpose(0, 1, 2, 4, 3, 5).reshape(freq_count, comp_count, part_count, points, SEG)
    copies = pairs if share_v == CHUNK else 1
    plane = pl.pallas_call(
        functools.partial(forward_kernel, columns, rows_dev),
        grid=(chunks,),
        in_specs=[angle_spec, pl.BlockSpec(memory_space=pltpu.HBM)],
        out_specs=pl.BlockSpec((copies, 1, 4, wide, CHUNK), lambda i: (0, i, 0, 0, 0)),
        out_shape=jax.ShapeDtypeStruct((copies, chunks, 4, wide, CHUNK), BF),
        scratch_shapes=[
            pltpu.VMEM(cur.shape, BF),
            pltpu.VMEM((4 * half, 4 * SEG), BF),
            pltpu.SemaphoreType.DMA(()),
        ],
        compiler_params=params(58),
        cost_estimate=cost(4.3e9, 1.6e6),
        name="columns",
    )(angles, cur)
    if share_v != CHUNK:
        plane = plane.reshape(chunks, 4, wide, CHUNK // share_v, share_v)
        plane = plane.transpose(0, 3, 1, 2, 4).reshape(1, tile_count, 4, wide, share_v)
        plane = jnp.broadcast_to(plane, (pairs,) + plane.shape[1:])
    plane = plane.reshape(peers, 4, wide, share_v)

    own = lax.all_to_all(plane, BOTH, 0, 0, tiled=True, axis_index_groups=core_groups)
    row_angles, owner, slot, own = lax.optimization_barrier(
        (row_angles, tile_owner, face_slot, own)
    )
    code = owner[:, 0] * points + slot
    code = jnp.stack([code, lax.ppermute(code, "tile", mirror)], axis=1)
    own_angles = lax.dynamic_slice_in_dim(row_angles, lax.axis_index("row") * share_u, share_u)
    row_table = pl.pallas_call(
        functools.partial(row_kernel, columns, rows_dev, row_count, tile_count),
        grid=(1,),
        in_specs=[whole((1, share_u))],
        out_specs=whole((depth, 2 * share_u)),
        out_shape=jax.ShapeDtypeStruct((depth, 2 * share_u), BF),
        compiler_params=params(),
        cost_estimate=cost(1e8, 5e5),
        name="rows",
    )(own_angles.reshape(1, share_u))
    other = lax.ppermute(own, "row", core_swap)

    pair = pl.BlockSpec((peers, 2, wide, share_v), lambda i: (0, i, 0, 0))
    far = pl.BlockSpec((1, share_v, share_u), lambda i: (i, 0, 0))
    back_shape = jax.ShapeDtypeStruct((peers, 4, wide, share_v), BF)
    intensity, back, over = pl.pallas_call(
        middle_kernel,
        grid=(freq_count,),
        in_specs=[whole((depth, 2 * share_u)), pair, pair, far, far],
        out_specs=[far, pair, pair],
        out_shape=[
            jax.ShapeDtypeStruct((freq_count, share_v, share_u), F32), back_shape, back_shape
        ],
        compiler_params=params(),
        cost_estimate=cost(1.1e9, 5e6),
        name="objective",
    )(row_table, own, other, target, weight)

    over = lax.ppermute(over, "row", core_swap)
    split = (pairs * 2, tile_half, 4, wide, share_v)
    part = pl.BlockSpec((1, 2, tile_half, 4, wide, share_v), lambda i: (i, 0, 0, 0, 0, 0))
    fold_out = (pairs, 2, tile_half, 2, 4, wide, share_v)
    back = pl.pallas_call(
        fold_kernel,
        grid=(pairs,),
        in_specs=[part, part],
        out_specs=pl.BlockSpec((1,) + fold_out[1:], lambda i: (i, 0, 0, 0, 0, 0, 0)),
        out_shape=jax.ShapeDtypeStruct(fold_out, BF),
        compiler_params=params(),
        cost_estimate=cost(1e6, 1e6),
        name="fold",
    )(back.reshape((pairs, 2) + split[1:]), over.reshape((pairs, 2) + split[1:]))

    angles, code, back = lax.optimization_barrier((angles, code, back))
    back = back.reshape(peers, 2, 4, wide, share_v)
    back = lax.all_to_all(back, BOTH, 0, 0, tiled=True, axis_index_groups=core_groups)
    table, table_im, turn, choose, mark = pl.pallas_call(
        functools.partial(prepare_kernel, columns, rows_dev, tile_count, cap),
        grid=(chunks,),
        in_specs=[angle_spec, whole((points, 2))],
        out_specs=[
            table_spec,
            table_spec,
            turn_spec,
            whole((2, slots, points)),
            whole((units, PACK // 2, SEG)),
        ],
        out_shape=[
            jax.ShapeDtypeStruct((chunks, 4 * SEG, CHUNK), BF),
            jax.ShapeDtypeStruct((chunks, 4 * SEG, CHUNK), BF),
            jax.ShapeDtypeStruct((chunks, 2, half, CHUNK), F32),
            jax.ShapeDtypeStruct((2, slots, points), BF),
            jax.ShapeDtypeStruct((units, PACK // 2, SEG), BF),
        ],
        compiler_params=params(),
        cost_estimate=cost(4e9, 8e6),
        name="prepare",
    )(angles, code)

    back = back.reshape(pairs, tile_count, 2, 4, wide, share_v)
    if share_v != CHUNK:
        back = back.reshape(pairs, chunks, CHUNK // share_v, 2, 4, wide, share_v)
        back = back.transpose(0, 1, 3, 4, 5, 2, 6).reshape(pairs, chunks, 2, 4, wide, CHUNK)
    outgoing = pl.pallas_call(
        adjoint_kernel,
        grid=(chunks,),
        in_specs=[
            pl.BlockSpec((pairs, 1, 2, 4, wide, CHUNK), lambda i: (0, i, 0, 0, 0, 0)),
            table_spec,
            table_spec,
            turn_spec,
            whole((2, slots, points)),
            whole((units, PACK // 2, SEG)),
        ],
        out_specs=whole((units, held, SEG)),
        out_shape=jax.ShapeDtypeStruct((units, held, SEG), BF),
        scratch_shapes=[pltpu.VMEM((8 * half, 4 * SEG), F32)],
        compiler_params=params(),
        cost_estimate=cost(8.6e9, 8e6),
        name="adjoint",
    )(back, table, table_im, turn, choose, mark)

    if cap == PACK:
        arrived = lax.all_to_all(outgoing, BOTH, 0, 0, tiled=True, axis_index_groups=half_groups)
    else:
        arrived = exchange_small(outgoing, half_groups, cap)
    out_shape = (freq_count, comp_count, part_count, points, SEG)
    faces = pl.pallas_call(
        faces_kernel,
        grid=(1,),
        in_specs=[whole((units, held, SEG))],
        out_specs=whole(out_shape),
        out_shape=jax.ShapeDtypeStruct(out_shape, F32),
        compiler_params=params(),
        name="faces",
    )(arrived)
    return (intensity, faces)


def solution(mesh):
    in_specs = (
        P(None, None, None, ("row", "tile"), None),
        P(),
        P(),
        P(None, "tile", "row"),
        P(None, "tile", "row"),
        P(("row", "tile"), None),
        P(("row", "tile")),
    )
    out_specs = (P(None, "tile", "row"), P(None, None, None, ("row", "tile"), None))
    return jax.shard_map(body, mesh=mesh, in_specs=in_specs, out_specs=out_specs, check_vma=False)
```

time: 93.6 us -> 87.3 us (0.933)
  blocking collectives: 49.7 us -> 37.4 us
  Pallas kernels: 18 us -> 24.2 us
  waiting for transfers between devices: 8.91 us -> 12.6 us
  starting transfers between devices: 7.32 us -> 5.05 us
  local copies, waits for them, and re-layouts: 8.55 us -> 6.75 us
    all_to_all x2, blocking collectives: 49.7 us -> 37.4 us  [the longest x1 19.2 us: body(): lax.all_to_all(outgoing, BOTH, 0, 0, tiled=True, axis_index_groups=half_g...]
    all_to_all x1, starting transfers between devices: 7.32 us -> 3.57 us  [body(): lax.all_to_all(back, BOTH, 0, 0, tiled=True, axis_index_groups=core_groups)]
    ppermute x0 -> x3, waiting for transfers between devices: none -> 3.56 us  [the longest x1 3.56 us: body(): code = jnp.stack([code, lax.ppermute(code, 'tile', mirror)], axis=1)]
    pallas_call x2 -> x4, Pallas kernels: 7.59 us -> 11.1 us  [the longest x1 6.7 us: body(): pl.pallas_call(adjoint_kernel, grid=(chunks,), in_specs=[pl.BlockSpec((pa...]
    pallas_call x1, Pallas kernels: 5.53 us -> 8.22 us  [body(): pl.pallas_call(functools.partial(forward_kernel, columns, rows_dev), grid...]
    unnamed x26 -> x18, local copies, waits for them, and re-layouts: 7.52 us -> 5.85 us
    ppermute x0 -> x3, starting transfers between devices: none -> 1.48 us  [the longest x1 0.98 us: body(): code = jnp.stack([code, lax.ppermute(code, 'tile', mirror)], axis=1)]
  transfers between devices with their start and end apart: 1 -> 4, of which waited for: 1 -> 2; matrix products, arithmetic and copies ran while one was open for 0% -> 1% of each run, Pallas kernels for 3% -> 4%
where the time goes in v3:
time: 87.3 us; the launch traced here: 86.8 us
  blocking collectives  37.4 us (43%)
  Pallas kernels  24.2 us (28%)
  waiting for transfers between devices  12.6 us (14%)
  local copies, waits for them, and re-layouts  6.75 us (8%)
  starting transfers between devices  5.05 us (6%)
    all_to_all x1, blocking collectives, body(): lax.all_to_all(outgoing, BOTH, 0, 0, tiled=True, axis_index_groups=half_g...  19.2 us
    all_to_all x1, blocking collectives, body(): lax.all_to_all(plane, BOTH, 0, 0, tiled=True, axis_index_groups=core_groups)  18.2 us
    all_to_all x1, waiting for transfers between devices, body(): lax.all_to_all(back, BOTH, 0, 0, tiled=True, axis_index_groups=core_groups)  9.07 us
    pallas_call x1, Pallas kernels, body(): pl.pallas_call(functools.partial(forward_kernel, columns, rows_dev), grid...  8.22 us
    pallas_call x1, Pallas kernels, body(): pl.pallas_call(adjoint_kernel, grid=(chunks,), in_specs=[pl.BlockSpec((pa...  6.7 us
    unnamed x18, local copies, waits for them, and re-layouts  5.85 us
    all_to_all x1, starting transfers between devices, body(): lax.all_to_all(back, BOTH, 0, 0, tiled=True, axis_index_groups=core_groups)  3.57 us
    ppermute x1, waiting for transfers between devices, body(): code = jnp.stack([code, lax.ppermute(code, 'tile', mirror)], axis=1)  3.56 us
  transfers between devices with their start and end apart: 4, of which 2 were waited for; matrix products, arithmetic and copies ran while one was open for 1% of the time, Pallas kernels for 4%

profile of v3, /device:TPU:0, one launch (start us, length us, event | category | flops | bytes accessed | tf_op | source)
XLA Modules:
  0.0 86.8 jit_solution(3869110989498957598)
XLA Ops:
  0.6 0.0 copy-start
  0.6 0.0 copy-start.1
  0.7 8.2 %columns.1 = bf16[2,8,4,8,256]{4,3,2,1,0:T(8,128)(2,1)} custom-call(s32[8,1,256]{2,1,0:T(1,128)} %bitcast.19, bf16[2,4,2,256,128]{4,3,2,1,0:T(8,128)(2,1)} %bitcast.25), custom_call_target="tpu_custom_call" | custom-call | flops 4300000256 | bytes 1600000 | tf_op jit(solution)/shard_map/columns/pallas_call | solution.py:364
  8.9 18.2 %all_to_all.15.own_ref = bf16[16,4,8,256]{3,2,1,0:T(8,128)(2,1)S(1)} all-to-all(bf16[16,4,8,256]{3,2,1,0:T(8,128)(2,1)} %bitcast.21), channel_id=1, replica_groups={{0,1,2,3,4,5,6,7,16,17,18,19,20,21,22,23},{8,9,10,11,12,13,14,15,24,25,..., dimensions={0} | all-to-all | bytes 524288 | tf_op jit(solution)/shard_map/all_to_all | solution.py:385
  27.1 0.0 collective-permute-start
  27.1 0.8 dynamic_slice.3
  27.8 0.9 %rows.1.table = bf16[256,1024]{1,0:T(8,128)(2,1)S(1)} custom-call(s32[1,512]{1,0:T(1,128)S(1)} %bitcast.18), custom_call_target="tpu_custom_call" | custom-call | flops 100000000 | bytes 500000 | tf_op jit(solution)/shard_map/rows/pallas_call | solution.py:392
  28.8 0.0 copy-start.8
  28.8 0.0 copy-start.7
  28.8 0.0 collective-permute-done.far_ref
  28.8 0.0 copy-done
  28.8 0.0 copy-done.1
  28.8 2.6 %objective.1 = (f32[2,256,512]{2,1,0:T(8,128)}, bf16[16,4,8,256]{3,2,1,0:T(8,128)(2,1)S(1)}, bf16[16,4,8,256]{3,2,1,0:T(8,128)(2,1)S(1)}) custom-call(bf16[256,1024]{1,0:T(8,128)(2,1)S(1)} %rows.1.table, bf16[16,4,8,256]{3,2,1,0:T(8,128)(2,1)S(1)} %all_to_all.15.own_ref, bf16[16,4,8,256]{3,2,1,0:T(8,128)(2,1)S(1)} %collective-permute-done.far_ref, ...), custom_call_target="tpu_custom_call" | custom-call | flops 1100000000 | bytes 5000000 | tf_op jit(solution)/shard_map/objective/pallas_call | solution.py:407
  31.4 0.0 copy-start.2
  31.4 0.5 collective-permute-start.2
  31.9 0.0 copy-done.8
  31.9 0.0 copy-done.7
  31.9 1.0 %collective-permute-start.1 = (s32[256]{0:T(256)S(1)}, s32[256]{0:T(256)S(1)}, u32[]{:S(2)}, u32[]{:S(2)}) collective-permute-start(s32[256]{0:T(256)S(1)} %add.7), channel_id=1, source_target_pairs={{0,4},{1,5},{2,6},{3,7},{4,0},{5,1},{6,2},{7,3},{8,12},{9,13},{10,... | collective-permute-start | bytes 3080 | tf_op jit(solution)/shard_map/ppermute | solution.py:390
  32.9 3.6 %collective-permute-done.1 = s32[256]{0:T(256)S(1)} collective-permute-done((s32[256]{0:T(256)S(1)}, s32[256]{0:T(256)S(1)}, u32[]{:S(2)}, u32[]{:S(2)}) %collective-permute-start.1) | collective-permute-done | bytes 1056 | tf_op jit(solution)/shard_map/ppermute | solution.py:390
  36.5 0.0 collective-permute-done.2
  36.5 0.9 %fold.1 = bf16[2,2,4,2,4,8,256]{6,5,4,3,2,1,0:T(8,128)(2,1)} custom-call(bf16[2,2,4,4,8,256]{5,4,3,2,1,0:T(8,128)(2,1)S(1)} %bitcast.16, bf16[2,2,4,4,8,256]{5,4,3,2,1,0:T(8,128)(2,1)S(1)} %bitcast.17), custom_call_target="tpu_custom_call" | custom-call | flops 1000000 | bytes 1000000 | tf_op jit(solution)/shard_map/fold/pallas_call | solution.py:424
  37.3 3.6 %all-to-all-start.1 = ((bf16[16,2,4,8,256]{4,3,2,1,0:T(8,128)(2,1)}), bf16[16,2,4,8,256]{4,3,2,1,0:T(8,128)(2,1)S(1)}, u32[]{:S(2)}, u32[]{:S(2)}) async-start(bf16[16,2,4,8,256]{4,3,2,1,0:T(8,128)(2,1)} %bitcast.11), calls=%async_computation.1 | async-start | bytes 1048576 | tf_op jit(solution)/shard_map/all_to_all | solution.py:437
  40.9 0.1 copy.14.code_ref
  41.1 0.0 copy-done.2
  41.1 2.6 %prepare.1 = (bf16[8,512,256]{2,1,0:T(8,128)(2,1)S(1)}, bf16[8,512,256]{2,1,0:T(8,128)(2,1)S(1)}, f32[8,2,128,256]{3,2,1,0:T(8,128)S(1)}, bf16[2,256,256]{2,1,0:T(8,128)(2,1)S(1)}, bf16[16,8,128]{2,1,0:T(8,128)(2,1)S(1)}) custom-call(s32[8,1,256]{2,1,0:T(1,128)S(1)} %bitcast.20, s32[256,2]{1,0:T(8,128)S(1)} %copy.14.code_ref), custom_call_target="tpu_custom_call" | custom-call | flops 4000000000 | bytes 8000000 | tf_op jit(solution)/shard_map/prepare/pallas_call | solution.py:438
  43.7 0.0 copy-start.3
  43.7 1.3 %copy-done.3 = bf16[8,512,256]{2,1,0:T(8,128)(2,1)} copy-done((bf16[8,512,256]{2,1,0:T(8,128)(2,1)}, bf16[8,512,256]{2,1,0:T(8,128)(2,1)S(1)}, u32[]{:S(2)}) %copy-start.3) | copy-done | bytes 2097176
  45.0 0.0 copy-start.5
  45.0 1.3 %copy-done.5 = f32[8,2,128,256]{3,2,1,0:T(8,128)} copy-done((f32[8,2,128,256]{3,2,1,0:T(8,128)}, f32[8,2,128,256]{3,2,1,0:T(8,128)S(1)}, u32[]{:S(2)}) %copy-start.5) | copy-done | bytes 2097176
  46.4 9.1 %all-to-all-done.1 = bf16[16,2,4,8,256]{4,3,2,1,0:T(8,128)(2,1)S(1)} async-done(((bf16[16,2,4,8,256]{4,3,2,1,0:T(8,128)(2,1)}), bf16[16,2,4,8,256]{4,3,2,1,0:T(8,128)(2,1)S(1)}, u32[]{:S(2)}, u32[]{:S(2)}) %all-to-all-start.1) | async-done | bytes 524320 | tf_op jit(solution)/shard_map/all_to_all | solution.py:437
  55.4 0.0 copy-start.4
  55.4 1.6 %copy-done.4 = bf16[8,512,256]{2,1,0:T(8,128)(2,1)S(1)} copy-done((bf16[8,512,256]{2,1,0:T(8,128)(2,1)S(1)}, bf16[8,512,256]{2,1,0:T(8,128)(2,1)}, u32[]{:S(2)}) %copy-start.4) | copy-done | bytes 2097176
  57.0 0.0 copy-start.6
  57.0 1.6 %copy-done.6 = f32[8,2,128,256]{3,2,1,0:T(8,128)S(1)} copy-done((f32[8,2,128,256]{3,2,1,0:T(8,128)S(1)}, f32[8,2,128,256]{3,2,1,0:T(8,128)}, u32[]{:S(2)}) %copy-start.6) | copy-done | bytes 2097176
  58.6 6.7 %adjoint.1 = bf16[16,264,128]{2,1,0:T(8,128)(2,1)S(1)} custom-call(bf16[2,8,2,4,8,256]{5,4,3,2,1,0:T(8,128)(2,1)S(1)} %bitcast.15, bf16[8,512,256]{2,1,0:T(8,128)(2,1)S(1)} %get-tuple-element.27.w_ref, bf16[8,512,256]{2,1,0:T(8,128)(2,1)S(1)} %copy-done.4, f32[8,2,128,256]{3,2,1,0:T(8,128)S(1)} %copy-done.6, ...), custom_call_target="tpu_custom_call" | custom-call | flops 8600000512 | bytes 8000000 | tf_op jit(solution)/shard_map/adjoint/pallas_call | solution.py:465
  65.3 19.2 %all_to_all.16.got_ref = bf16[16,264,128]{2,1,0:T(8,128)(2,1)S(1)} all-to-all(bf16[16,264,128]{2,1,0:T(8,128)(2,1)S(1)} %adjoint.1), channel_id=1, replica_groups={{0,1,2,3,8,9,10,11,16,17,18,19,24,25,26,27},{4,5,6,7,12,13,14,15,20,21,..., dimensions={0} | all-to-all | bytes 2162688 | tf_op jit(solution)/shard_map/all_to_all | solution.py:485
  84.5 2.3 %faces.1 = f32[2,4,2,256,128]{4,3,2,1,0:T(8,128)} custom-call(bf16[16,264,128]{2,1,0:T(8,128)(2,1)S(1)} %all_to_all.16.got_ref), custom_call_target="tpu_custom_call" | custom-call | tf_op jit(solution)/shard_map/faces/pallas_call | solution.py:489
  (3 shorter events, 0.0 us)
Async XLA Ops:
  0.6 28.2 %copy-start = (f32[2,256,512]{2,1,0:T(8,128)S(1)}, f32[2,256,512]{2,1,0:T(8,128)}, u32[]{:S(2)}) copy-start(f32[2,256,512]{2,1,0:T(8,128)} %target_ref.1) | copy-start | bytes 3145732
  0.6 28.2 %copy-start.1 = (f32[2,256,512]{2,1,0:T(8,128)S(1)}, f32[2,256,512]{2,1,0:T(8,128)}, u32[]{:S(2)}) copy-start(f32[2,256,512]{2,1,0:T(8,128)} %weight_ref.1) | copy-start | bytes 3145732
  27.1 1.7 %collective-permute-start = (bf16[16,4,8,256]{3,2,1,0:T(8,128)(2,1)S(1)}, bf16[16,4,8,256]{3,2,1,0:T(8,128)(2,1)S(1)}, u32[]{:S(2)}, u32[]{:S(2)}) collective-permute-start(bf16[16,4,8,256]{3,2,1,0:T(8,128)(2,1)S(1)} %all_to_all.15.own_ref), channel_id=1, source_target_pairs={{0,8},{8,0},{16,24},{24,16},{1,9},{9,1},{17,25},{25,17},{2,10},{10... | collective-permute-start | bytes 786440 | tf_op jit(solution)/shard_map/ppermute | solution.py:402
  28.8 3.1 %copy-start.8 = (s32[256,1]{0,1:T(1,128)S(1)}, s32[256,1]{0,1:T(1,128)}, u32[]{:S(2)}) copy-start(s32[256,1]{0,1:T(1,128)} %param.12) | copy-start | bytes 3076
  28.8 3.1 %copy-start.7 = (s32[256]{0:T(256)S(1)}, s32[256]{0:T(256)}, u32[]{:S(2)}) copy-start(s32[256]{0:T(256)} %param.13) | copy-start | bytes 3076
  31.4 9.7 %copy-start.2 = (s32[2048]{0:T(1024)S(1)}, s32[2048]{0:T(1024)}, u32[]{:S(2)}) copy-start(s32[2048]{0:T(1024)} %param.9) | copy-start | bytes 24580
  31.4 5.1 %collective-permute-start.2 = (bf16[16,4,8,256]{3,2,1,0:T(8,128)(2,1)S(1)}, bf16[16,4,8,256]{3,2,1,0:T(8,128)(2,1)S(1)}, u32[]{:S(2)}, u32[]{:S(2)}) collective-permute-start(bf16[16,4,8,256]{3,2,1,0:T(8,128)(2,1)S(1)} %get-tuple-element.23), channel_id=1, source_target_pairs={{0,8},{8,0},{16,24},{24,16},{1,9},{9,1},{17,25},{25,17},{2,10},{10... | collective-permute-start | bytes 786440 | tf_op jit(solution)/shard_map/ppermute | solution.py:420
  31.9 4.5 %collective-permute-start.1 = (s32[256]{0:T(256)S(1)}, s32[256]{0:T(256)S(1)}, u32[]{:S(2)}, u32[]{:S(2)}) collective-permute-start(s32[256]{0:T(256)S(1)} %add.7), channel_id=1, source_target_pairs={{0,4},{1,5},{2,6},{3,7},{4,0},{5,1},{6,2},{7,3},{8,12},{9,13},{10,... | collective-permute-start | bytes 3080 | tf_op jit(solution)/shard_map/ppermute | solution.py:390
  37.3 18.1 %all-to-all-start.1 = ((bf16[16,2,4,8,256]{4,3,2,1,0:T(8,128)(2,1)}), bf16[16,2,4,8,256]{4,3,2,1,0:T(8,128)(2,1)S(1)}, u32[]{:S(2)}, u32[]{:S(2)}) async-start(bf16[16,2,4,8,256]{4,3,2,1,0:T(8,128)(2,1)} %bitcast.11), calls=%async_computation.1 | async-start | bytes 1048576 | tf_op jit(solution)/shard_map/all_to_all | solution.py:437
  43.7 1.3 %copy-start.3 = (bf16[8,512,256]{2,1,0:T(8,128)(2,1)}, bf16[8,512,256]{2,1,0:T(8,128)(2,1)S(1)}, u32[]{:S(2)}) copy-start(bf16[8,512,256]{2,1,0:T(8,128)(2,1)S(1)} %get-tuple-element.28.v_ref) | copy-start | bytes 6291460
  45.0 1.3 %copy-start.5 = (f32[8,2,128,256]{3,2,1,0:T(8,128)}, f32[8,2,128,256]{3,2,1,0:T(8,128)S(1)}, u32[]{:S(2)}) copy-start(f32[8,2,128,256]{3,2,1,0:T(8,128)S(1)} %get-tuple-element.29.t_ref) | copy-start | bytes 6291460
  55.4 1.6 %copy-start.4 = (bf16[8,512,256]{2,1,0:T(8,128)(2,1)S(1)}, bf16[8,512,256]{2,1,0:T(8,128)(2,1)}, u32[]{:S(2)}) copy-start(bf16[8,512,256]{2,1,0:T(8,128)(2,1)} %copy-done.3) | copy-start | bytes 6291460
  57.0 1.6 %copy-start.6 = (f32[8,2,128,256]{3,2,1,0:T(8,128)S(1)}, f32[8,2,128,256]{3,2,1,0:T(8,128)}, u32[]{:S(2)}) copy-start(f32[8,2,128,256]{3,2,1,0:T(8,128)} %copy-done.5) | copy-start | bytes 6291460

commit v4 on v3

--- a/solution.py
+++ b/solution.py
@@ -108,42 +108,38 @@
                     lhs[(2 * f + 1) * points:(2 * f + 2) * points, spot:spot + SEG] = (j[1] - j[2]).astype(BF)
 
     low = iota((8, width), 0) < 4
-    for fp in range(4):
-        grid_sum = jnp.dot(
-            lhs[pl.ds(fp * points, points), :], table, preferred_element_type=F32
-        )
-        real, imag = grid_sum[:, :width], grid_sum[:, width:]
+    grid_sum = jnp.dot(lhs[...], table, preferred_element_type=F32)
+    for f, p in [(i, j) for i in range(2) for j in range(2)]:
+        start = (2 * f + p) * points
+        real = grid_sum[start:start + points, :width]
+        imag = grid_sum[start:start + points, width:]
         out_re = jnp.sum((real * cos_a + imag * sin_a).reshape(points // 8, 8, width), axis=0)
         out_im = jnp.sum((imag * cos_a - real * sin_a).reshape(points // 8, 8, width), axis=0)
         out_re = out_re + pltpu.roll(out_re, 4, 0)
         out_im = out_im + pltpu.roll(out_im, 4, 0)
         out = jnp.where(low, out_re, out_im).astype(BF)
         for copy in range(f_ref.shape[0]):
-            f_ref[copy, 0, fp] = out
-
-
-def row_kernel(quarter, rows_dev, row_count, tile_count, row_ref, r_ref):
-    depth, share_u = r_ref.shape[0], row_ref.shape[1]
-    core = lax.axis_index("row") & 1
+            f_ref[copy, f, 0, p] = out
+
+
+def row_kernel(quarter, rows_dev, row_ref, r_ref):
+    sides, depth = r_ref.shape[:2]
+    share_u = row_ref.shape[-1]
     row = iota((depth, share_u), 0)
-    unit = row // (2 * rows_dev)
-    far = unit // (depth // (4 * rows_dev))
-    unit = unit - far * (depth // (4 * rows_dev))
-    group = (unit // tile_count) * 2 + jnp.where(far == 1, 1 - core, core)
-    x = (group * tile_count + unit % tile_count) * rows_dev + row % rows_dev
+    x = (row // (2 * rows_dev)) * rows_dev + row % rows_dev
     is_imag = row % (2 * rows_dev) >= rows_dev
-    scale = 1.0 / math.sqrt(rows_dev * row_count * tile_count)
-    cos_x, sin_x = cos_sin(x * row_ref[...], quarter, scale)
-    r_ref[:, :share_u] = jnp.where(is_imag, sin_x, cos_x).astype(BF)
-    r_ref[:, share_u:] = jnp.where(is_imag, cos_x, -sin_x).astype(BF)
-
-
-def prepare_kernel(quarter, rows_dev, tile_count, cap, angle_ref, code_ref, w_ref, v_ref, t_ref, choose_ref, mark_ref):
+    scale = 1.0 / math.sqrt(depth // 2)
+    for side in range(sides):
+        cos_x, sin_x = cos_sin(x * row_ref[side:side + 1], quarter, scale)
+        r_ref[side, :, :share_u] = jnp.where(is_imag, sin_x, cos_x).astype(BF)
+        r_ref[side, :, share_u:] = jnp.where(is_imag, cos_x, -sin_x).astype(BF)
+
+
+def prepare_kernel(quarter, rows_dev, tile_count, cap, angle_ref, code_ref, w_ref, t_ref, choose_ref, mark_ref):
     points = code_ref.shape[0]
     slots, units = choose_ref.shape[1], mark_ref.shape[0]
     angles = angle_ref[0]
-    table = rotation(*fine_table(quarter, angles))
-    w_ref[0], v_ref[0] = table[:, :CHUNK], table[:, CHUNK:]
+    w_ref[0] = rotation(*fine_table(quarter, angles))
     t_ref[0, 0], t_ref[0, 1] = coarse_table(quarter, rows_dev, angles)
 
     @pl.when(pl.program_id(0) == 0)
@@ -174,42 +170,46 @@
         mark_ref[...] = marked.astype(F32).astype(BF)
 
 
-def middle_kernel(table, own_ref, far_ref, target_ref, weight_ref, int_ref, back_ref, over_ref):
-    count, pairs, rows, share_v = own_ref.shape
-    depth = 2 * count * rows
-    share_u = table.shape[1] // 2
-
-    mixed = []
-    for p in range(2):
-        plane = jnp.concatenate([own_ref[:, p], far_ref[:, p]], axis=0)
-        plane = plane.astype(F32).reshape(depth, share_v).astype(BF)
-        mixed.append(
-            lax.dot_general(plane, table[...], (((0,), (0,)), ((), ())), preferred_element_type=F32)
-        )
-    power = mixed[0] * mixed[0] + mixed[1] * mixed[1]
-    intensity = power[:, :share_u] + power[:, share_u:]
-    int_ref[0] = intensity
-    factor = 4.0 * weight_ref[0] * (intensity - target_ref[0])
-    factor = jnp.concatenate([factor, factor], axis=1)
-    for p in range(2):
-        far_grad = (factor * mixed[p]).astype(BF)
-        back = lax.dot_general(
-            table[...], far_grad, (((1,), (1,)), ((), ())), preferred_element_type=F32
-        )
-        back = back.reshape(2 * count, rows, share_v).astype(BF)
-        back_ref[:, p] = back[:count]
-        over_ref[:, p] = back[count:]
-
-
-def fold_kernel(own_ref, got_ref, out_ref):
-    for side in range(2):
-        total = own_ref[:, side].astype(F32) + got_ref[:, side].astype(F32)
-        total = total.astype(BF)
-        out_ref[:, side, :, 0] = total
-        out_ref[:, 1 - side, :, 1] = total
-
-
-def adjoint_kernel(got_ref, w_ref, v_ref, t_ref, choose_ref, mark_ref, out_ref, total):
+def middle_kernel(
+    table, got_ref, target_ref, far_target_ref, weight_ref, far_weight_ref, int_ref, far_int_ref, back_ref
+):
+    devices, pols, rows, share_v = got_ref.shape
+    depth = devices * rows
+    share_u = table.shape[2] // 2
+    planes = [
+        got_ref[:, p].astype(F32).reshape(depth, share_v).astype(BF) for p in range(pols)
+    ]
+    sums = [None, None]
+    sides = [
+        (target_ref, weight_ref, int_ref), (far_target_ref, far_weight_ref, far_int_ref)
+    ]
+    for side, (goal_ref, gain_ref, power_ref) in enumerate(sides):
+        mixed = [
+            lax.dot_general(
+                plane, table[side], (((0,), (0,)), ((), ())), preferred_element_type=F32
+            )
+            for plane in planes
+        ]
+        power = mixed[0] * mixed[0] + mixed[1] * mixed[1]
+        intensity = power[:, :share_u] + power[:, share_u:]
+        power_ref[...] = intensity
+        factor = 4.0 * gain_ref[...] * (intensity - goal_ref[...])
+        factor = jnp.concatenate([factor, factor], axis=1)
+        for p in range(pols):
+            far_grad = (factor * mixed[p]).astype(BF)
+            back = lax.dot_general(
+                table[side], far_grad, (((1,), (1,)), ((), ())), preferred_element_type=F32
+            )
+            sums[p] = back if side == 0 else sums[p] + back
+    groups, halves, count = back_ref.shape[:3]
+    for p in range(pols):
+        total = sums[p].reshape(groups, halves, count, rows, share_v).astype(BF)
+        for half in range(halves):
+            back_ref[:, half, :, 0, p] = total[:, half]
+            back_ref[:, 1 - half, :, 1, p] = total[:, half]
+
+
+def adjoint_kernel(got_ref, w_ref, t_ref, choose_ref, mark_ref, out_ref, total):
     points, width = t_ref.shape[2], t_ref.shape[3]
     units = out_ref.shape[0]
     step = pl.program_id(0)
@@ -222,7 +222,7 @@
     low = iota((8, width), 0) < 4
     parts = []
     for side, fp in [(i, j) for i in range(2) for j in range(4)]:
-        plane = jnp.sum(got_ref[:, 0, side, fp].astype(F32), axis=0)
+        plane = jnp.sum(got_ref[:, fp // 2, 0, side, fp % 2].astype(F32), axis=0)
         other = pltpu.roll(plane, 4, 0)
         real = jnp.where(low, plane, other)
         imag = jnp.where(low, other, plane)
@@ -239,8 +239,7 @@
         )
     lhs = jnp.concatenate(parts, axis=0)
     total[...] += lax.dot_general(
-        lhs, jnp.concatenate([w_ref[0], v_ref[0]], axis=1), (((1,), (1,)), ((), ())),
-        preferred_element_type=F32,
+        lhs, w_ref[0], (((1,), (1,)), ((), ())), preferred_element_type=F32
     )
 
     @pl.when(step == pl.num_programs(0) - 1)
@@ -339,23 +338,17 @@
     units = slots // PACK
     held = 16 * PACK + PACK // 2
     pairs = row_count // 2
-    peers = pairs * tile_count
     wide = 2 * rows_dev
     depth = devices * wide
     tile_half = tile_count // 2
-    core_groups = [
-        [(2 * x + core) * tile_count + t for x in range(pairs) for t in range(tile_count)]
-        for core in range(2)
-    ]
     half_groups = [
         [r * tile_count + side * tile_half + t for r in range(row_count) for t in range(tile_half)]
         for side in range(2)
     ]
-    core_swap = [(i, i ^ 1) for i in range(row_count)]
     mirror = [(i, (i + tile_half) % tile_count) for i in range(tile_count)]
     angles = column_angles.reshape(chunks, 1, CHUNK)
     angle_spec = pl.BlockSpec((1, 1, CHUNK), lambda i: (i, 0, 0))
-    table_spec = pl.BlockSpec((1, 4 * SEG, CHUNK), lambda i: (i, 0, 0))
+    table_spec = pl.BlockSpec((1, 4 * SEG, 2 * CHUNK), lambda i: (i, 0, 0))
     turn_spec = pl.BlockSpec((1, 2, half, CHUNK), lambda i: (i, 0, 0, 0))
 
     cur = currents.reshape(freq_count, comp_count, part_count, rows_dev, tiles, SEG)
@@ -365,8 +358,8 @@
         functools.partial(forward_kernel, columns, rows_dev),
         grid=(chunks,),
         in_specs=[angle_spec, pl.BlockSpec(memory_space=pltpu.HBM)],
-        out_specs=pl.BlockSpec((copies, 1, 4, wide, CHUNK), lambda i: (0, i, 0, 0, 0)),
-        out_shape=jax.ShapeDtypeStruct((copies, chunks, 4, wide, CHUNK), BF),
+        out_specs=pl.BlockSpec((copies, 2, 1, 2, wide, CHUNK), lambda i: (0, 0, i, 0, 0, 0)),
+        out_shape=jax.ShapeDtypeStruct((copies, 2, chunks, 2, wide, CHUNK), BF),
         scratch_shapes=[
             pltpu.VMEM(cur.shape, BF),
             pltpu.VMEM((4 * half, 4 * SEG), BF),
@@ -377,97 +370,95 @@
         name="columns",
     )(angles, cur)
     if share_v != CHUNK:
-        plane = plane.reshape(chunks, 4, wide, CHUNK // share_v, share_v)
-        plane = plane.transpose(0, 3, 1, 2, 4).reshape(1, tile_count, 4, wide, share_v)
+        plane = plane.reshape(2, chunks, 2, wide, CHUNK // share_v, share_v)
+        plane = plane.transpose(0, 1, 4, 2, 3, 5).reshape(1, 2, tile_count, 2, wide, share_v)
         plane = jnp.broadcast_to(plane, (pairs,) + plane.shape[1:])
-    plane = plane.reshape(peers, 4, wide, share_v)
-
-    own = lax.all_to_all(plane, BOTH, 0, 0, tiled=True, axis_index_groups=core_groups)
-    row_angles, owner, slot, own = lax.optimization_barrier(
-        (row_angles, tile_owner, face_slot, own)
-    )
+    plane = plane.reshape(devices, 2, wide, share_v)
+
+    row_angles, owner, slot, target, weight, plane = lax.optimization_barrier(
+        (row_angles, tile_owner, face_slot, target, weight, plane)
+    )
+    got = lax.all_to_all(plane, BOTH, 0, 0, tiled=True)
+    here = lax.axis_index("row")
+    core = here % 2
+    swap = [(i, i ^ 1) for i in range(row_count)]
     code = owner[:, 0] * points + slot
     code = jnp.stack([code, lax.ppermute(code, "tile", mirror)], axis=1)
-    own_angles = lax.dynamic_slice_in_dim(row_angles, lax.axis_index("row") * share_u, share_u)
+    own_angles = jnp.stack(
+        [lax.dynamic_slice_in_dim(row_angles, i * share_u, share_u) for i in (here, here ^ 1)]
+    )
+    own, far = [], []
+    for array in (target, weight):
+        own.append(lax.dynamic_index_in_dim(array, core, 0, keepdims=False))
+        other = lax.dynamic_index_in_dim(array, 1 - core, 0, keepdims=False)
+        far.append(lax.ppermute(other, "row", swap))
     row_table = pl.pallas_call(
-        functools.partial(row_kernel, columns, rows_dev, row_count, tile_count),
+        functools.partial(row_kernel, columns, rows_dev),
         grid=(1,),
-        in_specs=[whole((1, share_u))],
-        out_specs=whole((depth, 2 * share_u)),
-        out_shape=jax.ShapeDtypeStruct((depth, 2 * share_u), BF),
+        in_specs=[whole((2, share_u))],
+        out_specs=whole((2, depth, 2 * share_u)),
+        out_shape=jax.ShapeDtypeStruct((2, depth, 2 * share_u), BF),
         compiler_params=params(),
         cost_estimate=cost(1e8, 5e5),
         name="rows",
-    )(own_angles.reshape(1, share_u))
-    other = lax.ppermute(own, "row", core_swap)
-
-    pair = pl.BlockSpec((peers, 2, wide, share_v), lambda i: (0, i, 0, 0))
-    far = pl.BlockSpec((1, share_v, share_u), lambda i: (i, 0, 0))
-    back_shape = jax.ShapeDtypeStruct((peers, 4, wide, share_v), BF)
-    intensity, back, over = pl.pallas_call(
+    )(own_angles)
+
+    far_shape = (share_v, share_u)
+    back_shape = (row_count, 2, tile_half, 2, 2, wide, share_v)
+    power, far_power, back = pl.pallas_call(
         middle_kernel,
-        grid=(freq_count,),
-        in_specs=[whole((depth, 2 * share_u)), pair, pair, far, far],
-        out_specs=[far, pair, pair],
+        grid=(1,),
+        in_specs=[whole((2, depth, 2 * share_u)), whole((devices, 2, wide, share_v))]
+        + [whole(far_shape)] * 4,
+        out_specs=[whole(far_shape), whole(far_shape), whole(back_shape)],
         out_shape=[
-            jax.ShapeDtypeStruct((freq_count, share_v, share_u), F32), back_shape, back_shape
+            jax.ShapeDtypeStruct(far_shape, F32),
+            jax.ShapeDtypeStruct(far_shape, F32),
+            jax.ShapeDtypeStruct(back_shape, BF),
         ],
         compiler_params=params(),
         cost_estimate=cost(1.1e9, 5e6),
         name="objective",
-    )(row_table, own, other, target, weight)
-
-    over = lax.ppermute(over, "row", core_swap)
-    split = (pairs * 2, tile_half, 4, wide, share_v)
-    part = pl.BlockSpec((1, 2, tile_half, 4, wide, share_v), lambda i: (i, 0, 0, 0, 0, 0))
-    fold_out = (pairs, 2, tile_half, 2, 4, wide, share_v)
-    back = pl.pallas_call(
-        fold_kernel,
-        grid=(pairs,),
-        in_specs=[part, part],
-        out_specs=pl.BlockSpec((1,) + fold_out[1:], lambda i: (i, 0, 0, 0, 0, 0, 0)),
-        out_shape=jax.ShapeDtypeStruct(fold_out, BF),
-        compiler_params=params(),
-        cost_estimate=cost(1e6, 1e6),
-        name="fold",
-    )(back.reshape((pairs, 2) + split[1:]), over.reshape((pairs, 2) + split[1:]))
+    )(row_table, got, own[0], far[0], own[1], far[1])
 
     angles, code, back = lax.optimization_barrier((angles, code, back))
-    back = back.reshape(peers, 2, 4, wide, share_v)
-    back = lax.all_to_all(back, BOTH, 0, 0, tiled=True, axis_index_groups=core_groups)
-    table, table_im, turn, choose, mark = pl.pallas_call(
+    back = back.reshape(devices, 2, 2, wide, share_v)
+    back = lax.all_to_all(back, BOTH, 0, 0, tiled=True)
+    far_power = lax.ppermute(far_power, "row", swap)
+    intensity = jnp.where(
+        core == 0, jnp.stack([power, far_power]), jnp.stack([far_power, power])
+    )
+    table, turn, choose, mark = pl.pallas_call(
         functools.partial(prepare_kernel, columns, rows_dev, tile_count, cap),
         grid=(chunks,),
         in_specs=[angle_spec, whole((points, 2))],
         out_specs=[
-            table_spec,
             table_spec,
             turn_spec,
             whole((2, slots, points)),
             whole((units, PACK // 2, SEG)),
         ],
         out_shape=[
-            jax.ShapeDtypeStruct((chunks, 4 * SEG, CHUNK), BF),
-            jax.ShapeDtypeStruct((chunks, 4 * SEG, CHUNK), BF),
-            jax.ShapeDtypeStruct((chunks, 2, half, CHUNK), F32),
+            jax.ShapeDtypeStruct((8 * chunks, 4 * SEG, 2 * CHUNK), BF),
+            jax.ShapeDtypeStruct((16 * chunks, 2, half, CHUNK), F32),
             jax.ShapeDtypeStruct((2, slots, points), BF),
             jax.ShapeDtypeStruct((units, PACK // 2, SEG), BF),
         ],
-        compiler_params=params(),
+        compiler_params=params(40),
         cost_estimate=cost(4e9, 8e6),
         name="prepare",
     )(angles, code)
-
-    back = back.reshape(pairs, tile_count, 2, 4, wide, share_v)
+    intensity, mark = lax.optimization_barrier((intensity, mark))
+
+    back = back.reshape(pairs, 2, tile_count, 2, 2, wide, share_v)
     if share_v != CHUNK:
-        back = back.reshape(pairs, chunks, CHUNK // share_v, 2, 4, wide, share_v)
-        back = back.transpose(0, 1, 3, 4, 5, 2, 6).reshape(pairs, chunks, 2, 4, wide, CHUNK)
+        back = back.reshape(pairs, 2, chunks, CHUNK // share_v, 2, 2, wide, share_v)
+        back = back.transpose(0, 1, 2, 4, 5, 6, 3, 7).reshape(pairs, 2, chunks, 2, 2, wide, CHUNK)
     outgoing = pl.pallas_call(
         adjoint_kernel,
         grid=(chunks,),
         in_specs=[
-            pl.BlockSpec((pairs, 1, 2, 4, wide, CHUNK), lambda i: (0, i, 0, 0, 0, 0)),
-            table_spec,
+            pl.BlockSpec((pairs, 2, 1, 2, 2, wide, CHUNK), lambda i: (0, 0, i, 0, 0, 0, 0)),
             table_spec,
             turn_spec,
             whole((2, slots, points)),
@@ -476,10 +467,10 @@
         out_specs=whole((units, held, SEG)),
         out_shape=jax.ShapeDtypeStruct((units, held, SEG), BF),
         scratch_shapes=[pltpu.VMEM((8 * half, 4 * SEG), F32)],
-        compiler_params=params(),
+        compiler_params=params(40),
         cost_estimate=cost(8.6e9, 8e6),
         name="adjoint",
-    )(back, table, table_im, turn, choose, mark)
+    )(back, table, turn, choose, mark)
 
     if cap == PACK:
         arrived = lax.all_to_all(outgoing, BOTH, 0, 0, tiled=True, axis_index_groups=half_groups)

time: 87.3 us -> 81.1 us (0.929)
  blocking collectives: 37.4 us -> 19.1 us
  starting transfers between devices: 5.05 us -> 13.3 us
  Pallas kernels: 24.2 us -> 30.1 us
  local copies, waits for them, and re-layouts: 6.75 us -> 2.79 us
  other arithmetic: 0.01 us -> 1.11 us
    all_to_all x1 -> x0, blocking collectives: 18.2 us -> none  [body(): lax.all_to_all(plane, BOTH, 0, 0, tiled=True, axis_index_groups=core_groups)]
    all_to_all x1 -> x2, starting transfers between devices: 3.57 us -> 9.91 us  [the longest x1 7.3 us: body(): got = lax.all_to_all(plane, BOTH, 0, 0, tiled=True)]
    unnamed x18 -> x14, local copies, waits for them, and re-layouts: 5.85 us -> 0.83 us
    pallas_call x1, Pallas kernels: 2.62 us -> 5.46 us  [body(): pl.pallas_call(functools.partial(prepare_kernel, columns, rows_dev, tile_...]
    pallas_call x1, Pallas kernels: 6.7 us -> 9.01 us  [body(): pl.pallas_call(adjoint_kernel, grid=(chunks,), in_specs=[pl.BlockSpec((pa...]
    ppermute x1, starting transfers between devices: 0.98 us -> 2.74 us  [body(): code = jnp.stack([code, lax.ppermute(code, 'tile', mirror)], axis=1)]
    squeeze x0 -> x2, local copies, waits for them, and re-layouts: none -> 1.76 us  [body(): other = lax.dynamic_index_in_dim(array, 1 - core, 0, keepdims=False)]
    all_to_all x1 -> x2, waiting for transfers between devices: 9.07 us -> 10.7 us  [the longest x1 9.48 us: body(): back = lax.all_to_all(back, BOTH, 0, 0, tiled=True)]
  transfers between devices with their start and end apart: 4 -> 6, of which waited for: 2 -> 3; matrix products, arithmetic and copies ran while one was open for 1% -> 4% of each run, Pallas kernels for 4% -> 9%
where the time goes in v4:
time: 81.1 us; the launch traced here: 80.5 us
  Pallas kernels  30.1 us (37%)
  blocking collectives  19.1 us (24%)
  waiting for transfers between devices  13.4 us (17%)
  starting transfers between devices  13.3 us (16%)
  local copies, waits for them, and re-layouts  2.79 us (3%)
  other arithmetic  1.11 us (1%)
    all_to_all x1, blocking collectives, body(): lax.all_to_all(outgoing, BOTH, 0, 0, tiled=True, axis_index_groups=half_g...  19.1 us
    all_to_all x1, waiting for transfers between devices, body(): back = lax.all_to_all(back, BOTH, 0, 0, tiled=True)  9.48 us
    pallas_call x1, Pallas kernels, body(): pl.pallas_call(adjoint_kernel, grid=(chunks,), in_specs=[pl.BlockSpec((pa...  9.01 us
    pallas_call x1, Pallas kernels, body(): pl.pallas_call(functools.partial(forward_kernel, columns, rows_dev), grid...  8.05 us
    all_to_all x1, starting transfers between devices, body(): got = lax.all_to_all(plane, BOTH, 0, 0, tiled=True)  7.3 us
    pallas_call x1, Pallas kernels, body(): pl.pallas_call(functools.partial(prepare_kernel, columns, rows_dev, tile_...  5.46 us
    pallas_call x1, Pallas kernels, body(): pl.pallas_call(middle_kernel, grid=(1,), in_specs=[whole((2, depth, 2 * s...  3.72 us
    ppermute x1, starting transfers between devices, body(): code = jnp.stack([code, lax.ppermute(code, 'tile', mirror)], axis=1)  2.74 us
  transfers between devices with their start and end apart: 6, of which 3 were waited for; matrix products, arithmetic and copies ran while one was open for 4% of the time, Pallas kernels for 9%

profile of v4, /device:TPU:0, one launch (start us, length us, event | category | flops | bytes accessed | tf_op | source)
XLA Modules:
  0.0 80.5 jit_solution(5519148430971054548)
XLA Ops:
  0.6 0.0 copy-start.2
  0.6 8.0 %columns.1 = bf16[2,2,8,2,8,256]{5,4,3,2,1,0:T(8,128)(2,1)} custom-call(s32[8,1,256]{2,1,0:T(1,128)} %bitcast.26, bf16[2,4,2,256,128]{4,3,2,1,0:T(8,128)(2,1)} %bitcast.35), custom_call_target="tpu_custom_call" | custom-call | flops 4300000256 | bytes 1600000 | tf_op jit(solution)/shard_map/columns/pallas_call | solution.py:357
  8.7 0.0 copy-start.3
  8.7 7.3 %all-to-all-start = ((bf16[32,2,8,256]{3,2,1,0:T(8,128)(2,1)}), bf16[32,2,8,256]{3,2,1,0:T(8,128)(2,1)S(1)}, u32[]{:S(2)}, u32[]{:S(2)}) async-start(bf16[32,2,8,256]{3,2,1,0:T(8,128)(2,1)} %bitcast.29), calls=%async_computation | async-start | bytes 524288 | tf_op jit(solution)/shard_map/all_to_all | solution.py:381
  16.0 0.0 copy-done.2
  16.0 0.0 copy-start.6
  16.1 0.0 copy-start.5
  16.1 0.0 copy-start.4
  16.1 0.9 %dynamic-slice_bitcast_fusion.2 = (f32[256,512]{1,0:T(8,128)}, f32[256,512]{1,0:T(8,128)S(1)}) fusion(f32[2,256,512]{2,1,0:T(8,128)S(1)} %copy-done.2, s32[]{:T(128)S(6)} %select_n.35, s32[]{:T(128)S(6)} %select_n.34), kind=kLoop, calls=%fused_computation.3 | loop fusion | bytes 2097160 | tf_op jit(solution)/shard_map/jit(dynamic_index_in_dim)/squeeze | solution.py:393
  17.0 0.3 collective-permute-start
  17.2 0.0 copy-done.3
  17.2 0.9 %dynamic-slice_bitcast_fusion = (f32[256,512]{1,0:T(8,128)}, f32[256,512]{1,0:T(8,128)S(1)}) fusion(f32[2,256,512]{2,1,0:T(8,128)S(1)} %copy-done.3, s32[]{:T(128)S(6)} %select_n.35, s32[]{:T(128)S(6)} %select_n.34), kind=kLoop, calls=%fused_computation.1 | loop fusion | bytes 2097160 | tf_op jit(solution)/shard_map/jit(dynamic_index_in_dim)/squeeze | solution.py:393
  18.1 0.3 collective-permute-start.1
  18.4 0.0 copy-done.6
  18.4 0.0 copy-done.5
  18.4 2.7 %collective-permute-start.3 = (s32[256]{0:T(256)S(1)}, s32[256]{0:T(256)S(1)}, u32[]{:S(2)}, u32[]{:S(2)}) collective-permute-start(s32[256]{0:T(256)S(1)} %add.28), channel_id=1, source_target_pairs={{0,4},{1,5},{2,6},{3,7},{4,0},{5,1},{6,2},{7,3},{8,12},{9,13},{10,... | collective-permute-start | bytes 3080 | tf_op jit(solution)/shard_map/ppermute | solution.py:386
  21.1 0.0 copy-done.4
  21.1 0.1 fusion
  21.2 1.6 %rows.1.table = bf16[2,256,1024]{2,1,0:T(8,128)(2,1)S(1)} custom-call(s32[2,512]{1,0:T(2,128)S(1)} %pad_add_fusion.row_ref), custom_call_target="tpu_custom_call" | custom-call | flops 100000000 | bytes 500000 | tf_op jit(solution)/shard_map/rows/pallas_call | solution.py:395
  22.8 2.6 %collective-permute-done.3 = s32[256]{0:T(256)S(1)} collective-permute-done((s32[256]{0:T(256)S(1)}, s32[256]{0:T(256)S(1)}, u32[]{:S(2)}, u32[]{:S(2)}) %collective-permute-start.3) | collective-permute-done | bytes 1056 | tf_op jit(solution)/shard_map/ppermute | solution.py:386
  25.4 1.2 %all-to-all-done.got_ref = bf16[32,2,8,256]{3,2,1,0:T(8,128)(2,1)S(1)} async-done(((bf16[32,2,8,256]{3,2,1,0:T(8,128)(2,1)}), bf16[32,2,8,256]{3,2,1,0:T(8,128)(2,1)S(1)}, u32[]{:S(2)}, u32[]{:S(2)}) %all-to-all-start) | async-done | bytes 262176 | tf_op jit(solution)/shard_map/all_to_all | solution.py:381
  26.7 0.0 collective-permute-done.far_target_ref
  26.7 0.0 collective-permute-done.1.far_weight_ref
  26.7 0.0 copy-start.1
  26.7 3.7 %objective.1 = (f32[256,512]{1,0:T(8,128)S(1)}, f32[256,512]{1,0:T(8,128)S(1)}, bf16[4,2,4,2,2,8,256]{6,5,4,3,2,1,0:T(8,128)(2,1)}) custom-call(bf16[2,256,1024]{2,1,0:T(8,128)(2,1)S(1)} %rows.1.table, bf16[32,2,8,256]{3,2,1,0:T(8,128)(2,1)S(1)} %all-to-all-done.got_ref, f32[256,512]{1,0:T(8,128)S(1)} %get-tuple-element.41.target_ref, ...), custom_call_target="tpu_custom_call" | custom-call | flops 1100000000 | bytes 5000000 | tf_op jit(solution)/shard_map/objective/pallas_call | solution.py:408
  30.4 0.0 copy-start
  30.4 0.8 copy-done
  31.2 2.6 %all-to-all-start.1 = ((bf16[32,2,2,8,256]{4,3,2,1,0:T(8,128)(2,1)}), bf16[32,2,2,8,256]{4,3,2,1,0:T(8,128)(2,1)S(1)}, u32[]{:S(2)}, u32[]{:S(2)}) async-start(bf16[32,2,2,8,256]{4,3,2,1,0:T(8,128)(2,1)} %bitcast.16), calls=%async_computation.1 | async-start | bytes 1048576 | tf_op jit(solution)/shard_map/all_to_all | solution.py:426
  33.8 0.2 collective-permute-start.2
  34.0 0.1 copy.14.code_ref
  34.1 0.0 copy-done.1
  34.1 5.5 %prepare.1 = (bf16[64,512,512]{2,1,0:T(8,128)(2,1)}, f32[128,2,128,256]{3,2,1,0:T(8,128)}, bf16[2,256,256]{2,1,0:T(8,128)(2,1)S(1)}, bf16[16,8,128]{2,1,0:T(8,128)(2,1)S(1)}) custom-call(s32[8,1,256]{2,1,0:T(1,128)S(1)} %bitcast.27, s32[256,2]{1,0:T(8,128)S(1)} %copy.14.code_ref), custom_call_target="tpu_custom_call" | custom-call | flops 4000000000 | bytes 8000000 | tf_op jit(solution)/shard_map/prepare/pallas_call | solution.py:431
  39.6 0.0 collective-permute-done.2
  39.6 1.1 %maximum_select_fusion = f32[2,256,512]{2,1,0:T(8,128)} fusion(f32[1,256,512]{2,1,0:T(8,128)S(1)} %bitcast.28, f32[1,256,512]{2,1,0:T(8,128)S(1)} %bitcast.25, pred[]{:T(512)S(6)} %eq.5), kind=kLoop, calls=%fused_computation | loop fusion | flops 786432 | bytes 2097153 | tf_op jit(solution)/shard_map/jit(_where)/select_n | solution.py:428
  40.7 9.5 %all-to-all-done.1 = bf16[32,2,2,8,256]{4,3,2,1,0:T(8,128)(2,1)S(1)} async-done(((bf16[32,2,2,8,256]{4,3,2,1,0:T(8,128)(2,1)}), bf16[32,2,2,8,256]{4,3,2,1,0:T(8,128)(2,1)S(1)}, u32[]{:S(2)}, u32[]{:S(2)}) %all-to-all-start.1) | async-done | bytes 524320 | tf_op jit(solution)/shard_map/all_to_all | solution.py:426
  50.2 9.0 %adjoint.1 = bf16[16,264,128]{2,1,0:T(8,128)(2,1)S(1)} custom-call(bf16[2,2,8,2,2,8,256]{6,5,4,3,2,1,0:T(8,128)(2,1)S(1)} %bitcast.24, bf16[64,512,512]{2,1,0:T(8,128)(2,1)} %get-tuple-element.34.w_ref, f32[128,2,128,256]{3,2,1,0:T(8,128)} %get-tuple-element.35.t_ref, bf16[2,256,256]{2,1,0:T(8,128)(2,1)S(1)} %get-tuple-element.36.choose_ref, ...), custom_call_target="tpu_custom_call" | custom-call | flops 8600000512 | bytes 8000000 | tf_op jit(solution)/shard_map/adjoint/pallas_call | solution.py:457
  59.2 19.1 %all_to_all.15.got_ref = bf16[16,264,128]{2,1,0:T(8,128)(2,1)S(1)} all-to-all(bf16[16,264,128]{2,1,0:T(8,128)(2,1)S(1)} %adjoint.1), channel_id=1, replica_groups={{0,1,2,3,8,9,10,11,16,17,18,19,24,25,26,27},{4,5,6,7,12,13,14,15,20,21,..., dimensions={0} | all-to-all | bytes 2162688 | tf_op jit(solution)/shard_map/all_to_all | solution.py:476
  78.2 2.3 %faces.1 = f32[2,4,2,256,128]{4,3,2,1,0:T(8,128)} custom-call(bf16[16,264,128]{2,1,0:T(8,128)(2,1)S(1)} %all_to_all.15.got_ref), custom_call_target="tpu_custom_call" | custom-call | tf_op jit(solution)/shard_map/faces/pallas_call | solution.py:480
  (4 shorter events, 0.0 us)
Async XLA Ops:
  0.6 15.4 %copy-start.2 = (f32[2,256,512]{2,1,0:T(8,128)S(1)}, f32[2,256,512]{2,1,0:T(8,128)}, u32[]{:S(2)}) copy-start(f32[2,256,512]{2,1,0:T(8,128)} %param.10) | copy-start | bytes 3145732
  8.7 8.5 %copy-start.3 = (f32[2,256,512]{2,1,0:T(8,128)S(1)}, f32[2,256,512]{2,1,0:T(8,128)}, u32[]{:S(2)}) copy-start(f32[2,256,512]{2,1,0:T(8,128)} %param.11) | copy-start | bytes 3145732
  8.7 18.0 %all-to-all-start = ((bf16[32,2,8,256]{3,2,1,0:T(8,128)(2,1)}), bf16[32,2,8,256]{3,2,1,0:T(8,128)(2,1)S(1)}, u32[]{:S(2)}, u32[]{:S(2)}) async-start(bf16[32,2,8,256]{3,2,1,0:T(8,128)(2,1)} %bitcast.29), calls=%async_computation | async-start | bytes 524288 | tf_op jit(solution)/shard_map/all_to_all | solution.py:381
  16.0 2.3 %copy-start.6 = (s32[256,1]{0,1:T(1,128)S(1)}, s32[256,1]{0,1:T(1,128)}, u32[]{:S(2)}) copy-start(s32[256,1]{0,1:T(1,128)} %param.12) | copy-start | bytes 3076
  16.1 2.3 %copy-start.5 = (s32[256]{0:T(256)S(1)}, s32[256]{0:T(256)}, u32[]{:S(2)}) copy-start(s32[256]{0:T(256)} %param.13) | copy-start | bytes 3076
  16.1 5.0 %copy-start.4 = (s32[2048]{0:T(1024)S(1)}, s32[2048]{0:T(1024)}, u32[]{:S(2)}) copy-start(s32[2048]{0:T(1024)} %param.8) | copy-start | bytes 24580
  17.0 9.7 %collective-permute-start = (f32[256,512]{1,0:T(8,128)}, f32[256,512]{1,0:T(8,128)S(1)}, u32[]{:S(2)}, u32[]{:S(2)}) collective-permute-start(f32[256,512]{1,0:T(8,128)} %get-tuple-element.40), channel_id=1, source_target_pairs={{0,8},{8,0},{16,24},{24,16},{1,9},{9,1},{17,25},{25,17},{2,10},{10... | collective-permute-start | bytes 1572872 | tf_op jit(solution)/shard_map/ppermute | solution.py:394
  18.1 8.6 %collective-permute-start.1 = (f32[256,512]{1,0:T(8,128)}, f32[256,512]{1,0:T(8,128)}, u32[]{:S(2)}, u32[]{:S(2)}) collective-permute-start(f32[256,512]{1,0:T(8,128)} %get-tuple-element.38), channel_id=1, source_target_pairs={{0,8},{8,0},{16,24},{24,16},{1,9},{9,1},{17,25},{25,17},{2,10},{10... | collective-permute-start | bytes 1572872 | tf_op jit(solution)/shard_map/ppermute | solution.py:394
  18.4 7.1 %collective-permute-start.3 = (s32[256]{0:T(256)S(1)}, s32[256]{0:T(256)S(1)}, u32[]{:S(2)}, u32[]{:S(2)}) collective-permute-start(s32[256]{0:T(256)S(1)} %add.28), channel_id=1, source_target_pairs={{0,4},{1,5},{2,6},{3,7},{4,0},{5,1},{6,2},{7,3},{8,12},{9,13},{10,... | collective-permute-start | bytes 3080 | tf_op jit(solution)/shard_map/ppermute | solution.py:386
  26.7 7.5 %copy-start.1 = (s32[2048]{0:T(1024)S(1)}, s32[2048]{0:T(1024)}, u32[]{:S(2)}) copy-start(s32[2048]{0:T(1024)} %param.9) | copy-start | bytes 24580
  30.4 0.8 copy-start
  31.2 19.0 %all-to-all-start.1 = ((bf16[32,2,2,8,256]{4,3,2,1,0:T(8,128)(2,1)}), bf16[32,2,2,8,256]{4,3,2,1,0:T(8,128)(2,1)S(1)}, u32[]{:S(2)}, u32[]{:S(2)}) async-start(bf16[32,2,2,8,256]{4,3,2,1,0:T(8,128)(2,1)} %bitcast.16), calls=%async_computation.1 | async-start | bytes 1048576 | tf_op jit(solution)/shard_map/all_to_all | solution.py:426
  33.8 5.8 %collective-permute-start.2 = (f32[256,512]{1,0:T(8,128)}, f32[256,512]{1,0:T(8,128)S(1)}, u32[]{:S(2)}, u32[]{:S(2)}) collective-permute-start(f32[256,512]{1,0:T(8,128)} %copy-done), channel_id=1, source_target_pairs={{0,8},{8,0},{16,24},{24,16},{1,9},{9,1},{17,25},{25,17},{2,10},{10... | collective-permute-start | bytes 1572872 | tf_op jit(solution)/shard_map/ppermute | solution.py:427

commit v5 on v4

v5 whole, which is shorter than its diff:
```python
import functools
import math

import jax
import jax.numpy as jnp
from jax import lax
from jax.experimental import pallas as pl
from jax.experimental.pallas import tpu as pltpu
from jax.sharding import PartitionSpec as P

SEG = 128
CHUNK = 256
PACK = 16
BOTH = ("row", "tile")
BF = jnp.bfloat16
F32 = jnp.float32


def cos_sin(turns, quarter, scale):
    bits = int(math.log2(quarter))
    turns = turns & (4 * quarter - 1)
    octant = (turns + quarter // 2) >> bits
    angle = (turns - (octant << bits)).astype(F32) * (math.pi / (2 * quarter))
    square = angle * angle
    sin_part = angle * scale + (angle * scale) * square * (
        -1.6666654611e-1 + square * (8.3321608736e-3 - square * 1.9515295891e-4)
    )
    cos_part = scale - square * (0.5 * scale) + (square * scale) * square * (
        4.166664568298827e-2 + square * (-1.388731625493765e-3 + square * 2.443315711809948e-5)
    )
    swap = (octant & 1) == 1
    cos_out = jnp.where(swap, sin_part, cos_part)
    sin_out = jnp.where(swap, cos_part, sin_part)
    cos_out = jnp.where(((octant + 1) & 2) == 2, -cos_out, cos_out)
    sin_out = jnp.where((octant & 2) == 2, -sin_out, sin_out)
    return cos_out, sin_out


def iota(shape, dim):
    return lax.broadcasted_iota(jnp.int32, shape, dim)


def turned(cos_0, sin_0, cos_1, sin_1):
    rows, width = cos_0.shape
    cos_out, sin_out = [], []
    for j in range(cos_1.shape[0]):
        cos_j = jnp.broadcast_to(cos_1[j:j + 1], (rows, width))
        sin_j = jnp.broadcast_to(sin_1[j:j + 1], (rows, width))
        cos_out.append(cos_0 * cos_j - sin_0 * sin_j)
        sin_out.append(sin_0 * cos_j + cos_0 * sin_j)
    return jnp.concatenate(cos_out, axis=0), jnp.concatenate(sin_out, axis=0)


def middle(quarter):
    return quarter // 2 + SEG - 1


def fine_table(quarter, angles):
    width = angles.shape[-1]
    start = quarter - middle(quarter) + iota((SEG // 8, width), 0) * 16
    cos_0, sin_0 = cos_sin(2 * iota((8, width), 0) * angles, 2 * quarter, 1.0 / math.sqrt(quarter))
    cos_1, sin_1 = cos_sin(start * angles, 2 * quarter, 1.0)
    return jnp.concatenate(turned(cos_0, sin_0, cos_1, sin_1), axis=0).astype(BF)


def coarse_table(quarter, rows_dev, angles):
    width = angles.shape[-1]
    tiles = quarter // SEG // 2
    group = 8 // rows_dev
    base = (iota((8, width), 0) // rows_dev) * (2 * SEG)
    start = iota((tiles // group, width), 0) * (2 * group * SEG) + middle(quarter)
    cos_0, sin_0 = cos_sin(base * angles, 2 * quarter, 1.0)
    cos_1, sin_1 = cos_sin(start * angles, 2 * quarter, 1.0)
    return turned(cos_0, sin_0, cos_1, sin_1)


def mirrored(block):
    flip = jnp.where(iota((SEG, SEG), 0) + iota((SEG, SEG), 1) == SEG - 1, 1.0, 0.0).astype(BF)
    return jnp.dot(block, flip, preferred_element_type=F32)


def forward_kernel(quarter, rows_dev, angle_ref, cur_hbm, f_ref, cur_ref, lhs, fine, coarse, sem):
    points = rows_dev * quarter // SEG // 2
    chunks, width = angle_ref.shape[0], angle_ref.shape[-1]
    load = pltpu.make_async_copy(cur_hbm, cur_ref, sem)
    load.start()
    for i in range(chunks):
        fine[i] = fine_table(quarter, angle_ref[i])
        coarse[i, 0], coarse[i, 1] = coarse_table(quarter, rows_dev, angle_ref[i])
    load.wait()
    low_half, high_half = pl.ds(0, points), pl.ds(points, points)
    for f in range(2):
        even, odd = [], []
        for c in range(2):
            right = [cur_ref[f, k, c, high_half, :].astype(F32) for k in range(4)]
            left = [mirrored(cur_ref[f, k, c, low_half, :]) for k in range(4)]
            right = [right[0] + right[3], right[1] - right[2]]
            left = [left[0] + left[3], left[1] - left[2]]
            even.append([i + j for i, j in zip(right, left)])
            odd.append([i - j for i, j in zip(right, left)])
        for p in range(2):
            real = pl.ds((2 * f + p) * points, points)
            imag = pl.ds((4 + 2 * f + p) * points, points)
            lhs[real, :SEG] = even[0][p].astype(BF)
            lhs[real, SEG:] = odd[1][p].astype(BF)
            lhs[imag, :SEG] = even[1][p].astype(BF)
            lhs[imag, SEG:] = (-odd[0][p]).astype(BF)
    low = iota((8, width), 0) < 4
    for i in range(chunks):
        grid_sum = jnp.dot(lhs[...], fine[i], preferred_element_type=F32)
        cos_a, sin_a = coarse[i, 0], coarse[i, 1]
        for f, p in [(i, j) for i in range(2) for j in range(2)]:
            start = (2 * f + p) * points
            real = grid_sum[start:start + points]
            imag = grid_sum[4 * points + start:5 * points + start]
            out_re = jnp.sum((real * cos_a + imag * sin_a).reshape(points // 8, 8, width), axis=0)
            out_im = jnp.sum((imag * cos_a - real * sin_a).reshape(points // 8, 8, width), axis=0)
            out_re = out_re + pltpu.roll(out_re, 4, 0)
            out_im = out_im + pltpu.roll(out_im, 4, 0)
            out = jnp.where(low, out_re, out_im).astype(BF)
            for copy in range(f_ref.shape[0]):
                f_ref[copy, f, i, p] = out


def row_kernel(quarter, rows_dev, row_ref, r_ref):
    sides, depth = r_ref.shape[:2]
    share_u = row_ref.shape[-1]
    row = iota((depth, share_u), 0)
    x = (row // (2 * rows_dev)) * rows_dev + row % rows_dev
    is_imag = row % (2 * rows_dev) >= rows_dev
    scale = 1.0 / math.sqrt(depth // 2)
    for side in range(sides):
        cos_x, sin_x = cos_sin(x * row_ref[side:side + 1], quarter, scale)
        r_ref[side, :, :share_u] = jnp.where(is_imag, sin_x, cos_x).astype(BF)
        r_ref[side, :, share_u:] = jnp.where(is_imag, cos_x, -sin_x).astype(BF)


def prepare_kernel(quarter, rows_dev, tile_count, cap, angle_ref, code_ref, w_ref, choose_ref, mark_ref):
    points = code_ref.shape[0]
    slots, units = choose_ref.shape[1], mark_ref.shape[0]
    for i in range(angle_ref.shape[0]):
        w_ref[i] = fine_table(quarter, angle_ref[i])
    segs = points // rows_dev
    half = tile_count // 2
    mine = lax.axis_index("tile") // half
    point = iota((points, points), 1)
    point = (point % rows_dev) * segs + (point // rows_dev)
    source = iota((points, points), 0)
    lane = iota((PACK // 2, SEG), 1) // (SEG // 4)
    marked = jnp.zeros((units, PACK // 2, SEG), jnp.int32)
    for side in range(2):
        code_col = code_ref[:, side:side + 1]
        code_row = jnp.sum(jnp.where(source == point, code_col, 0), axis=0, keepdims=True)
        owner_col, owner_row = code_col // points, code_row // points
        same = jnp.where((source < point) & (owner_col == owner_row), 1, 0)
        rank = jnp.sum(same, axis=0, keepdims=True)
        tile = owner_row % tile_count
        place = ((owner_row // tile_count) * half + tile % half) * cap + rank
        place = jnp.where(tile // half == mine, place, -1)
        hit = iota((slots, points), 0) == place
        choose_ref[side] = jnp.where(hit, 1.0, 0.0).astype(BF)
        marks = jnp.sum(jnp.where(hit, code_row % points + 1, 0), axis=1, keepdims=True)
        marks = jnp.broadcast_to(marks, (slots, SEG)).reshape(units, 2, PACK // 2, SEG)
        for part in range(2):
            marked = jnp.where(lane == 2 * side + part, marks[:, part], marked)
    mark_ref[...] = marked.astype(F32).astype(BF)


def middle_kernel(
    table, got_ref, target_ref, far_target_ref, weight_ref, far_weight_ref, int_ref, far_int_ref, back_ref
):
    devices, pols, rows, share_v = got_ref.shape
    depth = devices * rows
    share_u = table.shape[2] // 2
    core = lax.axis_index("row") % 2
    planes = [
        got_ref[:, p].astype(F32).reshape(depth, share_v).astype(BF) for p in range(pols)
    ]
    sums = [None, None]
    sides = [
        (target_ref, weight_ref, int_ref), (far_target_ref, far_weight_ref, far_int_ref)
    ]
    for side, (goal_ref, gain_ref, power_ref) in enumerate(sides):
        mixed = [
            lax.dot_general(
                plane, table[side], (((0,), (0,)), ((), ())), preferred_element_type=F32
            )
            for plane in planes
        ]
        power = mixed[0] * mixed[0] + mixed[1] * mixed[1]
        intensity = power[:, :share_u] + power[:, share_u:]
        power_ref[...] = intensity
        factor = 4.0 * gain_ref[core] * (intensity - goal_ref[core])
        factor = jnp.concatenate([factor, factor], axis=1)
        for p in range(pols):
            far_grad = (factor * mixed[p]).astype(BF)
            back = lax.dot_general(
                table[side], far_grad, (((1,), (1,)), ((), ())), preferred_element_type=F32
            )
            sums[p] = back if side == 0 else sums[p] + back
    groups, halves, count = back_ref.shape[:3]
    for p in range(pols):
        total = sums[p].reshape(groups, halves, count, rows, share_v).astype(BF)
        for half in range(halves):
            back_ref[:, half, :, 0, p] = total[:, half]
            back_ref[:, 1 - half, :, 1, p] = total[:, half]


def adjoint_kernel(quarter, rows_dev, got_ref, w_ref, angle_ref, choose_ref, mark_ref, out_ref, total):
    chunks, width = w_ref.shape[0], w_ref.shape[2]
    points = choose_ref.shape[2] // 2
    units = out_ref.shape[0]
    low = iota((8, width), 0) < 4
    for i in range(chunks):
        cos_a, sin_a = coarse_table(quarter, rows_dev, angle_ref[i])
        reals, imags = [], []
        for side, f, p in [(i, j, k) for i in range(2) for j in range(2) for k in range(2)]:
            plane = jnp.sum(got_ref[:, f, i, side, p].astype(F32), axis=0)
            other = pltpu.roll(plane, 4, 0)
            real = jnp.where(low, plane, other)
            imag = jnp.where(low, other, plane)
            real = jnp.broadcast_to(real[None], (points // 8, 8, width)).reshape(points, width)
            imag = jnp.broadcast_to(imag[None], (points // 8, 8, width)).reshape(points, width)
            reals.append((cos_a * real - sin_a * imag).astype(BF))
            imags.append((cos_a * imag + sin_a * real).astype(BF))
        found = lax.dot_general(
            jnp.concatenate(reals + imags, axis=0), w_ref[i], (((1,), (1,)), ((), ())),
            preferred_element_type=F32,
        )
        if i == 0:
            total[...] = found
        else:
            total[...] += found
    for side, fp in [(i, j) for i in range(2) for j in range(4)]:
        start = (4 * side + fp) * points
        real = total[start:start + points, :]
        imag = total[8 * points + start:9 * points + start, :]
        real_cos, real_sin, imag_cos, imag_sin = (
            real[:, :SEG], real[:, SEG:], imag[:, :SEG], imag[:, SEG:]
        )
        left = [
            mirrored((real_cos + imag_sin).astype(BF)).astype(BF),
            mirrored((imag_cos - real_sin).astype(BF)).astype(BF),
        ]
        right = [(real_cos - imag_sin).astype(BF), (imag_cos + real_sin).astype(BF)]
        block = jnp.concatenate(
            [jnp.concatenate(left, axis=1), jnp.concatenate(right, axis=1)], axis=0
        )
        sent = jnp.dot(choose_ref[side], block, preferred_element_type=F32).astype(BF)
        sent = sent.reshape(units, PACK, 2 * SEG)
        for c in range(2):
            rows = pl.ds((8 * side + 2 * fp + c) * PACK, PACK)
            out_ref[:, rows, :] = sent[:, :, c * SEG:(c + 1) * SEG]
    out_ref[:, 16 * PACK:, :] = mark_ref[...]


def faces_kernel(got_ref, out_ref):
    faces = out_ref.shape[3]
    units = got_ref.shape[0]
    slots = units * PACK
    marks = got_ref[:, 16 * PACK:, :].astype(F32)
    hits = []
    for side in range(2):
        spots = [(2 * side + part) * (SEG // 4) for part in range(2)]
        mark = jnp.concatenate([marks[:, :, i:i + 1] for i in spots], axis=1)
        mark = jnp.broadcast_to(mark.reshape(slots, 1), (slots, faces)).astype(jnp.int32)
        hits.append(jnp.where(iota((slots, faces), 1) + 1 == mark, 1.0, 0.0).astype(BF))
    choose = jnp.concatenate(hits, axis=0)
    for f in range(2):
        for p in range(2):
            for c in range(2):
                blocks = []
                for side in range(2):
                    rows = pl.ds((8 * side + 4 * f + 2 * p + c) * PACK, PACK)
                    blocks.append(got_ref[:, rows, :].reshape(slots, SEG))
                found = lax.dot_general(
                    choose, jnp.concatenate(blocks, axis=0), (((0,), (0,)), ((), ())),
                    preferred_element_type=F32,
                )
                if p == 0:
                    out_ref[f, 0, c] = found
                    out_ref[f, 3, c] = found
                else:
                    out_ref[f, 1, c] = found
                    out_ref[f, 2, c] = -found


def exchange_small(outgoing, groups, cap):
    units = outgoing.shape[0]
    peers = units * PACK // cap
    swap = functools.partial(
        lax.all_to_all, axis_name=BOTH, split_axis=1, concat_axis=1, tiled=True, axis_index_groups=groups
    )
    rows = outgoing[:, :16 * PACK].reshape(units, 16, PACK, SEG).transpose(1, 0, 2, 3)
    rows = swap(rows.reshape(16, peers, cap, SEG))
    rows = rows.reshape(16, units, PACK, SEG).transpose(1, 0, 2, 3).reshape(units, 16 * PACK, SEG)
    marks = outgoing[:, 16 * PACK:, ::SEG // 4].reshape(units, PACK // 2, 2, 2).transpose(2, 0, 3, 1)
    marks = swap(marks.reshape(2, peers, cap)).reshape(2, units, 2, PACK // 2)
    marks = marks.transpose(1, 3, 0, 2).reshape(units, PACK // 2, 4)
    return jnp.concatenate([rows, jnp.repeat(marks, SEG // 4, axis=2)], axis=1)


def params(mib=24):
    return pltpu.CompilerParams(
        dimension_semantics=("arbitrary",), vmem_limit_bytes=mib * 1024 * 1024
    )


def cost(flops, moved):
    return pl.CostEstimate(flops=int(flops), bytes_accessed=int(moved), transcendentals=0)


def whole(shape):
    return pl.BlockSpec(shape, lambda i: (0,) * len(shape))


def body(currents, row_angles, column_angles, target, weight, tile_owner, face_slot):
    row_count = lax.axis_size("row")
    tile_count = lax.axis_size("tile")
    devices = row_count * tile_count
    freq_count, comp_count, part_count, rows_dev, columns = currents.shape
    far_rows = row_angles.shape[0]
    far_cols = column_angles.shape[0]
    share_v = far_cols // tile_count
    share_u = far_rows // row_count
    chunks = far_cols // CHUNK
    tiles = columns // SEG
    points = rows_dev * tiles
    half = points // 2
    cap = 2 * points // devices
    slots = points
    units = slots // PACK
    held = 16 * PACK + PACK // 2
    pairs = row_count // 2
    wide = 2 * rows_dev
    depth = devices * wide
    tile_half = tile_count // 2
    half_groups = [
        [r * tile_count + side * tile_half + t for r in range(row_count) for t in range(tile_half)]
        for side in range(2)
    ]
    mirror = [(i, (i + tile_half) % tile_count) for i in range(tile_count)]
    angles = column_angles.reshape(chunks, 1, CHUNK)
    cur = currents.reshape(freq_count, comp_count, part_count, rows_dev, tiles, SEG)
    cur = cur.transpose(0, 1, 2, 4, 3, 5).reshape(freq_count, comp_count, part_count, points, SEG)
    copies = pairs if share_v == CHUNK else 1
    plane = pl.pallas_call(
        functools.partial(forward_kernel, columns, rows_dev),
        grid=(1,),
        in_specs=[whole(angles.shape), pl.BlockSpec(memory_space=pltpu.HBM)],
        out_specs=whole((copies, 2, chunks, 2, wide, CHUNK)),
        out_shape=jax.ShapeDtypeStruct((copies, 2, chunks, 2, wide, CHUNK), BF),
        scratch_shapes=[
            pltpu.VMEM(cur.shape, BF),
            pltpu.VMEM((8 * half, 2 * SEG), BF),
            pltpu.VMEM((chunks, 2 * SEG, CHUNK), BF),
            pltpu.VMEM((chunks, 2, half, CHUNK), F32),
            pltpu.SemaphoreType.DMA(()),
        ],
        compiler_params=params(58),
        cost_estimate=cost(4.3e9, 1.6e6),
        name="columns",
    )(angles, cur)
    if share_v != CHUNK:
        plane = plane.reshape(2, chunks, 2, wide, CHUNK // share_v, share_v)
        plane = plane.transpose(0, 1, 4, 2, 3, 5).reshape(1, 2, tile_count, 2, wide, share_v)
        plane = jnp.broadcast_to(plane, (pairs,) + plane.shape[1:])
    plane = plane.reshape(devices, 2, wide, share_v)

    row_angles, owner, slot, plane = lax.optimization_barrier(
        (row_angles, tile_owner, face_slot, plane)
    )
    got = lax.all_to_all(plane, BOTH, 0, 0, tiled=True)
    here = lax.axis_index("row")
    core = here % 2
    swap = [(i, i ^ 1) for i in range(row_count)]
    code = owner[:, 0] * points + slot
    code = jnp.stack([code, lax.ppermute(code, "tile", mirror)], axis=1)
    own_angles = jnp.stack(
        [lax.dynamic_slice_in_dim(row_angles, i * share_u, share_u) for i in (here, here ^ 1)]
    )
    far_target = lax.ppermute(target, "row", swap)
    far_weight = lax.ppermute(weight, "row", swap)
    row_table = pl.pallas_call(
        functools.partial(row_kernel, columns, rows_dev),
        grid=(1,),
        in_specs=[whole((2, share_u))],
        out_specs=whole((2, depth, 2 * share_u)),
        out_shape=jax.ShapeDtypeStruct((2, depth, 2 * share_u), BF),
        compiler_params=params(),
        cost_estimate=cost(1e8, 5e5),
        name="rows",
    )(own_angles)

    far_shape = (share_v, share_u)
    back_shape = (row_count, 2, tile_half, 2, 2, wide, share_v)
    power, far_power, back = pl.pallas_call(
        middle_kernel,
        grid=(1,),
        in_specs=[whole((2, depth, 2 * share_u)), whole((devices, 2, wide, share_v))]
        + [whole(target.shape)] * 4,
        out_specs=[whole(far_shape), whole(far_shape), whole(back_shape)],
        out_shape=[
            jax.ShapeDtypeStruct(far_shape, F32),
            jax.ShapeDtypeStruct(far_shape, F32),
            jax.ShapeDtypeStruct(back_shape, BF),
        ],
        compiler_params=params(),
        cost_estimate=cost(1.1e9, 5e6),
        name="objective",
    )(row_table, got, target, far_target, weight, far_weight)

    angles, code, back = lax.optimization_barrier((angles, code, back))
    back = back.reshape(devices, 2, 2, wide, share_v)
    back = lax.all_to_all(back, BOTH, 0, 0, tiled=True)
    table, choose, mark = pl.pallas_call(
        functools.partial(prepare_kernel, columns, rows_dev, tile_count, cap),
        grid=(1,),
        in_specs=[whole(angles.shape), whole((points, 2))],
        out_specs=[
            whole((chunks, 2 * SEG, CHUNK)),
            whole((2, slots, points)),
            whole((units, PACK // 2, SEG)),
        ],
        out_shape=[
            jax.ShapeDtypeStruct((chunks, 2 * SEG, CHUNK), BF),
            jax.ShapeDtypeStruct((2, slots, points), BF),
            jax.ShapeDtypeStruct((units, PACK // 2, SEG), BF),
        ],
        compiler_params=params(),
        cost_estimate=cost(1e9, 2e6),
        name="prepare",
    )(angles, code)
    far_power, mark = lax.optimization_barrier((far_power, mark))
    far_power = lax.ppermute(far_power, "row", swap)
    intensity = jnp.where(
        core == 0, jnp.stack([power, far_power]), jnp.stack([far_power, power])
    )
    intensity, mark = lax.optimization_barrier((intensity, mark))

    back = back.reshape(pairs, 2, tile_count, 2, 2, wide, share_v)
    if share_v != CHUNK:
        back = back.reshape(pairs, 2, chunks, CHUNK // share_v, 2, 2, wide, share_v)
        back = back.transpose(0, 1, 2, 4, 5, 6, 3, 7).reshape(pairs, 2, chunks, 2, 2, wide, CHUNK)
    outgoing = pl.pallas_call(
        functools.partial(adjoint_kernel, columns, rows_dev),
        grid=(1,),
        in_specs=[
            whole((pairs, 2, chunks, 2, 2, wide, CHUNK)),
            whole((chunks, 2 * SEG, CHUNK)),
            whole(angles.shape),
            whole((2, slots, points)),
            whole((units, PACK // 2, SEG)),
        ],
        out_specs=whole((units, held, SEG)),
        out_shape=jax.ShapeDtypeStruct((units, held, SEG), BF),
        scratch_shapes=[pltpu.VMEM((16 * half, 2 * SEG), F32)],
        compiler_params=params(),
        cost_estimate=cost(4.3e9, 4e6),
        name="adjoint",
    )(back, table, angles, choose, mark)

    if cap == PACK:
        arrived = lax.all_to_all(outgoing, BOTH, 0, 0, tiled=True, axis_index_groups=half_groups)
    else:
        arrived = exchange_small(outgoing, half_groups, cap)
    out_shape = (freq_count, comp_count, part_count, points, SEG)
    faces = pl.pallas_call(
        faces_kernel,
        grid=(1,),
        in_specs=[whole((units, held, SEG))],
        out_specs=whole(out_shape),
        out_shape=jax.ShapeDtypeStruct(out_shape, F32),
        compiler_params=params(),
        name="faces",
    )(arrived)
    return (intensity, faces)


def solution(mesh):
    in_specs = (
        P(None, None, None, ("row", "tile"), None),
        P(),
        P(),
        P(None, "tile", "row"),
        P(None, "tile", "row"),
        P(("row", "tile"), None),
        P(("row", "tile")),
    )
    out_specs = (P(None, "tile", "row"), P(None, None, None, ("row", "tile"), None))
    return jax.shard_map(body, mesh=mesh, in_specs=in_specs, out_specs=out_specs, check_vma=False)
```

time: 81.1 us -> 76.2 us (0.940)
  Pallas kernels: 30.1 us -> 18.8 us
  waiting for transfers between devices: 13.4 us -> 18.5 us
  other arithmetic: 1.11 us -> 2.34 us
    pallas_call x1, Pallas kernels: 5.46 us -> 1.26 us  [body(): pl.pallas_call(functools.partial(prepare_kernel, columns, rows_dev, tile_...]
    pallas_call x1, Pallas kernels: 9.01 us -> 5.3 us  [body(): pl.pallas_call(functools.partial(adjoint_kernel, columns, rows_dev), grid...]
    pallas_call x1, Pallas kernels: 8.05 us -> 5.01 us  [body(): pl.pallas_call(functools.partial(forward_kernel, columns, rows_dev), grid...]
    ppermute x1, waiting for transfers between devices: 2.65 us -> 4.96 us  [body(): code = jnp.stack([code, lax.ppermute(code, 'tile', mirror)], axis=1)]
    ppermute x1, waiting for transfers between devices: 0.01 us -> 2.02 us  [body(): far_power = lax.ppermute(far_power, 'row', swap)]
    squeeze x2 -> x0, local copies, waits for them, and re-layouts: 1.76 us -> none  [body(): other = lax.dynamic_index_in_dim(array, 1 - core, 0, keepdims=False)]
    unnamed x14 -> x22, local copies, waits for them, and re-layouts: 0.83 us -> 2.42 us
    select_n x1, other arithmetic: 1.08 us -> 2.32 us  [body(): jnp.where(core == 0, jnp.stack([power, far_power]), jnp.stack([far_power,...]
  transfers between devices with their start and end apart: 6 -> 6, of which waited for: 3 -> 4; matrix products, arithmetic and copies ran while one was open for 4% -> 3% of each run, Pallas kernels for 9% -> 10%
where the time goes in v5:
time: 76.2 us; the launch traced here: 75.8 us
  blocking collectives  19.1 us (25%)
  Pallas kernels  18.8 us (25%)
  waiting for transfers between devices  18.5 us (24%)
  starting transfers between devices  13.6 us (18%)
  local copies, waits for them, and re-layouts  2.63 us (3%)
  other arithmetic  2.34 us (3%)
  between operations  0.81 us (1%)
    all_to_all x1, blocking collectives, body(): lax.all_to_all(outgoing, BOTH, 0, 0, tiled=True, axis_index_groups=half_g...  19.1 us
    all_to_all x1, waiting for transfers between devices, body(): back = lax.all_to_all(back, BOTH, 0, 0, tiled=True)  10.3 us
    all_to_all x1, starting transfers between devices, body(): got = lax.all_to_all(plane, BOTH, 0, 0, tiled=True)  7.28 us
    pallas_call x1, Pallas kernels, body(): pl.pallas_call(functools.partial(adjoint_kernel, columns, rows_dev), grid...  5.3 us
    pallas_call x1, Pallas kernels, body(): pl.pallas_call(functools.partial(forward_kernel, columns, rows_dev), grid...  5.01 us
    ppermute x1, waiting for transfers between devices, body(): code = jnp.stack([code, lax.ppermute(code, 'tile', mirror)], axis=1)  4.96 us
    pallas_call x1, Pallas kernels, body(): pl.pallas_call(middle_kernel, grid=(1,), in_specs=[whole((2, depth, 2 * s...  3.41 us
    all_to_all x1, starting transfers between devices, body(): back = lax.all_to_all(back, BOTH, 0, 0, tiled=True)  2.92 us
  transfers between devices with their start and end apart: 6, of which 4 were waited for; matrix products, arithmetic and copies ran while one was open for 3% of the time, Pallas kernels for 10%

profile of v5, /device:TPU:0, one launch (start us, length us, event | category | flops | bytes accessed | tf_op | source)
XLA Modules:
  0.0 75.8 jit_solution(17368128344695671436)
XLA Ops:
  0.6 0.5 collective-permute-start
  1.1 0.1 collective-permute-start.1
  1.2 0.0 copy-start.10
  1.2 0.0 copy-start.9
  1.2 0.0 copy-start.8
  1.2 0.0 copy-start.1
  1.2 5.0 %columns.1 = bf16[2,2,8,2,8,256]{5,4,3,2,1,0:T(8,128)(2,1)} custom-call(s32[8,1,256]{2,1,0:T(1,128)} %bitcast.19, bf16[2,4,2,256,128]{4,3,2,1,0:T(8,128)(2,1)} %bitcast.28), custom_call_target="tpu_custom_call" | custom-call | flops 4300000256 | bytes 1600000 | tf_op jit(solution)/shard_map/columns/pallas_call | solution.py:347
  6.3 0.0 copy-start
  6.3 7.3 %all-to-all-start = ((bf16[32,2,8,256]{3,2,1,0:T(8,128)(2,1)}), bf16[32,2,8,256]{3,2,1,0:T(8,128)(2,1)S(1)}, u32[]{:S(2)}, u32[]{:S(2)}) async-start(bf16[32,2,8,256]{3,2,1,0:T(8,128)(2,1)} %bitcast.22), calls=%async_computation | async-start | bytes 524288 | tf_op jit(solution)/shard_map/all_to_all | solution.py:373
  13.6 0.0 copy-done.10
  13.6 0.0 copy-done.9
  13.6 2.7 %collective-permute-start.2 = (s32[256]{0:T(256)S(1)}, s32[256]{0:T(256)S(1)}, u32[]{:S(2)}, u32[]{:S(2)}) collective-permute-start(s32[256]{0:T(256)S(1)} %add.16), channel_id=1, source_target_pairs={{0,4},{1,5},{2,6},{3,7},{4,0},{5,1},{6,2},{7,3},{8,12},{9,13},{10,... | collective-permute-start | bytes 3080 | tf_op jit(solution)/shard_map/ppermute | solution.py:378
  16.3 0.0 copy-done.8
  16.3 0.1 fusion
  16.4 1.6 %rows.1.table = bf16[2,256,1024]{2,1,0:T(8,128)(2,1)S(1)} custom-call(s32[2,512]{1,0:T(2,128)S(1)} %pad_add_fusion.row_ref), custom_call_target="tpu_custom_call" | custom-call | flops 100000000 | bytes 500000 | tf_op jit(solution)/shard_map/rows/pallas_call | solution.py:384
  18.0 5.0 %collective-permute-done.2 = s32[256]{0:T(256)S(1)} collective-permute-done((s32[256]{0:T(256)S(1)}, s32[256]{0:T(256)S(1)}, u32[]{:S(2)}, u32[]{:S(2)}) %collective-permute-start.2) | collective-permute-done | bytes 1056 | tf_op jit(solution)/shard_map/ppermute | solution.py:378
  23.0 1.2 %all-to-all-done.got_ref = bf16[32,2,8,256]{3,2,1,0:T(8,128)(2,1)S(1)} async-done(((bf16[32,2,8,256]{3,2,1,0:T(8,128)(2,1)}), bf16[32,2,8,256]{3,2,1,0:T(8,128)(2,1)S(1)}, u32[]{:S(2)}, u32[]{:S(2)}) %all-to-all-start) | async-done | bytes 262176 | tf_op jit(solution)/shard_map/all_to_all | solution.py:373
  24.2 0.0 collective-permute-done.far_target_ref
  24.2 0.0 collective-permute-done.1.far_weight_ref
  24.2 0.0 copy-done.1
  24.2 0.0 copy-done
  24.2 3.4 %objective.1 = (f32[256,512]{1,0:T(8,128)S(1)}, f32[256,512]{1,0:T(8,128)S(1)}, bf16[4,2,4,2,2,8,256]{6,5,4,3,2,1,0:T(8,128)(2,1)S(1)}) custom-call(bf16[2,256,1024]{2,1,0:T(8,128)(2,1)S(1)} %rows.1.table, bf16[32,2,8,256]{3,2,1,0:T(8,128)(2,1)S(1)} %all-to-all-done.got_ref, f32[2,256,512]{2,1,0:T(8,128)S(1)} %copy-done, ...), custom_call_target="tpu_custom_call" | custom-call | flops 1100000000 | bytes 5000000 | tf_op jit(solution)/shard_map/objective/pallas_call | solution.py:397
  27.7 0.0 copy-start.2
  27.7 0.8 %copy-done.2 = f32[256,512]{1,0:T(8,128)} copy-done((f32[256,512]{1,0:T(8,128)}, f32[256,512]{1,0:T(8,128)S(1)}, u32[]{:S(2)}) %copy-start.2) | copy-done | bytes 524312
  28.5 0.0 copy-start.4
  28.5 0.8 %copy-done.4 = bf16[4,2,4,2,2,8,256]{6,5,4,3,2,1,0:T(8,128)(2,1)} copy-done((bf16[4,2,4,2,2,8,256]{6,5,4,3,2,1,0:T(8,128)(2,1)}, bf16[4,2,4,2,2,8,256]{6,5,4,3,2,1,0:T(8,128)(2,1)S(1)}, u32[]{:S(2)}) %copy-start.4) | copy-done | bytes 524312
  29.3 0.0 copy-start.5
  29.3 0.8 %copy-done.5 = f32[256,512]{1,0:T(8,128)} copy-done((f32[256,512]{1,0:T(8,128)}, f32[256,512]{1,0:T(8,128)S(1)}, u32[]{:S(2)}) %copy-start.5) | copy-done | bytes 524312
  30.1 0.0 copy-start.7
  30.1 2.9 %all-to-all-start.1 = ((bf16[32,2,2,8,256]{4,3,2,1,0:T(8,128)(2,1)}), bf16[32,2,2,8,256]{4,3,2,1,0:T(8,128)(2,1)S(1)}, u32[]{:S(2)}, u32[]{:S(2)}) async-start(bf16[32,2,2,8,256]{4,3,2,1,0:T(8,128)(2,1)} %bitcast.18), calls=%async_computation.1 | async-start | bytes 1048576 | tf_op jit(solution)/shard_map/all_to_all | solution.py:415
  33.0 0.1 copy.14.code_ref
  33.1 0.0 copy-done.7
  33.1 0.0 copy-start.6
  33.1 0.0 copy-start.3
  33.2 1.3 %prepare.1 = (bf16[8,256,256]{2,1,0:T(8,128)(2,1)S(1)}, bf16[2,256,256]{2,1,0:T(8,128)(2,1)S(1)}, bf16[16,8,128]{2,1,0:T(8,128)(2,1)S(1)}) custom-call(s32[8,1,256]{2,1,0:T(1,128)S(1)} %bitcast.20, s32[256,2]{1,0:T(8,128)S(1)} %copy.14.code_ref), custom_call_target="tpu_custom_call" | custom-call | flops 1000000000 | bytes 2000000 | tf_op jit(solution)/shard_map/prepare/pallas_call | solution.py:416
  34.4 0.0 copy-done.6
  34.4 0.1 collective-permute-start.3
  34.5 2.0 %collective-permute-done.3 = f32[256,512]{1,0:T(8,128)} collective-permute-done((f32[256,512]{1,0:T(8,128)S(1)}, f32[256,512]{1,0:T(8,128)}, u32[]{:S(2)}, u32[]{:S(2)}) %collective-permute-start.3) | collective-permute-done | bytes 524320 | tf_op jit(solution)/shard_map/ppermute | solution.py:435
  36.5 0.0 copy-done.3
  36.5 2.3 %maximum_select_fusion = f32[2,256,512]{2,1,0:T(8,128)} fusion(f32[1,256,512]{2,1,0:T(8,128)} %bitcast.11, f32[1,256,512]{2,1,0:T(8,128)S(1)} %bitcast.16, pred[]{:T(512)S(6)} %eq.5), kind=kLoop, calls=%fused_computation | loop fusion | flops 786432 | bytes 2097153 | tf_op jit(solution)/shard_map/jit(_where)/select_n | solution.py:436
  38.9 10.3 %all-to-all-done.1 = bf16[32,2,2,8,256]{4,3,2,1,0:T(8,128)(2,1)S(1)} async-done(((bf16[32,2,2,8,256]{4,3,2,1,0:T(8,128)(2,1)}), bf16[32,2,2,8,256]{4,3,2,1,0:T(8,128)(2,1)S(1)}, u32[]{:S(2)}, u32[]{:S(2)}) %all-to-all-start.1) | async-done | bytes 524320 | tf_op jit(solution)/shard_map/all_to_all | solution.py:415
  49.1 5.3 %adjoint.1 = bf16[16,264,128]{2,1,0:T(8,128)(2,1)S(1)} custom-call(bf16[2,2,8,2,2,8,256]{6,5,4,3,2,1,0:T(8,128)(2,1)S(1)} %bitcast.17, bf16[8,256,256]{2,1,0:T(8,128)(2,1)S(1)} %get-tuple-element.33.w_ref, s32[8,1,256]{2,1,0:T(1,128)S(1)} %bitcast.21, bf16[2,256,256]{2,1,0:T(8,128)(2,1)S(1)} %get-tuple-element.34.choose_ref, ...), custom_call_target="tpu_custom_call" | custom-call | flops 4300000256 | bytes 4000000 | tf_op jit(solution)/shard_map/adjoint/pallas_call | solution.py:445
  54.5 19.1 %all_to_all.15.got_ref = bf16[16,264,128]{2,1,0:T(8,128)(2,1)S(1)} all-to-all(bf16[16,264,128]{2,1,0:T(8,128)(2,1)S(1)} %adjoint.1), channel_id=1, replica_groups={{0,1,2,3,8,9,10,11,16,17,18,19,24,25,26,27},{4,5,6,7,12,13,14,15,20,21,..., dimensions={0} | all-to-all | bytes 2162688 | tf_op jit(solution)/shard_map/all_to_all | solution.py:464
  73.5 2.3 %faces.1 = f32[2,4,2,256,128]{4,3,2,1,0:T(8,128)} custom-call(bf16[16,264,128]{2,1,0:T(8,128)(2,1)S(1)} %all_to_all.15.got_ref), custom_call_target="tpu_custom_call" | custom-call | tf_op jit(solution)/shard_map/faces/pallas_call | solution.py:468
  (4 shorter events, 0.0 us)
Async XLA Ops:
  0.6 23.6 %collective-permute-start = (f32[2,256,512]{2,1,0:T(8,128)}, f32[2,256,512]{2,1,0:T(8,128)}, u32[]{:S(2)}, u32[]{:S(2)}) collective-permute-start(f32[2,256,512]{2,1,0:T(8,128)} %target_ref.1), channel_id=1, source_target_pairs={{0,8},{8,0},{16,24},{24,16},{1,9},{9,1},{17,25},{25,17},{2,10},{10... | collective-permute-start | bytes 3145736 | tf_op jit(solution)/shard_map/ppermute | solution.py:382
  1.1 23.1 %collective-permute-start.1 = (f32[2,256,512]{2,1,0:T(8,128)}, f32[2,256,512]{2,1,0:T(8,128)}, u32[]{:S(2)}, u32[]{:S(2)}) collective-permute-start(f32[2,256,512]{2,1,0:T(8,128)} %weight_ref.1), channel_id=1, source_target_pairs={{0,8},{8,0},{16,24},{24,16},{1,9},{9,1},{17,25},{25,17},{2,10},{10... | collective-permute-start | bytes 3145736 | tf_op jit(solution)/shard_map/ppermute | solution.py:383
  1.2 12.3 %copy-start.10 = (s32[256,1]{0,1:T(1,128)S(1)}, s32[256,1]{0,1:T(1,128)}, u32[]{:S(2)}) copy-start(s32[256,1]{0,1:T(1,128)} %param.12) | copy-start | bytes 3076
  1.2 12.4 %copy-start.9 = (s32[256]{0:T(256)S(1)}, s32[256]{0:T(256)}, u32[]{:S(2)}) copy-start(s32[256]{0:T(256)} %param.13) | copy-start | bytes 3076
  1.2 15.1 %copy-start.8 = (s32[2048]{0:T(1024)S(1)}, s32[2048]{0:T(1024)}, u32[]{:S(2)}) copy-start(s32[2048]{0:T(1024)} %param.8) | copy-start | bytes 24580
  1.2 23.0 %copy-start.1 = (f32[2,256,512]{2,1,0:T(8,128)S(1)}, f32[2,256,512]{2,1,0:T(8,128)}, u32[]{:S(2)}) copy-start(f32[2,256,512]{2,1,0:T(8,128)} %weight_ref.1) | copy-start | bytes 3145732
  6.3 18.0 %copy-start = (f32[2,256,512]{2,1,0:T(8,128)S(1)}, f32[2,256,512]{2,1,0:T(8,128)}, u32[]{:S(2)}) copy-start(f32[2,256,512]{2,1,0:T(8,128)} %target_ref.1) | copy-start | bytes 3145732
  6.3 17.9 %all-to-all-start = ((bf16[32,2,8,256]{3,2,1,0:T(8,128)(2,1)}), bf16[32,2,8,256]{3,2,1,0:T(8,128)(2,1)S(1)}, u32[]{:S(2)}, u32[]{:S(2)}) async-start(bf16[32,2,8,256]{3,2,1,0:T(8,128)(2,1)} %bitcast.22), calls=%async_computation | async-start | bytes 524288 | tf_op jit(solution)/shard_map/all_to_all | solution.py:373
  13.6 9.4 %collective-permute-start.2 = (s32[256]{0:T(256)S(1)}, s32[256]{0:T(256)S(1)}, u32[]{:S(2)}, u32[]{:S(2)}) collective-permute-start(s32[256]{0:T(256)S(1)} %add.16), channel_id=1, source_target_pairs={{0,4},{1,5},{2,6},{3,7},{4,0},{5,1},{6,2},{7,3},{8,12},{9,13},{10,... | collective-permute-start | bytes 3080 | tf_op jit(solution)/shard_map/ppermute | solution.py:378
  27.7 0.8 %copy-start.2 = (f32[256,512]{1,0:T(8,128)}, f32[256,512]{1,0:T(8,128)S(1)}, u32[]{:S(2)}) copy-start(f32[256,512]{1,0:T(8,128)S(1)} %get-tuple-element.21) | copy-start | bytes 1572868
  28.5 0.8 %copy-start.4 = (bf16[4,2,4,2,2,8,256]{6,5,4,3,2,1,0:T(8,128)(2,1)}, bf16[4,2,4,2,2,8,256]{6,5,4,3,2,1,0:T(8,128)(2,1)S(1)}, u32[]{:S(2)}) copy-start(bf16[4,2,4,2,2,8,256]{6,5,4,3,2,1,0:T(8,128)(2,1)S(1)} %get-tuple-element.32) | copy-start | bytes 1572868
  29.3 0.8 %copy-start.5 = (f32[256,512]{1,0:T(8,128)}, f32[256,512]{1,0:T(8,128)S(1)}, u32[]{:S(2)}) copy-start(f32[256,512]{1,0:T(8,128)S(1)} %get-tuple-element.29) | copy-start | bytes 1572868
  30.1 3.1 %copy-start.7 = (s32[2048]{0:T(1024)S(1)}, s32[2048]{0:T(1024)}, u32[]{:S(2)}) copy-start(s32[2048]{0:T(1024)} %param.9) | copy-start | bytes 24580
  30.1 19.1 %all-to-all-start.1 = ((bf16[32,2,2,8,256]{4,3,2,1,0:T(8,128)(2,1)}), bf16[32,2,2,8,256]{4,3,2,1,0:T(8,128)(2,1)S(1)}, u32[]{:S(2)}, u32[]{:S(2)}) async-start(bf16[32,2,2,8,256]{4,3,2,1,0:T(8,128)(2,1)} %bitcast.18), calls=%async_computation.1 | async-start | bytes 1048576 | tf_op jit(solution)/shard_map/all_to_all | solution.py:415
  33.1 1.3 %copy-start.6 = (f32[256,512]{1,0:T(8,128)S(1)}, f32[256,512]{1,0:T(8,128)}, u32[]{:S(2)}) copy-start(f32[256,512]{1,0:T(8,128)} %copy-done.5) | copy-start | bytes 1572868
  33.1 3.4 %copy-start.3 = (f32[256,512]{1,0:T(8,128)S(1)}, f32[256,512]{1,0:T(8,128)}, u32[]{:S(2)}) copy-start(f32[256,512]{1,0:T(8,128)} %copy-done.2) | copy-start | bytes 1572868
  34.4 2.1 %collective-permute-start.3 = (f32[256,512]{1,0:T(8,128)S(1)}, f32[256,512]{1,0:T(8,128)}, u32[]{:S(2)}, u32[]{:S(2)}) collective-permute-start(f32[256,512]{1,0:T(8,128)S(1)} %copy-done.6), channel_id=1, source_target_pairs={{0,8},{8,0},{16,24},{24,16},{1,9},{9,1},{17,25},{25,17},{2,10},{10... | collective-permute-start | bytes 1572872 | tf_op jit(solution)/shard_map/ppermute | solution.py:435

commit v6 on v5

--- a/solution.py
+++ b/solution.py
@@ -82,14 +82,19 @@
 def forward_kernel(quarter, rows_dev, angle_ref, cur_hbm, f_ref, cur_ref, lhs, fine, coarse, sem):
     points = rows_dev * quarter // SEG // 2
     chunks, width = angle_ref.shape[0], angle_ref.shape[-1]
-    load = pltpu.make_async_copy(cur_hbm, cur_ref, sem)
-    load.start()
+    loads = [
+        [pltpu.make_async_copy(cur_hbm.at[f, k], cur_ref.at[f, k], sem.at[f, k]) for k in range(4)]
+        for f in range(2)
+    ]
+    for load in loads[0] + loads[1]:
+        load.start()
     for i in range(chunks):
         fine[i] = fine_table(quarter, angle_ref[i])
         coarse[i, 0], coarse[i, 1] = coarse_table(quarter, rows_dev, angle_ref[i])
-    load.wait()
     low_half, high_half = pl.ds(0, points), pl.ds(points, points)
     for f in range(2):
+        for load in loads[f]:
+            load.wait()
         even, odd = [], []
         for c in range(2):
             right = [cur_ref[f, k, c, high_half, :].astype(F32) for k in range(4)]
@@ -135,7 +140,13 @@
         r_ref[side, :, share_u:] = jnp.where(is_imag, cos_x, -sin_x).astype(BF)
 
 
-def prepare_kernel(quarter, rows_dev, tile_count, cap, angle_ref, code_ref, w_ref, choose_ref, mark_ref):
+def prepare_kernel(
+    quarter, rows_dev, tile_count, cap, angle_ref, code_ref, power_ref, far_power_ref,
+    w_ref, choose_ref, mark_ref, int_ref,
+):
+    core = lax.axis_index("row") % 2
+    int_ref[core] = power_ref[0]
+    int_ref[1 - core] = far_power_ref[...]
     points = code_ref.shape[0]
     slots, units = choose_ref.shape[1], mark_ref.shape[0]
     for i in range(angle_ref.shape[0]):
@@ -167,7 +178,8 @@
 
 
 def middle_kernel(
-    table, got_ref, target_ref, far_target_ref, weight_ref, far_weight_ref, int_ref, far_int_ref, back_ref
+    table, got_ref, target_ref, far_target_ref, weight_ref, far_weight_ref,
+    power_hbm, back_ref, powers, sems,
 ):
     devices, pols, rows, share_v = got_ref.shape
     depth = devices * rows
@@ -177,10 +189,9 @@
         got_ref[:, p].astype(F32).reshape(depth, share_v).astype(BF) for p in range(pols)
     ]
     sums = [None, None]
-    sides = [
-        (target_ref, weight_ref, int_ref), (far_target_ref, far_weight_ref, far_int_ref)
-    ]
-    for side, (goal_ref, gain_ref, power_ref) in enumerate(sides):
+    stores = []
+    sides = [(target_ref, weight_ref), (far_target_ref, far_weight_ref)]
+    for side, (goal_ref, gain_ref) in enumerate(sides):
         mixed = [
             lax.dot_general(
                 plane, table[side], (((0,), (0,)), ((), ())), preferred_element_type=F32
@@ -189,7 +200,9 @@
         ]
         power = mixed[0] * mixed[0] + mixed[1] * mixed[1]
         intensity = power[:, :share_u] + power[:, share_u:]
-        power_ref[...] = intensity
+        powers[side] = intensity
+        stores.append(pltpu.make_async_copy(powers.at[side], power_hbm.at[side], sems.at[side]))
+        stores[-1].start()
         factor = 4.0 * gain_ref[core] * (intensity - goal_ref[core])
         factor = jnp.concatenate([factor, factor], axis=1)
         for p in range(pols):
@@ -204,9 +217,13 @@
         for half in range(halves):
             back_ref[:, half, :, 0, p] = total[:, half]
             back_ref[:, 1 - half, :, 1, p] = total[:, half]
-
-
-def adjoint_kernel(quarter, rows_dev, got_ref, w_ref, angle_ref, choose_ref, mark_ref, out_ref, total):
+    for store in stores:
+        store.wait()
+
+
+def adjoint_kernel(
+    quarter, rows_dev, got_ref, w_ref, angle_ref, choose_ref, mark_ref, out_ref, total
+):
     chunks, width = w_ref.shape[0], w_ref.shape[2]
     points = choose_ref.shape[2] // 2
     units = out_ref.shape[0]
@@ -254,7 +271,7 @@
     out_ref[:, 16 * PACK:, :] = mark_ref[...]
 
 
-def faces_kernel(got_ref, out_ref):
+def faces_kernel(got_ref, out_hbm, out_ref, sems):
     faces = out_ref.shape[3]
     units = got_ref.shape[0]
     slots = units * PACK
@@ -266,23 +283,28 @@
         mark = jnp.broadcast_to(mark.reshape(slots, 1), (slots, faces)).astype(jnp.int32)
         hits.append(jnp.where(iota((slots, faces), 1) + 1 == mark, 1.0, 0.0).astype(BF))
     choose = jnp.concatenate(hits, axis=0)
-    for f in range(2):
-        for p in range(2):
-            for c in range(2):
-                blocks = []
-                for side in range(2):
-                    rows = pl.ds((8 * side + 4 * f + 2 * p + c) * PACK, PACK)
-                    blocks.append(got_ref[:, rows, :].reshape(slots, SEG))
-                found = lax.dot_general(
-                    choose, jnp.concatenate(blocks, axis=0), (((0,), (0,)), ((), ())),
-                    preferred_element_type=F32,
-                )
-                if p == 0:
-                    out_ref[f, 0, c] = found
-                    out_ref[f, 3, c] = found
-                else:
-                    out_ref[f, 1, c] = found
-                    out_ref[f, 2, c] = -found
+    stores = []
+    for f, p in [(i, j) for i in range(2) for j in range(2)]:
+        for c in range(2):
+            blocks = []
+            for side in range(2):
+                rows = pl.ds((8 * side + 4 * f + 2 * p + c) * PACK, PACK)
+                blocks.append(got_ref[:, rows, :].reshape(slots, SEG))
+            found = lax.dot_general(
+                choose, jnp.concatenate(blocks, axis=0), (((0,), (0,)), ((), ())),
+                preferred_element_type=F32,
+            )
+            out_ref[f, p, c] = found
+            if p == 1:
+                out_ref[f, 2, c] = -found
+        places = [(0, 0), (0, 3)] if p == 0 else [(1, 1), (2, 2)]
+        for source, k in places:
+            stores.append(
+                pltpu.make_async_copy(out_ref.at[f, source], out_hbm.at[f, k], sems.at[f, k])
+            )
+            stores[-1].start()
+    for store in stores:
+        store.wait()
 
 
 def exchange_small(outgoing, groups, cap):
@@ -298,6 +320,9 @@
     marks = swap(marks.reshape(2, peers, cap)).reshape(2, units, 2, PACK // 2)
     marks = marks.transpose(1, 3, 0, 2).reshape(units, PACK // 2, 4)
     return jnp.concatenate([rows, jnp.repeat(marks, SEG // 4, axis=2)], axis=1)
+
+
+VM = pl.BlockSpec(memory_space=pltpu.VMEM)
 
 
 def params(mib=24):
@@ -339,15 +364,20 @@
         [r * tile_count + side * tile_half + t for r in range(row_count) for t in range(tile_half)]
         for side in range(2)
     ]
+    swap = [(i, i ^ 1) for i in range(row_count)]
     mirror = [(i, (i + tile_half) % tile_count) for i in range(tile_count)]
     angles = column_angles.reshape(chunks, 1, CHUNK)
+    far_target = lax.ppermute(target, "row", swap)
+    far_weight = lax.ppermute(weight, "row", swap)
+    far_owner = lax.ppermute(tile_owner, "tile", mirror)
+    far_slot = lax.ppermute(face_slot, "tile", mirror)
     cur = currents.reshape(freq_count, comp_count, part_count, rows_dev, tiles, SEG)
     cur = cur.transpose(0, 1, 2, 4, 3, 5).reshape(freq_count, comp_count, part_count, points, SEG)
     copies = pairs if share_v == CHUNK else 1
     plane = pl.pallas_call(
         functools.partial(forward_kernel, columns, rows_dev),
         grid=(1,),
-        in_specs=[whole(angles.shape), pl.BlockSpec(memory_space=pltpu.HBM)],
+        in_specs=[VM, pl.BlockSpec(memory_space=pltpu.HBM)],
         out_specs=whole((copies, 2, chunks, 2, wide, CHUNK)),
         out_shape=jax.ShapeDtypeStruct((copies, 2, chunks, 2, wide, CHUNK), BF),
         scratch_shapes=[
@@ -355,7 +385,7 @@
             pltpu.VMEM((8 * half, 2 * SEG), BF),
             pltpu.VMEM((chunks, 2 * SEG, CHUNK), BF),
             pltpu.VMEM((chunks, 2, half, CHUNK), F32),
-            pltpu.SemaphoreType.DMA(()),
+            pltpu.SemaphoreType.DMA((2, 4)),
         ],
         compiler_params=params(58),
         cost_estimate=cost(4.3e9, 1.6e6),
@@ -367,76 +397,69 @@
         plane = jnp.broadcast_to(plane, (pairs,) + plane.shape[1:])
     plane = plane.reshape(devices, 2, wide, share_v)
 
-    row_angles, owner, slot, plane = lax.optimization_barrier(
-        (row_angles, tile_owner, face_slot, plane)
-    )
+    row_angles, plane = lax.optimization_barrier((row_angles, plane))
     got = lax.all_to_all(plane, BOTH, 0, 0, tiled=True)
     here = lax.axis_index("row")
-    core = here % 2
-    swap = [(i, i ^ 1) for i in range(row_count)]
-    code = owner[:, 0] * points + slot
-    code = jnp.stack([code, lax.ppermute(code, "tile", mirror)], axis=1)
     own_angles = jnp.stack(
         [lax.dynamic_slice_in_dim(row_angles, i * share_u, share_u) for i in (here, here ^ 1)]
     )
-    far_target = lax.ppermute(target, "row", swap)
-    far_weight = lax.ppermute(weight, "row", swap)
     row_table = pl.pallas_call(
         functools.partial(row_kernel, columns, rows_dev),
         grid=(1,),
-        in_specs=[whole((2, share_u))],
+        in_specs=[VM],
         out_specs=whole((2, depth, 2 * share_u)),
         out_shape=jax.ShapeDtypeStruct((2, depth, 2 * share_u), BF),
         compiler_params=params(),
         cost_estimate=cost(1e8, 5e5),
         name="rows",
     )(own_angles)
-
     far_shape = (share_v, share_u)
+    spare = (56 << 20) // (4 * share_v * share_u)
     back_shape = (row_count, 2, tile_half, 2, 2, wide, share_v)
-    power, far_power, back = pl.pallas_call(
+    powers, back = pl.pallas_call(
         middle_kernel,
         grid=(1,),
-        in_specs=[whole((2, depth, 2 * share_u)), whole((devices, 2, wide, share_v))]
-        + [whole(target.shape)] * 4,
-        out_specs=[whole(far_shape), whole(far_shape), whole(back_shape)],
+        in_specs=[VM] * 6,
+        out_specs=[pl.BlockSpec(memory_space=pl.ANY), whole(back_shape)],
         out_shape=[
-            jax.ShapeDtypeStruct(far_shape, F32),
-            jax.ShapeDtypeStruct(far_shape, F32),
+            jax.ShapeDtypeStruct((spare,) + far_shape, F32),
             jax.ShapeDtypeStruct(back_shape, BF),
         ],
+        scratch_shapes=[pltpu.VMEM((2,) + far_shape, F32), pltpu.SemaphoreType.DMA((2,))],
         compiler_params=params(),
         cost_estimate=cost(1.1e9, 5e6),
         name="objective",
     )(row_table, got, target, far_target, weight, far_weight)
 
-    angles, code, back = lax.optimization_barrier((angles, code, back))
+    owner, slot, far_owner, far_slot, angles, powers, back = lax.optimization_barrier(
+        (tile_owner, face_slot, far_owner, far_slot, angles, powers, back)
+    )
+    far_power = lax.ppermute(powers[1], "row", swap)
+    code = jnp.stack(
+        [owner[:, 0] * points + slot, far_owner[:, 0] * points + far_slot], axis=1
+    )
     back = back.reshape(devices, 2, 2, wide, share_v)
     back = lax.all_to_all(back, BOTH, 0, 0, tiled=True)
-    table, choose, mark = pl.pallas_call(
+    table, choose, mark, intensity = pl.pallas_call(
         functools.partial(prepare_kernel, columns, rows_dev, tile_count, cap),
         grid=(1,),
-        in_specs=[whole(angles.shape), whole((points, 2))],
+        in_specs=[VM, VM, pl.BlockSpec((1,) + far_shape, lambda i: (0, 0, 0)), VM],
         out_specs=[
             whole((chunks, 2 * SEG, CHUNK)),
             whole((2, slots, points)),
             whole((units, PACK // 2, SEG)),
+            whole(target.shape),
         ],
         out_shape=[
             jax.ShapeDtypeStruct((chunks, 2 * SEG, CHUNK), BF),
             jax.ShapeDtypeStruct((2, slots, points), BF),
             jax.ShapeDtypeStruct((units, PACK // 2, SEG), BF),
+            jax.ShapeDtypeStruct(target.shape, F32),
         ],
         compiler_params=params(),
         cost_estimate=cost(1e9, 2e6),
         name="prepare",
-    )(angles, code)
-    far_power, mark = lax.optimization_barrier((far_power, mark))
-    far_power = lax.ppermute(far_power, "row", swap)
-    intensity = jnp.where(
-        core == 0, jnp.stack([power, far_power]), jnp.stack([far_power, power])
-    )
-    intensity, mark = lax.optimization_barrier((intensity, mark))
+    )(angles, code, powers, far_power)
 
     back = back.reshape(pairs, 2, tile_count, 2, 2, wide, share_v)
     if share_v != CHUNK:
@@ -445,13 +468,7 @@
     outgoing = pl.pallas_call(
         functools.partial(adjoint_kernel, columns, rows_dev),
         grid=(1,),
-        in_specs=[
-            whole((pairs, 2, chunks, 2, 2, wide, CHUNK)),
-            whole((chunks, 2 * SEG, CHUNK)),
-            whole(angles.shape),
-            whole((2, slots, points)),
-            whole((units, PACK // 2, SEG)),
-        ],
+        in_specs=[VM] * 5,
         out_specs=whole((units, held, SEG)),
         out_shape=jax.ShapeDtypeStruct((units, held, SEG), BF),
         scratch_shapes=[pltpu.VMEM((16 * half, 2 * SEG), F32)],
@@ -468,9 +485,13 @@
     faces = pl.pallas_call(
         faces_kernel,
         grid=(1,),
-        in_specs=[whole((units, held, SEG))],
-        out_specs=whole(out_shape),
+        in_specs=[VM],
+        out_specs=pl.BlockSpec(memory_space=pl.ANY),
         out_shape=jax.ShapeDtypeStruct(out_shape, F32),
+        scratch_shapes=[
+            pltpu.VMEM((freq_count, 3, part_count, points, SEG), F32),
+            pltpu.SemaphoreType.DMA((2, 4)),
+        ],
         compiler_params=params(),
         name="faces",
     )(arrived)

time: 76.2 us -> 74.5 us (0.978)
  other arithmetic: 2.34 us -> 0.03 us
  Pallas kernels: 18.8 us -> 20.6 us
  waiting for transfers between devices: 18.5 us -> 17.5 us
    ppermute x2 -> x3, waiting for transfers between devices: 6.98 us -> 1.71 us  [the longest x1 1.7 us: body(): far_power = lax.ppermute(powers[1], 'row', swap)]
    all_to_all x1, waiting for transfers between devices: 1.23 us -> 5.99 us  [body(): got = lax.all_to_all(plane, BOTH, 0, 0, tiled=True)]
    select_n x1 -> x0, other arithmetic: 2.32 us -> none  [body(): jnp.where(core == 0, jnp.stack([power, far_power]), jnp.stack([far_power,...]
    pallas_call x1, Pallas kernels: 1.26 us -> 3.27 us  [body(): pl.pallas_call(functools.partial(prepare_kernel, columns, rows_dev, tile_...]
    unnamed x22 -> x14, local copies, waits for them, and re-layouts: 2.42 us -> 0.81 us
    squeeze x0 -> x1, local copies, waits for them, and re-layouts: none -> 1.08 us  [body(): far_power = lax.ppermute(powers[1], 'row', swap)]
    ppermute x2 -> x3, starting transfers between devices: 2.81 us -> 3.06 us  [the longest x1 2.74 us: body(): far_owner = lax.ppermute(tile_owner, 'tile', mirror)]
  transfers between devices with their start and end apart: 6 -> 7, of which waited for: 4 -> 3; matrix products, arithmetic and copies ran while one was open for 3% -> 2% of each run, Pallas kernels for 10% -> 18%
where the time goes in v6:
time: 74.5 us; the launch traced here: 74 us
  Pallas kernels  20.6 us (28%)
  blocking collectives  19.1 us (26%)
  waiting for transfers between devices  17.5 us (23%)
  starting transfers between devices  13.7 us (18%)
  local copies, waits for them, and re-layouts  2.1 us (3%)
  between operations  0.94 us (1%)
    all_to_all x1, blocking collectives, body(): lax.all_to_all(outgoing, BOTH, 0, 0, tiled=True, axis_index_groups=half_g...  19.1 us
    all_to_all x1, waiting for transfers between devices, body(): back = lax.all_to_all(back, BOTH, 0, 0, tiled=True)  9.84 us
    all_to_all x1, starting transfers between devices, body(): got = lax.all_to_all(plane, BOTH, 0, 0, tiled=True)  7.28 us
    all_to_all x1, waiting for transfers between devices, body(): got = lax.all_to_all(plane, BOTH, 0, 0, tiled=True)  5.99 us
    pallas_call x1, Pallas kernels, body(): pl.pallas_call(functools.partial(adjoint_kernel, columns, rows_dev), grid...  5.3 us
    pallas_call x1, Pallas kernels, body(): pl.pallas_call(functools.partial(forward_kernel, columns, rows_dev), grid...  5.08 us
    pallas_call x1, Pallas kernels, body(): pl.pallas_call(middle_kernel, grid=(1,), in_specs=[VM] * 6, out_specs=[pl...  3.5 us
    pallas_call x1, Pallas kernels, body(): pl.pallas_call(functools.partial(prepare_kernel, columns, rows_dev, tile_...  3.27 us
  transfers between devices with their start and end apart: 7, of which 3 were waited for; matrix products, arithmetic and copies ran while one was open for 2% of the time, Pallas kernels for 18%

profile of v6, /device:TPU:0, one launch (start us, length us, event | category | flops | bytes accessed | tf_op | source)
XLA Modules:
  0.0 74.0 jit_solution(12027022775573014011)
XLA Ops:
  0.6 0.5 collective-permute-start.2
  1.1 0.1 collective-permute-start.3
  1.2 0.0 copy-start.6
  1.2 0.0 copy-start.5
  1.2 0.0 copy-start.4
  1.2 0.0 copy-start.1
  1.2 5.1 %columns.1 = bf16[2,2,8,2,8,256]{5,4,3,2,1,0:T(8,128)(2,1)} custom-call(s32[8,1,256]{2,1,0:T(1,128)} %bitcast.19, bf16[2,4,2,256,128]{4,3,2,1,0:T(8,128)(2,1)} %bitcast.29), custom_call_target="tpu_custom_call" | custom-call | flops 4300000256 | bytes 1600000 | tf_op jit(solution)/shard_map/columns/pallas_call | solution.py:377
  6.3 0.0 copy-start
  6.3 7.3 %all-to-all-start = ((bf16[32,2,8,256]{3,2,1,0:T(8,128)(2,1)}), bf16[32,2,8,256]{3,2,1,0:T(8,128)(2,1)S(1)}, u32[]{:S(2)}, u32[]{:S(2)}) async-start(bf16[32,2,8,256]{3,2,1,0:T(8,128)(2,1)} %bitcast.22), calls=%async_computation | async-start | bytes 524288 | tf_op jit(solution)/shard_map/all_to_all | solution.py:401
  13.6 0.0 copy-done.6
  13.6 2.7 %collective-permute-start = (s32[256,1]{0,1:T(1,128)S(1)}, s32[256,1]{0,1:T(1,128)S(1)}, u32[]{:S(2)}, u32[]{:S(2)}) collective-permute-start(s32[256,1]{0,1:T(1,128)S(1)} %copy-done.6), channel_id=1, source_target_pairs={{0,4},{1,5},{2,6},{3,7},{4,0},{5,1},{6,2},{7,3},{8,12},{9,13},{10,... | collective-permute-start | bytes 3080 | tf_op jit(solution)/shard_map/ppermute | solution.py:372
  16.4 0.0 copy-done.5
  16.4 0.3 collective-permute-start.1
  16.6 0.0 copy-done.4
  16.6 0.1 fusion
  16.7 1.6 %rows.1.table = bf16[2,256,1024]{2,1,0:T(8,128)(2,1)S(1)} custom-call(s32[2,512]{1,0:T(2,128)S(1)} %pad_add_fusion.row_ref), custom_call_target="tpu_custom_call" | custom-call | flops 100000000 | bytes 500000 | tf_op jit(solution)/shard_map/rows/pallas_call | solution.py:406
  18.3 6.0 %all-to-all-done.got_ref = bf16[32,2,8,256]{3,2,1,0:T(8,128)(2,1)S(1)} async-done(((bf16[32,2,8,256]{3,2,1,0:T(8,128)(2,1)}), bf16[32,2,8,256]{3,2,1,0:T(8,128)(2,1)S(1)}, u32[]{:S(2)}, u32[]{:S(2)}) %all-to-all-start) | async-done | bytes 262176 | tf_op jit(solution)/shard_map/all_to_all | solution.py:401
  24.3 0.0 collective-permute-done.2.far_target_ref
  24.3 0.0 collective-permute-done.3.far_weight_ref
  24.3 0.0 copy-done.1
  24.3 0.0 copy-done
  24.3 3.5 %objective.1 = (f32[112,256,512]{2,1,0:T(8,128)}, bf16[4,2,4,2,2,8,256]{6,5,4,3,2,1,0:T(8,128)(2,1)S(1)}) custom-call(bf16[2,256,1024]{2,1,0:T(8,128)(2,1)S(1)} %rows.1.table, bf16[32,2,8,256]{3,2,1,0:T(8,128)(2,1)S(1)} %all-to-all-done.got_ref, f32[2,256,512]{2,1,0:T(8,128)S(1)} %copy-done, f32[2,256,512]{2,1,0:T(8,128)} %collective-permute-done.2.far_target_ref, ...), custom_call_target="tpu_custom_call" | custom-call | flops 1100000000 | bytes 5000000 | tf_op jit(solution)/shard_map/objective/pallas_call | solution.py:419
  27.8 0.0 copy-start.2
  27.8 0.8 %copy-done.2 = bf16[4,2,4,2,2,8,256]{6,5,4,3,2,1,0:T(8,128)(2,1)} copy-done((bf16[4,2,4,2,2,8,256]{6,5,4,3,2,1,0:T(8,128)(2,1)}, bf16[4,2,4,2,2,8,256]{6,5,4,3,2,1,0:T(8,128)(2,1)S(1)}, u32[]{:S(2)}) %copy-start.2) | copy-done | bytes 524312
  28.6 0.0 copy-start.3
  28.6 0.0 collective-permute-done
  28.6 0.0 collective-permute-done.1
  28.6 2.8 %all-to-all-start.1 = ((bf16[32,2,2,8,256]{4,3,2,1,0:T(8,128)(2,1)}), bf16[32,2,2,8,256]{4,3,2,1,0:T(8,128)(2,1)S(1)}, u32[]{:S(2)}, u32[]{:S(2)}) async-start(bf16[32,2,2,8,256]{4,3,2,1,0:T(8,128)(2,1)} %bitcast.17), calls=%async_computation.1 | async-start | bytes 1048576 | tf_op jit(solution)/shard_map/all_to_all | solution.py:442
  31.4 1.1 %slice_bitcast_fusion = f32[256,512]{1,0:T(8,128)S(1)} fusion(f32[112,256,512]{2,1,0:T(8,128)} %get-tuple-element.26.power_ref), kind=kLoop, calls=%fused_computation | loop fusion | bytes 1048576 | tf_op jit(solution)/shard_map/squeeze | solution.py:437
  32.5 0.1 collective-permute-start.4
  32.7 0.1 copy.14.code_ref
  32.8 1.7 %collective-permute-done.4.far_power_ref = f32[256,512]{1,0:T(8,128)S(1)} collective-permute-done((f32[256,512]{1,0:T(8,128)S(1)}, f32[256,512]{1,0:T(8,128)S(1)}, u32[]{:S(2)}, u32[]{:S(2)}) %collective-permute-start.4) | collective-permute-done | bytes 524320 | tf_op jit(solution)/shard_map/ppermute | solution.py:437
  34.5 0.0 copy-done.3
  34.5 3.3 %prepare.1 = (bf16[8,256,256]{2,1,0:T(8,128)(2,1)S(1)}, bf16[2,256,256]{2,1,0:T(8,128)(2,1)S(1)}, bf16[16,8,128]{2,1,0:T(8,128)(2,1)S(1)}, f32[2,256,512]{2,1,0:T(8,128)}) custom-call(s32[8,1,256]{2,1,0:T(1,128)S(1)} %bitcast.20, s32[256,2]{1,0:T(8,128)S(1)} %copy.14.code_ref, f32[112,256,512]{2,1,0:T(8,128)} %get-tuple-element.26.power_ref, ...), custom_call_target="tpu_custom_call" | custom-call | flops 1000000000 | bytes 2000000 | tf_op jit(solution)/shard_map/prepare/pallas_call | solution.py:443
  37.8 9.8 %all-to-all-done.1 = bf16[32,2,2,8,256]{4,3,2,1,0:T(8,128)(2,1)S(1)} async-done(((bf16[32,2,2,8,256]{4,3,2,1,0:T(8,128)(2,1)}), bf16[32,2,2,8,256]{4,3,2,1,0:T(8,128)(2,1)S(1)}, u32[]{:S(2)}, u32[]{:S(2)}) %all-to-all-start.1) | async-done | bytes 524320 | tf_op jit(solution)/shard_map/all_to_all | solution.py:442
  47.6 5.3 %adjoint.1 = bf16[16,264,128]{2,1,0:T(8,128)(2,1)S(1)} custom-call(bf16[2,2,8,2,2,8,256]{6,5,4,3,2,1,0:T(8,128)(2,1)S(1)} %bitcast.18, bf16[8,256,256]{2,1,0:T(8,128)(2,1)S(1)} %get-tuple-element.29.w_ref, s32[8,1,256]{2,1,0:T(1,128)S(1)} %bitcast.21, bf16[2,256,256]{2,1,0:T(8,128)(2,1)S(1)} %get-tuple-element.30.choose_ref, ...), custom_call_target="tpu_custom_call" | custom-call | flops 4300000256 | bytes 4000000 | tf_op jit(solution)/shard_map/adjoint/pallas_call | solution.py:468
  52.9 19.1 %all_to_all.15.got_ref = bf16[16,264,128]{2,1,0:T(8,128)(2,1)S(1)} all-to-all(bf16[16,264,128]{2,1,0:T(8,128)(2,1)S(1)} %adjoint.1), channel_id=1, replica_groups={{0,1,2,3,8,9,10,11,16,17,18,19,24,25,26,27},{4,5,6,7,12,13,14,15,20,21,..., dimensions={0} | all-to-all | bytes 2162688 | tf_op jit(solution)/shard_map/all_to_all | solution.py:481
  72.0 1.9 %faces.1 = f32[2,4,2,256,128]{4,3,2,1,0:T(8,128)} custom-call(bf16[16,264,128]{2,1,0:T(8,128)(2,1)S(1)} %all_to_all.15.got_ref), custom_call_target="tpu_custom_call" | custom-call | tf_op jit(solution)/shard_map/faces/pallas_call | solution.py:485
  (5 shorter events, 0.0 us)
Async XLA Ops:
  0.6 23.7 %collective-permute-start.2 = (f32[2,256,512]{2,1,0:T(8,128)}, f32[2,256,512]{2,1,0:T(8,128)}, u32[]{:S(2)}, u32[]{:S(2)}) collective-permute-start(f32[2,256,512]{2,1,0:T(8,128)} %target_ref.1), channel_id=1, source_target_pairs={{0,8},{8,0},{16,24},{24,16},{1,9},{9,1},{17,25},{25,17},{2,10},{10... | collective-permute-start | bytes 3145736 | tf_op jit(solution)/shard_map/ppermute | solution.py:370
  1.1 23.2 %collective-permute-start.3 = (f32[2,256,512]{2,1,0:T(8,128)}, f32[2,256,512]{2,1,0:T(8,128)}, u32[]{:S(2)}, u32[]{:S(2)}) collective-permute-start(f32[2,256,512]{2,1,0:T(8,128)} %weight_ref.1), channel_id=1, source_target_pairs={{0,8},{8,0},{16,24},{24,16},{1,9},{9,1},{17,25},{25,17},{2,10},{10... | collective-permute-start | bytes 3145736 | tf_op jit(solution)/shard_map/ppermute | solution.py:371
  1.2 12.4 %copy-start.6 = (s32[256,1]{0,1:T(1,128)S(1)}, s32[256,1]{0,1:T(1,128)}, u32[]{:S(2)}) copy-start(s32[256,1]{0,1:T(1,128)} %param.12) | copy-start | bytes 3076
  1.2 15.1 %copy-start.5 = (s32[256]{0:T(256)S(1)}, s32[256]{0:T(256)}, u32[]{:S(2)}) copy-start(s32[256]{0:T(256)} %param.13) | copy-start | bytes 3076
  1.2 15.4 %copy-start.4 = (s32[2048]{0:T(1024)S(1)}, s32[2048]{0:T(1024)}, u32[]{:S(2)}) copy-start(s32[2048]{0:T(1024)} %param.8) | copy-start | bytes 24580
  1.2 23.1 %copy-start.1 = (f32[2,256,512]{2,1,0:T(8,128)S(1)}, f32[2,256,512]{2,1,0:T(8,128)}, u32[]{:S(2)}) copy-start(f32[2,256,512]{2,1,0:T(8,128)} %weight_ref.1) | copy-start | bytes 3145732
  6.3 18.0 %copy-start = (f32[2,256,512]{2,1,0:T(8,128)S(1)}, f32[2,256,512]{2,1,0:T(8,128)}, u32[]{:S(2)}) copy-start(f32[2,256,512]{2,1,0:T(8,128)} %target_ref.1) | copy-start | bytes 3145732
  6.3 18.0 %all-to-all-start = ((bf16[32,2,8,256]{3,2,1,0:T(8,128)(2,1)}), bf16[32,2,8,256]{3,2,1,0:T(8,128)(2,1)S(1)}, u32[]{:S(2)}, u32[]{:S(2)}) async-start(bf16[32,2,8,256]{3,2,1,0:T(8,128)(2,1)} %bitcast.22), calls=%async_computation | async-start | bytes 524288 | tf_op jit(solution)/shard_map/all_to_all | solution.py:401
  13.6 15.0 %collective-permute-start = (s32[256,1]{0,1:T(1,128)S(1)}, s32[256,1]{0,1:T(1,128)S(1)}, u32[]{:S(2)}, u32[]{:S(2)}) collective-permute-start(s32[256,1]{0,1:T(1,128)S(1)} %copy-done.6), channel_id=1, source_target_pairs={{0,4},{1,5},{2,6},{3,7},{4,0},{5,1},{6,2},{7,3},{8,12},{9,13},{10,... | collective-permute-start | bytes 3080 | tf_op jit(solution)/shard_map/ppermute | solution.py:372
  16.4 12.2 %collective-permute-start.1 = (s32[256]{0:T(256)S(1)}, s32[256]{0:T(256)S(1)}, u32[]{:S(2)}, u32[]{:S(2)}) collective-permute-start(s32[256]{0:T(256)S(1)} %copy-done.5), channel_id=1, source_target_pairs={{0,4},{1,5},{2,6},{3,7},{4,0},{5,1},{6,2},{7,3},{8,12},{9,13},{10,... | collective-permute-start | bytes 3080 | tf_op jit(solution)/shard_map/ppermute | solution.py:373
  27.8 0.8 %copy-start.2 = (bf16[4,2,4,2,2,8,256]{6,5,4,3,2,1,0:T(8,128)(2,1)}, bf16[4,2,4,2,2,8,256]{6,5,4,3,2,1,0:T(8,128)(2,1)S(1)}, u32[]{:S(2)}) copy-start(bf16[4,2,4,2,2,8,256]{6,5,4,3,2,1,0:T(8,128)(2,1)S(1)} %get-tuple-element.28) | copy-start | bytes 1572868
  28.6 5.9 %copy-start.3 = (s32[2048]{0:T(1024)S(1)}, s32[2048]{0:T(1024)}, u32[]{:S(2)}) copy-start(s32[2048]{0:T(1024)} %param.9) | copy-start | bytes 24580
  28.6 19.0 %all-to-all-start.1 = ((bf16[32,2,2,8,256]{4,3,2,1,0:T(8,128)(2,1)}), bf16[32,2,2,8,256]{4,3,2,1,0:T(8,128)(2,1)S(1)}, u32[]{:S(2)}, u32[]{:S(2)}) async-start(bf16[32,2,2,8,256]{4,3,2,1,0:T(8,128)(2,1)} %bitcast.17), calls=%async_computation.1 | async-start | bytes 1048576 | tf_op jit(solution)/shard_map/all_to_all | solution.py:442
  32.5 2.0 %collective-permute-start.4 = (f32[256,512]{1,0:T(8,128)S(1)}, f32[256,512]{1,0:T(8,128)S(1)}, u32[]{:S(2)}, u32[]{:S(2)}) collective-permute-start(f32[256,512]{1,0:T(8,128)S(1)} %slice_bitcast_fusion), channel_id=1, source_target_pairs={{0,8},{8,0},{16,24},{24,16},{1,9},{9,1},{17,25},{25,17},{2,10},{10... | collective-permute-start | bytes 1572872 | tf_op jit(solution)/shard_map/ppermute | solution.py:437

commit v7 on v6

--- a/solution.py
+++ b/solution.py
@@ -157,8 +157,8 @@
     point = iota((points, points), 1)
     point = (point % rows_dev) * segs + (point // rows_dev)
     source = iota((points, points), 0)
-    lane = iota((PACK // 2, SEG), 1) // (SEG // 4)
-    marked = jnp.zeros((units, PACK // 2, SEG), jnp.int32)
+    spot = iota((slots, SEG), 1) - iota((slots, SEG), 0) % PACK
+    marked = jnp.zeros((slots, SEG), jnp.int32)
     for side in range(2):
         code_col = code_ref[:, side:side + 1]
         code_row = jnp.sum(jnp.where(source == point, code_col, 0), axis=0, keepdims=True)
@@ -171,27 +171,32 @@
         hit = iota((slots, points), 0) == place
         choose_ref[side] = jnp.where(hit, 1.0, 0.0).astype(BF)
         marks = jnp.sum(jnp.where(hit, code_row % points + 1, 0), axis=1, keepdims=True)
-        marks = jnp.broadcast_to(marks, (slots, SEG)).reshape(units, 2, PACK // 2, SEG)
-        for part in range(2):
-            marked = jnp.where(lane == 2 * side + part, marks[:, part], marked)
+        marked = jnp.where(spot == side * PACK, marks, marked)
+    marked = jnp.sum(marked.reshape(units, PACK, SEG), axis=1, keepdims=True)
+    marked = jnp.broadcast_to(marked, mark_ref.shape)
     mark_ref[...] = marked.astype(F32).astype(BF)
 
 
 def middle_kernel(
     table, got_ref, target_ref, far_target_ref, weight_ref, far_weight_ref,
-    power_hbm, back_ref, powers, sems,
+    power_hbm, back_ref, powers, fars, sems,
 ):
     devices, pols, rows, share_v = got_ref.shape
     depth = devices * rows
     share_u = table.shape[2] // 2
     core = lax.axis_index("row") % 2
+    loads = [
+        pltpu.make_async_copy(array.at[core], fars.at[i], sems.at[2 + i])
+        for i, array in enumerate((far_target_ref, far_weight_ref))
+    ]
+    for load in loads:
+        load.start()
     planes = [
         got_ref[:, p].astype(F32).reshape(depth, share_v).astype(BF) for p in range(pols)
     ]
     sums = [None, None]
     stores = []
-    sides = [(target_ref, weight_ref), (far_target_ref, far_weight_ref)]
-    for side, (goal_ref, gain_ref) in enumerate(sides):
+    for side in range(2):
         mixed = [
             lax.dot_general(
                 plane, table[side], (((0,), (0,)), ((), ())), preferred_element_type=F32
@@ -203,7 +208,13 @@
         powers[side] = intensity
         stores.append(pltpu.make_async_copy(powers.at[side], power_hbm.at[side], sems.at[side]))
         stores[-1].start()
-        factor = 4.0 * gain_ref[core] * (intensity - goal_ref[core])
+        if side == 0:
+            goal, gain = target_ref[core], weight_ref[core]
+        else:
+            for load in loads:
+                load.wait()
+            goal, gain = fars[0], fars[1]
+        factor = 4.0 * gain * (intensity - goal)
         factor = jnp.concatenate([factor, factor], axis=1)
         for p in range(pols):
             far_grad = (factor * mixed[p]).astype(BF)
@@ -276,24 +287,30 @@
     units = got_ref.shape[0]
     slots = units * PACK
     marks = got_ref[:, 16 * PACK:, :].astype(F32)
-    hits = []
-    for side in range(2):
-        spots = [(2 * side + part) * (SEG // 4) for part in range(2)]
-        mark = jnp.concatenate([marks[:, :, i:i + 1] for i in spots], axis=1)
-        mark = jnp.broadcast_to(mark.reshape(slots, 1), (slots, faces)).astype(jnp.int32)
-        hits.append(jnp.where(iota((slots, faces), 1) + 1 == mark, 1.0, 0.0).astype(BF))
-    choose = jnp.concatenate(hits, axis=0)
+    fit = SEG // (2 * PACK)
+    rows = []
+    for i in range(0, units, fit):
+        row = marks[i]
+        for j in range(1, fit):
+            row = row + pltpu.roll(marks[i + j], 2 * PACK * j, 1)
+        rows.append(row)
+    label = jnp.concatenate(rows, axis=1).astype(jnp.int32)
+    face = iota((PACK // 2, 2 * slots), 0) + 1
+    choose = jnp.concatenate(
+        [
+            jnp.where(face + i == label, 1.0, 0.0) for i in range(0, faces, PACK // 2)
+        ],
+        axis=0,
+    ).astype(BF)
     stores = []
     for f, p in [(i, j) for i in range(2) for j in range(2)]:
         for c in range(2):
             blocks = []
             for side in range(2):
                 rows = pl.ds((8 * side + 4 * f + 2 * p + c) * PACK, PACK)
-                blocks.append(got_ref[:, rows, :].reshape(slots, SEG))
-            found = lax.dot_general(
-                choose, jnp.concatenate(blocks, axis=0), (((0,), (0,)), ((), ())),
-                preferred_element_type=F32,
-            )
+                blocks.append(got_ref[:, rows, :])
+            block = jnp.concatenate(blocks, axis=1).reshape(2 * slots, SEG)
+            found = jnp.dot(choose, block, preferred_element_type=F32)
             out_ref[f, p, c] = found
             if p == 1:
                 out_ref[f, 2, c] = -found
@@ -316,10 +333,12 @@
     rows = outgoing[:, :16 * PACK].reshape(units, 16, PACK, SEG).transpose(1, 0, 2, 3)
     rows = swap(rows.reshape(16, peers, cap, SEG))
     rows = rows.reshape(16, units, PACK, SEG).transpose(1, 0, 2, 3).reshape(units, 16 * PACK, SEG)
-    marks = outgoing[:, 16 * PACK:, ::SEG // 4].reshape(units, PACK // 2, 2, 2).transpose(2, 0, 3, 1)
-    marks = swap(marks.reshape(2, peers, cap)).reshape(2, units, 2, PACK // 2)
-    marks = marks.transpose(1, 3, 0, 2).reshape(units, PACK // 2, 4)
-    return jnp.concatenate([rows, jnp.repeat(marks, SEG // 4, axis=2)], axis=1)
+    marks = outgoing[:, 16 * PACK, :2 * PACK].reshape(units, 2, PACK).transpose(1, 0, 2)
+    marks = swap(marks.reshape(2, peers, cap)).reshape(2, units, PACK)
+    marks = marks.transpose(1, 0, 2).reshape(units, 1, 2 * PACK)
+    marks = jnp.pad(marks, ((0, 0), (0, 0), (0, SEG - 2 * PACK)))
+    marks = jnp.broadcast_to(marks, (units, PACK // 2, SEG))
+    return jnp.concatenate([rows, marks], axis=1)
 
 
 VM = pl.BlockSpec(memory_space=pltpu.VMEM)
@@ -419,13 +438,17 @@
     powers, back = pl.pallas_call(
         middle_kernel,
         grid=(1,),
-        in_specs=[VM] * 6,
+        in_specs=[VM, VM, VM, pl.BlockSpec(memory_space=pl.ANY), VM, pl.BlockSpec(memory_space=pl.ANY)],
         out_specs=[pl.BlockSpec(memory_space=pl.ANY), whole(back_shape)],
         out_shape=[
             jax.ShapeDtypeStruct((spare,) + far_shape, F32),
             jax.ShapeDtypeStruct(back_shape, BF),
         ],
-        scratch_shapes=[pltpu.VMEM((2,) + far_shape, F32), pltpu.SemaphoreType.DMA((2,))],
+        scratch_shapes=[
+            pltpu.VMEM((2,) + far_shape, F32),
+            pltpu.VMEM((2,) + far_shape, F32),
+            pltpu.SemaphoreType.DMA((4,)),
+        ],
         compiler_params=params(),
         cost_estimate=cost(1.1e9, 5e6),
         name="objective",

time: 74.5 us -> 73 us (0.980)
  Pallas kernels: 20.6 us -> 19.1 us
    pallas_call x1, Pallas kernels: 3.5 us -> 2.13 us  [body(): pl.pallas_call(middle_kernel, grid=(1,), in_specs=[VM, VM, VM, pl.BlockSp...]
  transfers between devices with their start and end apart: 7 -> 7, of which waited for: 3 -> 3; matrix products, arithmetic and copies ran while one was open for 2% -> 2% of each run, Pallas kernels for 18% -> 17%
where the time goes in v7:
time: 73 us; the launch traced here: 72.5 us
  Pallas kernels  19.1 us (26%)
  blocking collectives  19.1 us (26%)
  waiting for transfers between devices  17.5 us (24%)
  starting transfers between devices  13.7 us (19%)
  local copies, waits for them, and re-layouts  2.1 us (3%)
  between operations  0.94 us (1%)
    all_to_all x1, blocking collectives, body(): lax.all_to_all(outgoing, BOTH, 0, 0, tiled=True, axis_index_groups=half_g...  19.1 us
    all_to_all x1, waiting for transfers between devices, body(): back = lax.all_to_all(back, BOTH, 0, 0, tiled=True)  9.82 us
    all_to_all x1, starting transfers between devices, body(): got = lax.all_to_all(plane, BOTH, 0, 0, tiled=True)  7.28 us
    all_to_all x1, waiting for transfers between devices, body(): got = lax.all_to_all(plane, BOTH, 0, 0, tiled=True)  5.99 us
    pallas_call x1, Pallas kernels, body(): pl.pallas_call(functools.partial(adjoint_kernel, columns, rows_dev), grid...  5.29 us
    pallas_call x1, Pallas kernels, body(): pl.pallas_call(functools.partial(forward_kernel, columns, rows_dev), grid...  5.08 us
    pallas_call x1, Pallas kernels, body(): pl.pallas_call(functools.partial(prepare_kernel, columns, rows_dev, tile_...  3.29 us
    all_to_all x1, starting transfers between devices, body(): back = lax.all_to_all(back, BOTH, 0, 0, tiled=True)  2.8 us
  transfers between devices with their start and end apart: 7, of which 3 were waited for; matrix products, arithmetic and copies ran while one was open for 2% of the time, Pallas kernels for 17%

profile of v7, /device:TPU:0, one launch (start us, length us, event | category | flops | bytes accessed | tf_op | source)
XLA Modules:
  0.0 72.5 jit_solution(18163449675254446165)
XLA Ops:
  0.6 0.5 collective-permute-start.2
  1.1 0.1 collective-permute-start.3
  1.2 0.0 copy-start.6
  1.2 0.0 copy-start.5
  1.2 0.0 copy-start.4
  1.2 0.0 copy-start.1
  1.2 5.1 %columns.1 = bf16[2,2,8,2,8,256]{5,4,3,2,1,0:T(8,128)(2,1)} custom-call(s32[8,1,256]{2,1,0:T(1,128)} %bitcast.19, bf16[2,4,2,256,128]{4,3,2,1,0:T(8,128)(2,1)} %bitcast.29), custom_call_target="tpu_custom_call" | custom-call | flops 4300000256 | bytes 1600000 | tf_op jit(solution)/shard_map/columns/pallas_call | solution.py:396
  6.3 0.0 copy-start
  6.3 7.3 %all-to-all-start = ((bf16[32,2,8,256]{3,2,1,0:T(8,128)(2,1)}), bf16[32,2,8,256]{3,2,1,0:T(8,128)(2,1)S(1)}, u32[]{:S(2)}, u32[]{:S(2)}) async-start(bf16[32,2,8,256]{3,2,1,0:T(8,128)(2,1)} %bitcast.22), calls=%async_computation | async-start | bytes 524288 | tf_op jit(solution)/shard_map/all_to_all | solution.py:420
  13.6 0.0 copy-done.6
  13.6 2.7 %collective-permute-start = (s32[256,1]{0,1:T(1,128)S(1)}, s32[256,1]{0,1:T(1,128)S(1)}, u32[]{:S(2)}, u32[]{:S(2)}) collective-permute-start(s32[256,1]{0,1:T(1,128)S(1)} %copy-done.6), channel_id=1, source_target_pairs={{0,4},{1,5},{2,6},{3,7},{4,0},{5,1},{6,2},{7,3},{8,12},{9,13},{10,... | collective-permute-start | bytes 3080 | tf_op jit(solution)/shard_map/ppermute | solution.py:391
  16.4 0.0 copy-done.5
  16.4 0.3 collective-permute-start.1
  16.6 0.0 copy-done.4
  16.6 0.1 fusion
  16.7 1.6 %rows.1.table = bf16[2,256,1024]{2,1,0:T(8,128)(2,1)S(1)} custom-call(s32[2,512]{1,0:T(2,128)S(1)} %pad_add_fusion.row_ref), custom_call_target="tpu_custom_call" | custom-call | flops 100000000 | bytes 500000 | tf_op jit(solution)/shard_map/rows/pallas_call | solution.py:425
  18.3 6.0 %all-to-all-done.got_ref = bf16[32,2,8,256]{3,2,1,0:T(8,128)(2,1)S(1)} async-done(((bf16[32,2,8,256]{3,2,1,0:T(8,128)(2,1)}), bf16[32,2,8,256]{3,2,1,0:T(8,128)(2,1)S(1)}, u32[]{:S(2)}, u32[]{:S(2)}) %all-to-all-start) | async-done | bytes 262176 | tf_op jit(solution)/shard_map/all_to_all | solution.py:420
  24.3 0.0 collective-permute-done.2.far_target_ref
  24.3 0.0 collective-permute-done.3.far_weight_ref
  24.3 0.0 copy-done.1
  24.3 0.0 copy-done
  24.3 2.1 %objective.1 = (f32[112,256,512]{2,1,0:T(8,128)}, bf16[4,2,4,2,2,8,256]{6,5,4,3,2,1,0:T(8,128)(2,1)S(1)}) custom-call(bf16[2,256,1024]{2,1,0:T(8,128)(2,1)S(1)} %rows.1.table, bf16[32,2,8,256]{3,2,1,0:T(8,128)(2,1)S(1)} %all-to-all-done.got_ref, f32[2,256,512]{2,1,0:T(8,128)S(1)} %copy-done, f32[2,256,512]{2,1,0:T(8,128)} %collective-permute-done.2.far_target_ref, ...), custom_call_target="tpu_custom_call" | custom-call | flops 1100000000 | bytes 5000000 | tf_op jit(solution)/shard_map/objective/pallas_call | solution.py:438
  26.5 0.0 copy-start.2
  26.5 0.8 %copy-done.2 = bf16[4,2,4,2,2,8,256]{6,5,4,3,2,1,0:T(8,128)(2,1)} copy-done((bf16[4,2,4,2,2,8,256]{6,5,4,3,2,1,0:T(8,128)(2,1)}, bf16[4,2,4,2,2,8,256]{6,5,4,3,2,1,0:T(8,128)(2,1)S(1)}, u32[]{:S(2)}) %copy-start.2) | copy-done | bytes 524312
  27.3 0.0 copy-start.3
  27.3 0.0 collective-permute-done
  27.3 0.0 collective-permute-done.1
  27.3 2.8 %all-to-all-start.1 = ((bf16[32,2,2,8,256]{4,3,2,1,0:T(8,128)(2,1)}), bf16[32,2,2,8,256]{4,3,2,1,0:T(8,128)(2,1)S(1)}, u32[]{:S(2)}, u32[]{:S(2)}) async-start(bf16[32,2,2,8,256]{4,3,2,1,0:T(8,128)(2,1)} %bitcast.17), calls=%async_computation.1 | async-start | bytes 1048576 | tf_op jit(solution)/shard_map/all_to_all | solution.py:465
  30.1 1.1 %slice_bitcast_fusion = f32[256,512]{1,0:T(8,128)S(1)} fusion(f32[112,256,512]{2,1,0:T(8,128)} %get-tuple-element.26.power_ref), kind=kLoop, calls=%fused_computation | loop fusion | bytes 1048576 | tf_op jit(solution)/shard_map/squeeze | solution.py:460
  31.2 0.1 collective-permute-start.4
  31.3 0.1 copy.14.code_ref
  31.4 1.7 %collective-permute-done.4.far_power_ref = f32[256,512]{1,0:T(8,128)S(1)} collective-permute-done((f32[256,512]{1,0:T(8,128)S(1)}, f32[256,512]{1,0:T(8,128)S(1)}, u32[]{:S(2)}, u32[]{:S(2)}) %collective-permute-start.4) | collective-permute-done | bytes 524320 | tf_op jit(solution)/shard_map/ppermute | solution.py:460
  33.1 0.0 copy-done.3
  33.1 3.3 %prepare.1 = (bf16[8,256,256]{2,1,0:T(8,128)(2,1)S(1)}, bf16[2,256,256]{2,1,0:T(8,128)(2,1)S(1)}, bf16[16,8,128]{2,1,0:T(8,128)(2,1)S(1)}, f32[2,256,512]{2,1,0:T(8,128)}) custom-call(s32[8,1,256]{2,1,0:T(1,128)S(1)} %bitcast.20, s32[256,2]{1,0:T(8,128)S(1)} %copy.14.code_ref, f32[112,256,512]{2,1,0:T(8,128)} %get-tuple-element.26.power_ref, ...), custom_call_target="tpu_custom_call" | custom-call | flops 1000000000 | bytes 2000000 | tf_op jit(solution)/shard_map/prepare/pallas_call | solution.py:466
  36.4 9.8 %all-to-all-done.1 = bf16[32,2,2,8,256]{4,3,2,1,0:T(8,128)(2,1)S(1)} async-done(((bf16[32,2,2,8,256]{4,3,2,1,0:T(8,128)(2,1)}), bf16[32,2,2,8,256]{4,3,2,1,0:T(8,128)(2,1)S(1)}, u32[]{:S(2)}, u32[]{:S(2)}) %all-to-all-start.1) | async-done | bytes 524320 | tf_op jit(solution)/shard_map/all_to_all | solution.py:465
  46.2 5.3 %adjoint.1 = bf16[16,264,128]{2,1,0:T(8,128)(2,1)S(1)} custom-call(bf16[2,2,8,2,2,8,256]{6,5,4,3,2,1,0:T(8,128)(2,1)S(1)} %bitcast.18, bf16[8,256,256]{2,1,0:T(8,128)(2,1)S(1)} %get-tuple-element.29.w_ref, s32[8,1,256]{2,1,0:T(1,128)S(1)} %bitcast.21, bf16[2,256,256]{2,1,0:T(8,128)(2,1)S(1)} %get-tuple-element.30.choose_ref, ...), custom_call_target="tpu_custom_call" | custom-call | flops 4300000256 | bytes 4000000 | tf_op jit(solution)/shard_map/adjoint/pallas_call | solution.py:491
  51.5 19.1 %all_to_all.15.got_ref = bf16[16,264,128]{2,1,0:T(8,128)(2,1)S(1)} all-to-all(bf16[16,264,128]{2,1,0:T(8,128)(2,1)S(1)} %adjoint.1), channel_id=1, replica_groups={{0,1,2,3,8,9,10,11,16,17,18,19,24,25,26,27},{4,5,6,7,12,13,14,15,20,21,..., dimensions={0} | all-to-all | bytes 2162688 | tf_op jit(solution)/shard_map/all_to_all | solution.py:504
  70.6 1.7 %faces.1 = f32[2,4,2,256,128]{4,3,2,1,0:T(8,128)} custom-call(bf16[16,264,128]{2,1,0:T(8,128)(2,1)S(1)} %all_to_all.15.got_ref), custom_call_target="tpu_custom_call" | custom-call | tf_op jit(solution)/shard_map/faces/pallas_call | solution.py:508
  (5 shorter events, 0.0 us)
Async XLA Ops:
  0.6 23.7 %collective-permute-start.2 = (f32[2,256,512]{2,1,0:T(8,128)}, f32[2,256,512]{2,1,0:T(8,128)}, u32[]{:S(2)}, u32[]{:S(2)}) collective-permute-start(f32[2,256,512]{2,1,0:T(8,128)} %target_ref.1), channel_id=1, source_target_pairs={{0,8},{8,0},{16,24},{24,16},{1,9},{9,1},{17,25},{25,17},{2,10},{10... | collective-permute-start | bytes 3145736 | tf_op jit(solution)/shard_map/ppermute | solution.py:389
  1.1 23.2 %collective-permute-start.3 = (f32[2,256,512]{2,1,0:T(8,128)}, f32[2,256,512]{2,1,0:T(8,128)}, u32[]{:S(2)}, u32[]{:S(2)}) collective-permute-start(f32[2,256,512]{2,1,0:T(8,128)} %weight_ref.1), channel_id=1, source_target_pairs={{0,8},{8,0},{16,24},{24,16},{1,9},{9,1},{17,25},{25,17},{2,10},{10... | collective-permute-start | bytes 3145736 | tf_op jit(solution)/shard_map/ppermute | solution.py:390
  1.2 12.4 %copy-start.6 = (s32[256,1]{0,1:T(1,128)S(1)}, s32[256,1]{0,1:T(1,128)}, u32[]{:S(2)}) copy-start(s32[256,1]{0,1:T(1,128)} %param.12) | copy-start | bytes 3076
  1.2 15.1 %copy-start.5 = (s32[256]{0:T(256)S(1)}, s32[256]{0:T(256)}, u32[]{:S(2)}) copy-start(s32[256]{0:T(256)} %param.13) | copy-start | bytes 3076
  1.2 15.4 %copy-start.4 = (s32[2048]{0:T(1024)S(1)}, s32[2048]{0:T(1024)}, u32[]{:S(2)}) copy-start(s32[2048]{0:T(1024)} %param.8) | copy-start | bytes 24580
  1.2 23.1 %copy-start.1 = (f32[2,256,512]{2,1,0:T(8,128)S(1)}, f32[2,256,512]{2,1,0:T(8,128)}, u32[]{:S(2)}) copy-start(f32[2,256,512]{2,1,0:T(8,128)} %weight_ref.1) | copy-start | bytes 3145732
  6.3 18.0 %copy-start = (f32[2,256,512]{2,1,0:T(8,128)S(1)}, f32[2,256,512]{2,1,0:T(8,128)}, u32[]{:S(2)}) copy-start(f32[2,256,512]{2,1,0:T(8,128)} %target_ref.1) | copy-start | bytes 3145732
  6.3 18.0 %all-to-all-start = ((bf16[32,2,8,256]{3,2,1,0:T(8,128)(2,1)}), bf16[32,2,8,256]{3,2,1,0:T(8,128)(2,1)S(1)}, u32[]{:S(2)}, u32[]{:S(2)}) async-start(bf16[32,2,8,256]{3,2,1,0:T(8,128)(2,1)} %bitcast.22), calls=%async_computation | async-start | bytes 524288 | tf_op jit(solution)/shard_map/all_to_all | solution.py:420
  13.6 13.6 %collective-permute-start = (s32[256,1]{0,1:T(1,128)S(1)}, s32[256,1]{0,1:T(1,128)S(1)}, u32[]{:S(2)}, u32[]{:S(2)}) collective-permute-start(s32[256,1]{0,1:T(1,128)S(1)} %copy-done.6), channel_id=1, source_target_pairs={{0,4},{1,5},{2,6},{3,7},{4,0},{5,1},{6,2},{7,3},{8,12},{9,13},{10,... | collective-permute-start | bytes 3080 | tf_op jit(solution)/shard_map/ppermute | solution.py:391
  16.4 10.9 %collective-permute-start.1 = (s32[256]{0:T(256)S(1)}, s32[256]{0:T(256)S(1)}, u32[]{:S(2)}, u32[]{:S(2)}) collective-permute-start(s32[256]{0:T(256)S(1)} %copy-done.5), channel_id=1, source_target_pairs={{0,4},{1,5},{2,6},{3,7},{4,0},{5,1},{6,2},{7,3},{8,12},{9,13},{10,... | collective-permute-start | bytes 3080 | tf_op jit(solution)/shard_map/ppermute | solution.py:392
  26.5 0.8 %copy-start.2 = (bf16[4,2,4,2,2,8,256]{6,5,4,3,2,1,0:T(8,128)(2,1)}, bf16[4,2,4,2,2,8,256]{6,5,4,3,2,1,0:T(8,128)(2,1)S(1)}, u32[]{:S(2)}) copy-start(bf16[4,2,4,2,2,8,256]{6,5,4,3,2,1,0:T(8,128)(2,1)S(1)} %get-tuple-element.28) | copy-start | bytes 1572868
  27.3 5.9 %copy-start.3 = (s32[2048]{0:T(1024)S(1)}, s32[2048]{0:T(1024)}, u32[]{:S(2)}) copy-start(s32[2048]{0:T(1024)} %param.9) | copy-start | bytes 24580
  27.3 19.0 %all-to-all-start.1 = ((bf16[32,2,2,8,256]{4,3,2,1,0:T(8,128)(2,1)}), bf16[32,2,2,8,256]{4,3,2,1,0:T(8,128)(2,1)S(1)}, u32[]{:S(2)}, u32[]{:S(2)}) async-start(bf16[32,2,2,8,256]{4,3,2,1,0:T(8,128)(2,1)} %bitcast.17), calls=%async_computation.1 | async-start | bytes 1048576 | tf_op jit(solution)/shard_map/all_to_all | solution.py:465
  31.2 2.0 %collective-permute-start.4 = (f32[256,512]{1,0:T(8,128)S(1)}, f32[256,512]{1,0:T(8,128)S(1)}, u32[]{:S(2)}, u32[]{:S(2)}) collective-permute-start(f32[256,512]{1,0:T(8,128)S(1)} %slice_bitcast_fusion), channel_id=1, source_target_pairs={{0,8},{8,0},{16,24},{24,16},{1,9},{9,1},{17,25},{25,17},{2,10},{10... | collective-permute-start | bytes 1572872 | tf_op jit(solution)/shard_map/ppermute | solution.py:460

commit v8 on v7

--- a/solution.py
+++ b/solution.py
@@ -259,26 +259,27 @@
             total[...] = found
         else:
             total[...] += found
-    for side, fp in [(i, j) for i in range(2) for j in range(4)]:
-        start = (4 * side + fp) * points
-        real = total[start:start + points, :]
-        imag = total[8 * points + start:9 * points + start, :]
-        real_cos, real_sin, imag_cos, imag_sin = (
-            real[:, :SEG], real[:, SEG:], imag[:, :SEG], imag[:, SEG:]
-        )
-        left = [
-            mirrored((real_cos + imag_sin).astype(BF)).astype(BF),
-            mirrored((imag_cos - real_sin).astype(BF)).astype(BF),
-        ]
-        right = [(real_cos - imag_sin).astype(BF), (imag_cos + real_sin).astype(BF)]
+    for side in range(2):
+        left, right = [], []
+        for fp in range(4):
+            start = (4 * side + fp) * points
+            real = total[start:start + points, :]
+            imag = total[8 * points + start:9 * points + start, :]
+            real_cos, real_sin, imag_cos, imag_sin = (
+                real[:, :SEG], real[:, SEG:], imag[:, :SEG], imag[:, SEG:]
+            )
+            left += [(real_cos + imag_sin).astype(BF), (imag_cos - real_sin).astype(BF)]
+            right += [(real_cos - imag_sin).astype(BF), (imag_cos + real_sin).astype(BF)]
+        left = mirrored(jnp.concatenate(left, axis=0)).astype(BF)
+        left = [left[i * points:(i + 1) * points] for i in range(8)]
         block = jnp.concatenate(
             [jnp.concatenate(left, axis=1), jnp.concatenate(right, axis=1)], axis=0
         )
         sent = jnp.dot(choose_ref[side], block, preferred_element_type=F32).astype(BF)
-        sent = sent.reshape(units, PACK, 2 * SEG)
-        for c in range(2):
-            rows = pl.ds((8 * side + 2 * fp + c) * PACK, PACK)
-            out_ref[:, rows, :] = sent[:, :, c * SEG:(c + 1) * SEG]
+        sent = sent.reshape(units, PACK, 8 * SEG)
+        for i in range(8):
+            rows = pl.ds((8 * side + i) * PACK, PACK)
+            out_ref[:, rows, :] = sent[:, :, i * SEG:(i + 1) * SEG]
     out_ref[:, 16 * PACK:, :] = mark_ref[...]
 
 
@@ -386,8 +387,6 @@
     swap = [(i, i ^ 1) for i in range(row_count)]
     mirror = [(i, (i + tile_half) % tile_count) for i in range(tile_count)]
     angles = column_angles.reshape(chunks, 1, CHUNK)
-    far_target = lax.ppermute(target, "row", swap)
-    far_weight = lax.ppermute(weight, "row", swap)
     far_owner = lax.ppermute(tile_owner, "tile", mirror)
     far_slot = lax.ppermute(face_slot, "tile", mirror)
     cur = currents.reshape(freq_count, comp_count, part_count, rows_dev, tiles, SEG)
@@ -416,7 +415,9 @@
         plane = jnp.broadcast_to(plane, (pairs,) + plane.shape[1:])
     plane = plane.reshape(devices, 2, wide, share_v)
 
-    row_angles, plane = lax.optimization_barrier((row_angles, plane))
+    row_angles, aim, gain, plane = lax.optimization_barrier((row_angles, target, weight, plane))
+    far_target = lax.ppermute(aim, "row", swap)
+    far_weight = lax.ppermute(gain, "row", swap)
     got = lax.all_to_all(plane, BOTH, 0, 0, tiled=True)
     here = lax.axis_index("row")
     own_angles = jnp.stack(

time: 73 us -> 71.9 us (0.985)
  Pallas kernels: 19.1 us -> 18.1 us
    pallas_call x1, Pallas kernels: 5.29 us -> 4.21 us  [body(): pl.pallas_call(functools.partial(adjoint_kernel, columns, rows_dev), grid...]
  transfers between devices with their start and end apart: 7 -> 7, of which waited for: 3 -> 3; matrix products, arithmetic and copies ran while one was open for 2% -> 2% of each run, Pallas kernels for 17% -> 10%
where the time goes in v8:
time: 71.9 us; the launch traced here: 71.5 us
  blocking collectives  19.1 us (27%)
  Pallas kernels  18.1 us (25%)
  waiting for transfers between devices  17.5 us (24%)
  starting transfers between devices  13.7 us (19%)
  local copies, waits for them, and re-layouts  2.1 us (3%)
  between operations  0.96 us (1%)
    all_to_all x1, blocking collectives, body(): lax.all_to_all(outgoing, BOTH, 0, 0, tiled=True, axis_index_groups=half_g...  19.1 us
    all_to_all x1, waiting for transfers between devices, body(): back = lax.all_to_all(back, BOTH, 0, 0, tiled=True)  9.82 us
    all_to_all x1, starting transfers between devices, body(): got = lax.all_to_all(plane, BOTH, 0, 0, tiled=True)  7.26 us
    all_to_all x1, waiting for transfers between devices, body(): got = lax.all_to_all(plane, BOTH, 0, 0, tiled=True)  5.99 us
    pallas_call x1, Pallas kernels, body(): pl.pallas_call(functools.partial(forward_kernel, columns, rows_dev), grid...  5.13 us
    pallas_call x1, Pallas kernels, body(): pl.pallas_call(functools.partial(adjoint_kernel, columns, rows_dev), grid...  4.21 us
    pallas_call x1, Pallas kernels, body(): pl.pallas_call(functools.partial(prepare_kernel, columns, rows_dev, tile_...  3.29 us
    all_to_all x1, starting transfers between devices, body(): back = lax.all_to_all(back, BOTH, 0, 0, tiled=True)  2.8 us
  transfers between devices with their start and end apart: 7, of which 3 were waited for; matrix products, arithmetic and copies ran while one was open for 2% of the time, Pallas kernels for 10%

profile of v8, /device:TPU:0, one launch (start us, length us, event | category | flops | bytes accessed | tf_op | source)
XLA Modules:
  0.0 71.5 jit_solution(13126164139528576549)
XLA Ops:
  0.6 0.0 copy-start
  0.6 0.0 copy-start.1
  0.7 0.0 copy-start.6
  0.7 0.0 copy-start.5
  0.7 0.0 copy-start.4
  0.7 5.1 %columns.1 = bf16[2,2,8,2,8,256]{5,4,3,2,1,0:T(8,128)(2,1)} custom-call(s32[8,1,256]{2,1,0:T(1,128)} %bitcast.19, bf16[2,4,2,256,128]{4,3,2,1,0:T(8,128)(2,1)} %bitcast.29), custom_call_target="tpu_custom_call" | custom-call | flops 4300000256 | bytes 1600000 | tf_op jit(solution)/shard_map/columns/pallas_call | solution.py:395
  5.8 0.0 copy-done
  5.8 0.5 collective-permute-start.2
  6.4 0.0 copy-done.1
  6.4 0.1 collective-permute-start.3
  6.4 7.3 %all-to-all-start = ((bf16[32,2,8,256]{3,2,1,0:T(8,128)(2,1)}), bf16[32,2,8,256]{3,2,1,0:T(8,128)(2,1)S(1)}, u32[]{:S(2)}, u32[]{:S(2)}) async-start(bf16[32,2,8,256]{3,2,1,0:T(8,128)(2,1)} %bitcast.22), calls=%async_computation | async-start | bytes 524288 | tf_op jit(solution)/shard_map/all_to_all | solution.py:421
  13.7 0.0 copy-done.6
  13.7 2.7 %collective-permute-start = (s32[256,1]{0,1:T(1,128)S(1)}, s32[256,1]{0,1:T(1,128)S(1)}, u32[]{:S(2)}, u32[]{:S(2)}) collective-permute-start(s32[256,1]{0,1:T(1,128)S(1)} %copy-done.6), channel_id=1, source_target_pairs={{0,4},{1,5},{2,6},{3,7},{4,0},{5,1},{6,2},{7,3},{8,12},{9,13},{10,... | collective-permute-start | bytes 3080 | tf_op jit(solution)/shard_map/ppermute | solution.py:390
  16.5 0.0 copy-done.5
  16.5 0.3 collective-permute-start.1
  16.7 0.0 copy-done.4
  16.7 0.1 fusion
  16.8 1.6 %rows.1.table = bf16[2,256,1024]{2,1,0:T(8,128)(2,1)S(1)} custom-call(s32[2,512]{1,0:T(2,128)S(1)} %pad_add_fusion.row_ref), custom_call_target="tpu_custom_call" | custom-call | flops 100000000 | bytes 500000 | tf_op jit(solution)/shard_map/rows/pallas_call | solution.py:426
  18.4 6.0 %all-to-all-done.got_ref = bf16[32,2,8,256]{3,2,1,0:T(8,128)(2,1)S(1)} async-done(((bf16[32,2,8,256]{3,2,1,0:T(8,128)(2,1)}), bf16[32,2,8,256]{3,2,1,0:T(8,128)(2,1)S(1)}, u32[]{:S(2)}, u32[]{:S(2)}) %all-to-all-start) | async-done | bytes 262176 | tf_op jit(solution)/shard_map/all_to_all | solution.py:421
  24.4 0.0 collective-permute-done.2.far_target_ref
  24.4 0.0 collective-permute-done.3.far_weight_ref
  24.4 2.1 %objective.1 = (f32[112,256,512]{2,1,0:T(8,128)}, bf16[4,2,4,2,2,8,256]{6,5,4,3,2,1,0:T(8,128)(2,1)S(1)}) custom-call(bf16[2,256,1024]{2,1,0:T(8,128)(2,1)S(1)} %rows.1.table, bf16[32,2,8,256]{3,2,1,0:T(8,128)(2,1)S(1)} %all-to-all-done.got_ref, f32[2,256,512]{2,1,0:T(8,128)S(1)} %copy-done, f32[2,256,512]{2,1,0:T(8,128)} %collective-permute-done.2.far_target_ref, ...), custom_call_target="tpu_custom_call" | custom-call | flops 1100000000 | bytes 5000000 | tf_op jit(solution)/shard_map/objective/pallas_call | solution.py:439
  26.5 0.0 copy-start.2
  26.5 0.8 %copy-done.2 = bf16[4,2,4,2,2,8,256]{6,5,4,3,2,1,0:T(8,128)(2,1)} copy-done((bf16[4,2,4,2,2,8,256]{6,5,4,3,2,1,0:T(8,128)(2,1)}, bf16[4,2,4,2,2,8,256]{6,5,4,3,2,1,0:T(8,128)(2,1)S(1)}, u32[]{:S(2)}) %copy-start.2) | copy-done | bytes 524312
  27.3 0.0 copy-start.3
  27.3 0.0 collective-permute-done
  27.3 0.0 collective-permute-done.1
  27.3 2.8 %all-to-all-start.1 = ((bf16[32,2,2,8,256]{4,3,2,1,0:T(8,128)(2,1)}), bf16[32,2,2,8,256]{4,3,2,1,0:T(8,128)(2,1)S(1)}, u32[]{:S(2)}, u32[]{:S(2)}) async-start(bf16[32,2,2,8,256]{4,3,2,1,0:T(8,128)(2,1)} %bitcast.17), calls=%async_computation.1 | async-start | bytes 1048576 | tf_op jit(solution)/shard_map/all_to_all | solution.py:466
  30.1 1.1 %slice_bitcast_fusion = f32[256,512]{1,0:T(8,128)S(1)} fusion(f32[112,256,512]{2,1,0:T(8,128)} %get-tuple-element.30.power_ref), kind=kLoop, calls=%fused_computation | loop fusion | bytes 1048576 | tf_op jit(solution)/shard_map/squeeze | solution.py:461
  31.2 0.1 collective-permute-start.4
  31.4 0.1 copy.14.code_ref
  31.5 1.7 %collective-permute-done.4.far_power_ref = f32[256,512]{1,0:T(8,128)S(1)} collective-permute-done((f32[256,512]{1,0:T(8,128)S(1)}, f32[256,512]{1,0:T(8,128)S(1)}, u32[]{:S(2)}, u32[]{:S(2)}) %collective-permute-start.4) | collective-permute-done | bytes 524320 | tf_op jit(solution)/shard_map/ppermute | solution.py:461
  33.2 0.0 copy-done.3
  33.2 3.3 %prepare.1 = (bf16[8,256,256]{2,1,0:T(8,128)(2,1)S(1)}, bf16[2,256,256]{2,1,0:T(8,128)(2,1)S(1)}, bf16[16,8,128]{2,1,0:T(8,128)(2,1)S(1)}, f32[2,256,512]{2,1,0:T(8,128)}) custom-call(s32[8,1,256]{2,1,0:T(1,128)S(1)} %bitcast.20, s32[256,2]{1,0:T(8,128)S(1)} %copy.14.code_ref, f32[112,256,512]{2,1,0:T(8,128)} %get-tuple-element.30.power_ref, ...), custom_call_target="tpu_custom_call" | custom-call | flops 1000000000 | bytes 2000000 | tf_op jit(solution)/shard_map/prepare/pallas_call | solution.py:467
  36.5 9.8 %all-to-all-done.1 = bf16[32,2,2,8,256]{4,3,2,1,0:T(8,128)(2,1)S(1)} async-done(((bf16[32,2,2,8,256]{4,3,2,1,0:T(8,128)(2,1)}), bf16[32,2,2,8,256]{4,3,2,1,0:T(8,128)(2,1)S(1)}, u32[]{:S(2)}, u32[]{:S(2)}) %all-to-all-start.1) | async-done | bytes 524320 | tf_op jit(solution)/shard_map/all_to_all | solution.py:466
  46.3 4.2 %adjoint.1 = bf16[16,264,128]{2,1,0:T(8,128)(2,1)S(1)} custom-call(bf16[2,2,8,2,2,8,256]{6,5,4,3,2,1,0:T(8,128)(2,1)S(1)} %bitcast.18, bf16[8,256,256]{2,1,0:T(8,128)(2,1)S(1)} %get-tuple-element.33.w_ref, s32[8,1,256]{2,1,0:T(1,128)S(1)} %bitcast.21, bf16[2,256,256]{2,1,0:T(8,128)(2,1)S(1)} %get-tuple-element.34.choose_ref, ...), custom_call_target="tpu_custom_call" | custom-call | flops 4300000256 | bytes 4000000 | tf_op jit(solution)/shard_map/adjoint/pallas_call | solution.py:492
  50.5 19.1 %all_to_all.15.got_ref = bf16[16,264,128]{2,1,0:T(8,128)(2,1)S(1)} all-to-all(bf16[16,264,128]{2,1,0:T(8,128)(2,1)S(1)} %adjoint.1), channel_id=1, replica_groups={{0,1,2,3,8,9,10,11,16,17,18,19,24,25,26,27},{4,5,6,7,12,13,14,15,20,21,..., dimensions={0} | all-to-all | bytes 2162688 | tf_op jit(solution)/shard_map/all_to_all | solution.py:505
  69.6 1.7 %faces.1 = f32[2,4,2,256,128]{4,3,2,1,0:T(8,128)} custom-call(bf16[16,264,128]{2,1,0:T(8,128)(2,1)S(1)} %all_to_all.15.got_ref), custom_call_target="tpu_custom_call" | custom-call | tf_op jit(solution)/shard_map/faces/pallas_call | solution.py:509
  (5 shorter events, 0.0 us)
Async XLA Ops:
  0.6 5.2 %copy-start = (f32[2,256,512]{2,1,0:T(8,128)S(1)}, f32[2,256,512]{2,1,0:T(8,128)}, u32[]{:S(2)}) copy-start(f32[2,256,512]{2,1,0:T(8,128)} %target_ref.1) | copy-start | bytes 3145732
  0.6 5.7 %copy-start.1 = (f32[2,256,512]{2,1,0:T(8,128)S(1)}, f32[2,256,512]{2,1,0:T(8,128)}, u32[]{:S(2)}) copy-start(f32[2,256,512]{2,1,0:T(8,128)} %weight_ref.1) | copy-start | bytes 3145732
  0.7 13.1 %copy-start.6 = (s32[256,1]{0,1:T(1,128)S(1)}, s32[256,1]{0,1:T(1,128)}, u32[]{:S(2)}) copy-start(s32[256,1]{0,1:T(1,128)} %param.12) | copy-start | bytes 3076
  0.7 15.8 %copy-start.5 = (s32[256]{0:T(256)S(1)}, s32[256]{0:T(256)}, u32[]{:S(2)}) copy-start(s32[256]{0:T(256)} %param.13) | copy-start | bytes 3076
  0.7 16.0 %copy-start.4 = (s32[2048]{0:T(1024)S(1)}, s32[2048]{0:T(1024)}, u32[]{:S(2)}) copy-start(s32[2048]{0:T(1024)} %param.8) | copy-start | bytes 24580
  5.8 18.5 %collective-permute-start.2 = (f32[2,256,512]{2,1,0:T(8,128)S(1)}, f32[2,256,512]{2,1,0:T(8,128)}, u32[]{:S(2)}, u32[]{:S(2)}) collective-permute-start(f32[2,256,512]{2,1,0:T(8,128)S(1)} %copy-done), channel_id=1, source_target_pairs={{0,8},{8,0},{16,24},{24,16},{1,9},{9,1},{17,25},{25,17},{2,10},{10... | collective-permute-start | bytes 3145736 | tf_op jit(solution)/shard_map/ppermute | solution.py:419
  6.4 18.0 %collective-permute-start.3 = (f32[2,256,512]{2,1,0:T(8,128)S(1)}, f32[2,256,512]{2,1,0:T(8,128)}, u32[]{:S(2)}, u32[]{:S(2)}) collective-permute-start(f32[2,256,512]{2,1,0:T(8,128)S(1)} %copy-done.1), channel_id=1, source_target_pairs={{0,8},{8,0},{16,24},{24,16},{1,9},{9,1},{17,25},{25,17},{2,10},{10... | collective-permute-start | bytes 3145736 | tf_op jit(solution)/shard_map/ppermute | solution.py:420
  6.4 17.9 %all-to-all-start = ((bf16[32,2,8,256]{3,2,1,0:T(8,128)(2,1)}), bf16[32,2,8,256]{3,2,1,0:T(8,128)(2,1)S(1)}, u32[]{:S(2)}, u32[]{:S(2)}) async-start(bf16[32,2,8,256]{3,2,1,0:T(8,128)(2,1)} %bitcast.22), calls=%async_computation | async-start | bytes 524288 | tf_op jit(solution)/shard_map/all_to_all | solution.py:421
  13.7 13.6 %collective-permute-start = (s32[256,1]{0,1:T(1,128)S(1)}, s32[256,1]{0,1:T(1,128)S(1)}, u32[]{:S(2)}, u32[]{:S(2)}) collective-permute-start(s32[256,1]{0,1:T(1,128)S(1)} %copy-done.6), channel_id=1, source_target_pairs={{0,4},{1,5},{2,6},{3,7},{4,0},{5,1},{6,2},{7,3},{8,12},{9,13},{10,... | collective-permute-start | bytes 3080 | tf_op jit(solution)/shard_map/ppermute | solution.py:390
  16.5 10.9 %collective-permute-start.1 = (s32[256]{0:T(256)S(1)}, s32[256]{0:T(256)S(1)}, u32[]{:S(2)}, u32[]{:S(2)}) collective-permute-start(s32[256]{0:T(256)S(1)} %copy-done.5), channel_id=1, source_target_pairs={{0,4},{1,5},{2,6},{3,7},{4,0},{5,1},{6,2},{7,3},{8,12},{9,13},{10,... | collective-permute-start | bytes 3080 | tf_op jit(solution)/shard_map/ppermute | solution.py:391
  26.5 0.8 %copy-start.2 = (bf16[4,2,4,2,2,8,256]{6,5,4,3,2,1,0:T(8,128)(2,1)}, bf16[4,2,4,2,2,8,256]{6,5,4,3,2,1,0:T(8,128)(2,1)S(1)}, u32[]{:S(2)}) copy-start(bf16[4,2,4,2,2,8,256]{6,5,4,3,2,1,0:T(8,128)(2,1)S(1)} %get-tuple-element.32) | copy-start | bytes 1572868
  27.3 5.9 %copy-start.3 = (s32[2048]{0:T(1024)S(1)}, s32[2048]{0:T(1024)}, u32[]{:S(2)}) copy-start(s32[2048]{0:T(1024)} %param.9) | copy-start | bytes 24580
  27.3 19.0 %all-to-all-start.1 = ((bf16[32,2,2,8,256]{4,3,2,1,0:T(8,128)(2,1)}), bf16[32,2,2,8,256]{4,3,2,1,0:T(8,128)(2,1)S(1)}, u32[]{:S(2)}, u32[]{:S(2)}) async-start(bf16[32,2,2,8,256]{4,3,2,1,0:T(8,128)(2,1)} %bitcast.17), calls=%async_computation.1 | async-start | bytes 1048576 | tf_op jit(solution)/shard_map/all_to_all | solution.py:466
  31.2 2.0 %collective-permute-start.4 = (f32[256,512]{1,0:T(8,128)S(1)}, f32[256,512]{1,0:T(8,128)S(1)}, u32[]{:S(2)}, u32[]{:S(2)}) collective-permute-start(f32[256,512]{1,0:T(8,128)S(1)} %slice_bitcast_fusion), channel_id=1, source_target_pairs={{0,8},{8,0},{16,24},{24,16},{1,9},{9,1},{17,25},{25,17},{2,10},{10... | collective-permute-start | bytes 1572872 | tf_op jit(solution)/shard_map/ppermute | solution.py:461

commit v9 on v8

--- a/solution.py
+++ b/solution.py
@@ -11,6 +11,7 @@
 SEG = 128
 CHUNK = 256
 PACK = 16
+SPAN = 4
 BOTH = ("row", "tile")
 BF = jnp.bfloat16
 F32 = jnp.float32
@@ -79,7 +80,9 @@
     return jnp.dot(block, flip, preferred_element_type=F32)
 
 
-def forward_kernel(quarter, rows_dev, angle_ref, cur_hbm, f_ref, cur_ref, lhs, fine, coarse, sem):
+def forward_kernel(
+    quarter, rows_dev, angle_ref, cur_hbm, f_hbm, f_ref, cur_ref, lhs, fine, coarse, sem, out_sem
+):
     points = rows_dev * quarter // SEG // 2
     chunks, width = angle_ref.shape[0], angle_ref.shape[-1]
     loads = [
@@ -111,6 +114,7 @@
             lhs[imag, :SEG] = even[1][p].astype(BF)
             lhs[imag, SEG:] = (-odd[0][p]).astype(BF)
     low = iota((8, width), 0) < 4
+    stores = []
     for i in range(chunks):
         grid_sum = jnp.dot(lhs[...], fine[i], preferred_element_type=F32)
         cos_a, sin_a = coarse[i, 0], coarse[i, 1]
@@ -125,6 +129,12 @@
             out = jnp.where(low, out_re, out_im).astype(BF)
             for copy in range(f_ref.shape[0]):
                 f_ref[copy, f, i, p] = out
+        stores.append(
+            pltpu.make_async_copy(f_ref.at[:, :, i], f_hbm.at[:, :, i], out_sem.at[i])
+        )
+        stores[-1].start()
+    for store in stores:
+        store.wait()
 
 
 def row_kernel(quarter, rows_dev, row_ref, r_ref):
@@ -304,23 +314,26 @@
         axis=0,
     ).astype(BF)
     stores = []
-    for f, p in [(i, j) for i in range(2) for j in range(2)]:
-        for c in range(2):
-            blocks = []
-            for side in range(2):
-                rows = pl.ds((8 * side + 4 * f + 2 * p + c) * PACK, PACK)
-                blocks.append(got_ref[:, rows, :])
-            block = jnp.concatenate(blocks, axis=1).reshape(2 * slots, SEG)
-            found = jnp.dot(choose, block, preferred_element_type=F32)
-            out_ref[f, p, c] = found
+    for first in range(0, 8, SPAN):
+        blocks = []
+        for i in range(first, first + SPAN):
+            pair = [got_ref[:, pl.ds((8 * side + i) * PACK, PACK), :] for side in range(2)]
+            blocks.append(jnp.concatenate(pair, axis=1).reshape(2 * slots, SEG))
+        found = jnp.dot(choose, jnp.concatenate(blocks, axis=1), preferred_element_type=F32)
+        for i in range(first, first + SPAN):
+            f, p, c = i // 4, i // 2 % 2, i % 2
+            piece = found[:, (i - first) * SEG:(i - first + 1) * SEG]
+            out_ref[f, p, c] = piece
             if p == 1:
-                out_ref[f, 2, c] = -found
-        places = [(0, 0), (0, 3)] if p == 0 else [(1, 1), (2, 2)]
-        for source, k in places:
-            stores.append(
-                pltpu.make_async_copy(out_ref.at[f, source], out_hbm.at[f, k], sems.at[f, k])
-            )
-            stores[-1].start()
+                out_ref[f, 2, c] = -piece
+            if c == 0:
+                continue
+            places = [(0, 0), (0, 3)] if p == 0 else [(1, 1), (2, 2)]
+            for source, k in places:
+                stores.append(
+                    pltpu.make_async_copy(out_ref.at[f, source], out_hbm.at[f, k], sems.at[f, k])
+                )
+                stores[-1].start()
     for store in stores:
         store.wait()
 
@@ -396,14 +409,16 @@
         functools.partial(forward_kernel, columns, rows_dev),
         grid=(1,),
         in_specs=[VM, pl.BlockSpec(memory_space=pltpu.HBM)],
-        out_specs=whole((copies, 2, chunks, 2, wide, CHUNK)),
+        out_specs=pl.BlockSpec(memory_space=pl.ANY),
         out_shape=jax.ShapeDtypeStruct((copies, 2, chunks, 2, wide, CHUNK), BF),
         scratch_shapes=[
+            pltpu.VMEM((copies, 2, chunks, 2, wide, CHUNK), BF),
             pltpu.VMEM(cur.shape, BF),
             pltpu.VMEM((8 * half, 2 * SEG), BF),
             pltpu.VMEM((chunks, 2 * SEG, CHUNK), BF),
             pltpu.VMEM((chunks, 2, half, CHUNK), F32),
             pltpu.SemaphoreType.DMA((2, 4)),
+            pltpu.SemaphoreType.DMA((chunks,)),
         ],
         compiler_params=params(58),
         cost_estimate=cost(4.3e9, 1.6e6),

time: 71.9 us -> 71.9 us (level)
  no operation moved by 1% of the time
where the time goes in v9:
time: 71.9 us; the launch traced here: 71.4 us
  blocking collectives  19.1 us (27%)
  Pallas kernels  18 us (25%)
  waiting for transfers between devices  17.5 us (24%)
  starting transfers between devices  13.7 us (19%)
  local copies, waits for them, and re-layouts  2.1 us (3%)
  between operations  0.96 us (1%)
    all_to_all x1, blocking collectives, body(): lax.all_to_all(outgoing, BOTH, 0, 0, tiled=True, axis_index_groups=half_g...  19.1 us
    all_to_all x1, waiting for transfers between devices, body(): back = lax.all_to_all(back, BOTH, 0, 0, tiled=True)  9.82 us
    all_to_all x1, starting transfers between devices, body(): got = lax.all_to_all(plane, BOTH, 0, 0, tiled=True)  7.26 us
    all_to_all x1, waiting for transfers between devices, body(): got = lax.all_to_all(plane, BOTH, 0, 0, tiled=True)  5.99 us
    pallas_call x1, Pallas kernels, body(): pl.pallas_call(functools.partial(forward_kernel, columns, rows_dev), grid...  5.1 us
    pallas_call x1, Pallas kernels, body(): pl.pallas_call(functools.partial(adjoint_kernel, columns, rows_dev), grid...  4.21 us
    pallas_call x1, Pallas kernels, body(): pl.pallas_call(functools.partial(prepare_kernel, columns, rows_dev, tile_...  3.29 us
    all_to_all x1, starting transfers between devices, body(): back = lax.all_to_all(back, BOTH, 0, 0, tiled=True)  2.8 us
  transfers between devices with their start and end apart: 7, of which 3 were waited for; matrix products, arithmetic and copies ran while one was open for 2% of the time, Pallas kernels for 10%

profile of v9, /device:TPU:0, one launch (start us, length us, event | category | flops | bytes accessed | tf_op | source)
XLA Modules:
  0.0 71.4 jit_solution(8340921058723004603)
XLA Ops:
  0.6 0.0 copy-start
  0.6 0.0 copy-start.1
  0.7 0.0 copy-start.6
  0.7 0.0 copy-start.5
  0.7 0.0 copy-start.4
  0.7 5.1 %columns.1 = bf16[2,2,8,2,8,256]{5,4,3,2,1,0:T(8,128)(2,1)} custom-call(s32[8,1,256]{2,1,0:T(1,128)} %bitcast.19, bf16[2,4,2,256,128]{4,3,2,1,0:T(8,128)(2,1)} %bitcast.29), custom_call_target="tpu_custom_call" | custom-call | flops 4300000256 | bytes 1600000 | tf_op jit(solution)/shard_map/columns/pallas_call | solution.py:408
  5.8 0.0 copy-done
  5.8 0.5 collective-permute-start.2
  6.3 0.0 copy-done.1
  6.3 0.1 collective-permute-start.3
  6.4 7.3 %all-to-all-start = ((bf16[32,2,8,256]{3,2,1,0:T(8,128)(2,1)}), bf16[32,2,8,256]{3,2,1,0:T(8,128)(2,1)S(1)}, u32[]{:S(2)}, u32[]{:S(2)}) async-start(bf16[32,2,8,256]{3,2,1,0:T(8,128)(2,1)} %bitcast.22), calls=%async_computation | async-start | bytes 524288 | tf_op jit(solution)/shard_map/all_to_all | solution.py:436
  13.7 0.0 copy-done.6
  13.7 2.7 %collective-permute-start = (s32[256,1]{0,1:T(1,128)S(1)}, s32[256,1]{0,1:T(1,128)S(1)}, u32[]{:S(2)}, u32[]{:S(2)}) collective-permute-start(s32[256,1]{0,1:T(1,128)S(1)} %copy-done.6), channel_id=1, source_target_pairs={{0,4},{1,5},{2,6},{3,7},{4,0},{5,1},{6,2},{7,3},{8,12},{9,13},{10,... | collective-permute-start | bytes 3080 | tf_op jit(solution)/shard_map/ppermute | solution.py:403
  16.4 0.0 copy-done.5
  16.4 0.3 collective-permute-start.1
  16.7 0.0 copy-done.4
  16.7 0.1 fusion
  16.8 1.6 %rows.1.table = bf16[2,256,1024]{2,1,0:T(8,128)(2,1)S(1)} custom-call(s32[2,512]{1,0:T(2,128)S(1)} %pad_add_fusion.row_ref), custom_call_target="tpu_custom_call" | custom-call | flops 100000000 | bytes 500000 | tf_op jit(solution)/shard_map/rows/pallas_call | solution.py:441
  18.4 6.0 %all-to-all-done.got_ref = bf16[32,2,8,256]{3,2,1,0:T(8,128)(2,1)S(1)} async-done(((bf16[32,2,8,256]{3,2,1,0:T(8,128)(2,1)}), bf16[32,2,8,256]{3,2,1,0:T(8,128)(2,1)S(1)}, u32[]{:S(2)}, u32[]{:S(2)}) %all-to-all-start) | async-done | bytes 262176 | tf_op jit(solution)/shard_map/all_to_all | solution.py:436
  24.4 0.0 collective-permute-done.2.far_target_ref
  24.4 0.0 collective-permute-done.3.far_weight_ref
  24.4 2.1 %objective.1 = (f32[112,256,512]{2,1,0:T(8,128)}, bf16[4,2,4,2,2,8,256]{6,5,4,3,2,1,0:T(8,128)(2,1)S(1)}) custom-call(bf16[2,256,1024]{2,1,0:T(8,128)(2,1)S(1)} %rows.1.table, bf16[32,2,8,256]{3,2,1,0:T(8,128)(2,1)S(1)} %all-to-all-done.got_ref, f32[2,256,512]{2,1,0:T(8,128)S(1)} %copy-done, f32[2,256,512]{2,1,0:T(8,128)} %collective-permute-done.2.far_target_ref, ...), custom_call_target="tpu_custom_call" | custom-call | flops 1100000000 | bytes 5000000 | tf_op jit(solution)/shard_map/objective/pallas_call | solution.py:454
  26.5 0.0 copy-start.2
  26.5 0.8 %copy-done.2 = bf16[4,2,4,2,2,8,256]{6,5,4,3,2,1,0:T(8,128)(2,1)} copy-done((bf16[4,2,4,2,2,8,256]{6,5,4,3,2,1,0:T(8,128)(2,1)}, bf16[4,2,4,2,2,8,256]{6,5,4,3,2,1,0:T(8,128)(2,1)S(1)}, u32[]{:S(2)}) %copy-start.2) | copy-done | bytes 524312
  27.3 0.0 copy-start.3
  27.3 0.0 collective-permute-done
  27.3 0.0 collective-permute-done.1
  27.3 2.8 %all-to-all-start.1 = ((bf16[32,2,2,8,256]{4,3,2,1,0:T(8,128)(2,1)}), bf16[32,2,2,8,256]{4,3,2,1,0:T(8,128)(2,1)S(1)}, u32[]{:S(2)}, u32[]{:S(2)}) async-start(bf16[32,2,2,8,256]{4,3,2,1,0:T(8,128)(2,1)} %bitcast.17), calls=%async_computation.1 | async-start | bytes 1048576 | tf_op jit(solution)/shard_map/all_to_all | solution.py:481
  30.1 1.1 %slice_bitcast_fusion = f32[256,512]{1,0:T(8,128)S(1)} fusion(f32[112,256,512]{2,1,0:T(8,128)} %get-tuple-element.30.power_ref), kind=kLoop, calls=%fused_computation | loop fusion | bytes 1048576 | tf_op jit(solution)/shard_map/squeeze | solution.py:476
  31.2 0.1 collective-permute-start.4
  31.3 0.1 copy.14.code_ref
  31.5 1.7 %collective-permute-done.4.far_power_ref = f32[256,512]{1,0:T(8,128)S(1)} collective-permute-done((f32[256,512]{1,0:T(8,128)S(1)}, f32[256,512]{1,0:T(8,128)S(1)}, u32[]{:S(2)}, u32[]{:S(2)}) %collective-permute-start.4) | collective-permute-done | bytes 524320 | tf_op jit(solution)/shard_map/ppermute | solution.py:476
  33.2 0.0 copy-done.3
  33.2 3.3 %prepare.1 = (bf16[8,256,256]{2,1,0:T(8,128)(2,1)S(1)}, bf16[2,256,256]{2,1,0:T(8,128)(2,1)S(1)}, bf16[16,8,128]{2,1,0:T(8,128)(2,1)S(1)}, f32[2,256,512]{2,1,0:T(8,128)}) custom-call(s32[8,1,256]{2,1,0:T(1,128)S(1)} %bitcast.20, s32[256,2]{1,0:T(8,128)S(1)} %copy.14.code_ref, f32[112,256,512]{2,1,0:T(8,128)} %get-tuple-element.30.power_ref, ...), custom_call_target="tpu_custom_call" | custom-call | flops 1000000000 | bytes 2000000 | tf_op jit(solution)/shard_map/prepare/pallas_call | solution.py:482
  36.5 9.8 %all-to-all-done.1 = bf16[32,2,2,8,256]{4,3,2,1,0:T(8,128)(2,1)S(1)} async-done(((bf16[32,2,2,8,256]{4,3,2,1,0:T(8,128)(2,1)}), bf16[32,2,2,8,256]{4,3,2,1,0:T(8,128)(2,1)S(1)}, u32[]{:S(2)}, u32[]{:S(2)}) %all-to-all-start.1) | async-done | bytes 524320 | tf_op jit(solution)/shard_map/all_to_all | solution.py:481
  46.3 4.2 %adjoint.1 = bf16[16,264,128]{2,1,0:T(8,128)(2,1)S(1)} custom-call(bf16[2,2,8,2,2,8,256]{6,5,4,3,2,1,0:T(8,128)(2,1)S(1)} %bitcast.18, bf16[8,256,256]{2,1,0:T(8,128)(2,1)S(1)} %get-tuple-element.33.w_ref, s32[8,1,256]{2,1,0:T(1,128)S(1)} %bitcast.21, bf16[2,256,256]{2,1,0:T(8,128)(2,1)S(1)} %get-tuple-element.34.choose_ref, ...), custom_call_target="tpu_custom_call" | custom-call | flops 4300000256 | bytes 4000000 | tf_op jit(solution)/shard_map/adjoint/pallas_call | solution.py:507
  50.5 19.1 %all_to_all.15.got_ref = bf16[16,264,128]{2,1,0:T(8,128)(2,1)S(1)} all-to-all(bf16[16,264,128]{2,1,0:T(8,128)(2,1)S(1)} %adjoint.1), channel_id=1, replica_groups={{0,1,2,3,8,9,10,11,16,17,18,19,24,25,26,27},{4,5,6,7,12,13,14,15,20,21,..., dimensions={0} | all-to-all | bytes 2162688 | tf_op jit(solution)/shard_map/all_to_all | solution.py:520
  69.6 1.7 %faces.1 = f32[2,4,2,256,128]{4,3,2,1,0:T(8,128)} custom-call(bf16[16,264,128]{2,1,0:T(8,128)(2,1)S(1)} %all_to_all.15.got_ref), custom_call_target="tpu_custom_call" | custom-call | tf_op jit(solution)/shard_map/faces/pallas_call | solution.py:524
  (5 shorter events, 0.0 us)
Async XLA Ops:
  0.6 5.2 %copy-start = (f32[2,256,512]{2,1,0:T(8,128)S(1)}, f32[2,256,512]{2,1,0:T(8,128)}, u32[]{:S(2)}) copy-start(f32[2,256,512]{2,1,0:T(8,128)} %target_ref.1) | copy-start | bytes 3145732
  0.6 5.7 %copy-start.1 = (f32[2,256,512]{2,1,0:T(8,128)S(1)}, f32[2,256,512]{2,1,0:T(8,128)}, u32[]{:S(2)}) copy-start(f32[2,256,512]{2,1,0:T(8,128)} %weight_ref.1) | copy-start | bytes 3145732
  0.7 13.0 %copy-start.6 = (s32[256,1]{0,1:T(1,128)S(1)}, s32[256,1]{0,1:T(1,128)}, u32[]{:S(2)}) copy-start(s32[256,1]{0,1:T(1,128)} %param.12) | copy-start | bytes 3076
  0.7 15.8 %copy-start.5 = (s32[256]{0:T(256)S(1)}, s32[256]{0:T(256)}, u32[]{:S(2)}) copy-start(s32[256]{0:T(256)} %param.13) | copy-start | bytes 3076
  0.7 16.0 %copy-start.4 = (s32[2048]{0:T(1024)S(1)}, s32[2048]{0:T(1024)}, u32[]{:S(2)}) copy-start(s32[2048]{0:T(1024)} %param.8) | copy-start | bytes 24580
  5.8 18.6 %collective-permute-start.2 = (f32[2,256,512]{2,1,0:T(8,128)S(1)}, f32[2,256,512]{2,1,0:T(8,128)}, u32[]{:S(2)}, u32[]{:S(2)}) collective-permute-start(f32[2,256,512]{2,1,0:T(8,128)S(1)} %copy-done), channel_id=1, source_target_pairs={{0,8},{8,0},{16,24},{24,16},{1,9},{9,1},{17,25},{25,17},{2,10},{10... | collective-permute-start | bytes 3145736 | tf_op jit(solution)/shard_map/ppermute | solution.py:434
  6.3 18.0 %collective-permute-start.3 = (f32[2,256,512]{2,1,0:T(8,128)S(1)}, f32[2,256,512]{2,1,0:T(8,128)}, u32[]{:S(2)}, u32[]{:S(2)}) collective-permute-start(f32[2,256,512]{2,1,0:T(8,128)S(1)} %copy-done.1), channel_id=1, source_target_pairs={{0,8},{8,0},{16,24},{24,16},{1,9},{9,1},{17,25},{25,17},{2,10},{10... | collective-permute-start | bytes 3145736 | tf_op jit(solution)/shard_map/ppermute | solution.py:435
  6.4 17.9 %all-to-all-start = ((bf16[32,2,8,256]{3,2,1,0:T(8,128)(2,1)}), bf16[32,2,8,256]{3,2,1,0:T(8,128)(2,1)S(1)}, u32[]{:S(2)}, u32[]{:S(2)}) async-start(bf16[32,2,8,256]{3,2,1,0:T(8,128)(2,1)} %bitcast.22), calls=%async_computation | async-start | bytes 524288 | tf_op jit(solution)/shard_map/all_to_all | solution.py:436
  13.7 13.6 %collective-permute-start = (s32[256,1]{0,1:T(1,128)S(1)}, s32[256,1]{0,1:T(1,128)S(1)}, u32[]{:S(2)}, u32[]{:S(2)}) collective-permute-start(s32[256,1]{0,1:T(1,128)S(1)} %copy-done.6), channel_id=1, source_target_pairs={{0,4},{1,5},{2,6},{3,7},{4,0},{5,1},{6,2},{7,3},{8,12},{9,13},{10,... | collective-permute-start | bytes 3080 | tf_op jit(solution)/shard_map/ppermute | solution.py:403
  16.4 10.9 %collective-permute-start.1 = (s32[256]{0:T(256)S(1)}, s32[256]{0:T(256)S(1)}, u32[]{:S(2)}, u32[]{:S(2)}) collective-permute-start(s32[256]{0:T(256)S(1)} %copy-done.5), channel_id=1, source_target_pairs={{0,4},{1,5},{2,6},{3,7},{4,0},{5,1},{6,2},{7,3},{8,12},{9,13},{10,... | collective-permute-start | bytes 3080 | tf_op jit(solution)/shard_map/ppermute | solution.py:404
  26.5 0.8 %copy-start.2 = (bf16[4,2,4,2,2,8,256]{6,5,4,3,2,1,0:T(8,128)(2,1)}, bf16[4,2,4,2,2,8,256]{6,5,4,3,2,1,0:T(8,128)(2,1)S(1)}, u32[]{:S(2)}) copy-start(bf16[4,2,4,2,2,8,256]{6,5,4,3,2,1,0:T(8,128)(2,1)S(1)} %get-tuple-element.32) | copy-start | bytes 1572868
  27.3 5.9 %copy-start.3 = (s32[2048]{0:T(1024)S(1)}, s32[2048]{0:T(1024)}, u32[]{:S(2)}) copy-start(s32[2048]{0:T(1024)} %param.9) | copy-start | bytes 24580
  27.3 19.0 %all-to-all-start.1 = ((bf16[32,2,2,8,256]{4,3,2,1,0:T(8,128)(2,1)}), bf16[32,2,2,8,256]{4,3,2,1,0:T(8,128)(2,1)S(1)}, u32[]{:S(2)}, u32[]{:S(2)}) async-start(bf16[32,2,2,8,256]{4,3,2,1,0:T(8,128)(2,1)} %bitcast.17), calls=%async_computation.1 | async-start | bytes 1048576 | tf_op jit(solution)/shard_map/all_to_all | solution.py:481
  31.2 2.0 %collective-permute-start.4 = (f32[256,512]{1,0:T(8,128)S(1)}, f32[256,512]{1,0:T(8,128)S(1)}, u32[]{:S(2)}, u32[]{:S(2)}) collective-permute-start(f32[256,512]{1,0:T(8,128)S(1)} %slice_bitcast_fusion), channel_id=1, source_target_pairs={{0,8},{8,0},{16,24},{24,16},{1,9},{9,1},{17,25},{25,17},{2,10},{10... | collective-permute-start | bytes 1572872 | tf_op jit(solution)/shard_map/ppermute | solution.py:476
